TPU v7x, 128 devices: a whole 4x4x4 slice. The times are simulated.
128 devices in a mesh: task: 8 (over z, core), mp: 16 (over y, x).
Axes of the slice: x: 4, y: 4, z: 4, core: 2. Of those that a mesh axis runs over, the one named last changes fastest.
Arguments:
- deter: float32 [2048, 4096], P('task', 'mp'), may hold values from -3 to 3
- draws: int32 [4, 32, 2048], P(None, None, 'task'), may hold values from 0 to 31
- actions: int32 [4, 2048], P(None, 'task'), may hold values from 0 to 17
- horizons: int32 [64], replicated, may hold values from 5 to 30, as said below
- offsets: int32 [4, 4], replicated, may hold values from 0 to 7, as said below
- embed_stoch: bfloat16 [1024, 1024], replicated, may hold values from -1 to 1
- embed_act: bfloat16 [18, 1024], replicated, may hold values from -6 to 6
- gru_weight: bfloat16 [5120, 3, 4096], P(None, None, 'mp'), may hold values from -0.078125 to 0.078125
- prior_weight: bfloat16 [4096, 1024], replicated, may hold values from -0.09375 to 0.09375
- logit_weight: bfloat16 [1024, 1024], replicated, may hold values from -0.75 to 0.75
- head_weight: bfloat16 [1024, 2], replicated, may hold values from -0.375 to 0.375
Outputs:
- log_prob: float32 [4, 2048], P(None, 'task')
- reward: float32 [4, 2048], P(None, 'task')
- continuation: float32 [4, 2048], P(None, 'task')
- final_deter: float32 [2048, 4096], P('task', 'mp')
Inputs may be any that keep to these rules, and one draw needn't show every extreme that they name: `horizons`: rows of task k are home rows k * (32) up to (k + 1) * 32 - 1. `offsets`: the 4 numbers of one row are distinct.
All inputs are finite; a program needn't handle non-finite values.
Results may differ from a plain program's by a relative error of at most 0.0045.
Values may be sent and summed in bfloat16 or wider, within the bound.
No kernel may reach another device: no remote copies, remote signals or barrier semaphores. Data moves between devices by JAX's collectives and lax.ppermute only.
A program may use at most 128 MiB of HBM per device.

v0:
```python
import functools

import jax
import jax.numpy as jnp
from jax import lax
from jax.experimental import pallas as pl
from jax.experimental.pallas import tpu as pltpu
from jax.sharding import PartitionSpec as P

HID = 1024
GROUPS = 32
CLASSES = 32
TASKS = 64
BLK_DEV = 4
STEPS = 4
WSTART = 16
ACT_PAD = 32
DEPTH = 40
LEVELS = (5, 6, 8)
PIECE = 32
F32 = jnp.float32
BF16 = jnp.bfloat16
I32 = jnp.int32


def silu(v):
    return v / (1.0 + jnp.exp(-v))


def sigmoid(v):
    return 1.0 / (1.0 + jnp.exp(-v))


def row_norm(pre):
    entries = pre.shape[1]
    avg = jnp.sum(pre, axis=1, keepdims=True) / entries
    squares = jnp.sum(pre * pre, axis=1, keepdims=True) / entries
    return (pre - avg) * lax.rsqrt(squares - avg * avg + 1e-5)


def spread_matrix():
    variable = lax.broadcasted_iota(I32, (GROUPS, HID), 0)
    entry = lax.broadcasted_iota(I32, (GROUPS, HID), 1)
    return (entry // CLASSES == variable).astype(F32).astype(BF16)


def chosen_mask(by_row, spread):
    wide = jnp.dot(by_row, spread, preferred_element_type=F32)
    entry = lax.broadcasted_iota(I32, wide.shape, 1)
    return wide == (entry % CLASSES).astype(F32)


def selector(length, at):
    place = lax.broadcasted_iota(I32, (length, at.shape[1]), 0)
    return (place == at).astype(F32).astype(BF16)


def side_by_side(ref):
    return jnp.concatenate([ref[q] for q in range(ref.shape[0])], axis=1)


def embed_kernel(at_ref, ev_ref, stoch_ref, act_ref, *refs):
    steps = ev_ref.shape[0]
    outs, all_picks, (hot_ref, pre_ref) = refs[:steps], refs[steps : 2 * steps], refs[2 * steps :]
    rows = pre_ref.shape[0]
    spread = spread_matrix()
    ids = lax.broadcasted_iota(I32, (PIECE, ACT_PAD), 1).astype(F32)
    for step in range(steps):
        picks_ref, out_ref = all_picks[step], outs[step]

        def mark(k, _, step=step, picks_ref=picks_ref):
            at = pl.ds(pl.multiple_of(k * PIECE, PIECE), PIECE)
            wanted = ev_ref[step, pl.ds(pl.multiple_of(at_ref[step, k], PIECE), PIECE)]
            picks_ref[at] = wanted
            hot_ref[at, :HID] = chosen_mask(wanted[:, :GROUPS], spread).astype(F32).astype(BF16)
            action = wanted[:, GROUPS : GROUPS + 1].astype(F32)
            hot_ref[at, HID:] = (ids == action).astype(F32).astype(BF16)
            return 0

        lax.fori_loop(0, rows // PIECE, mark, 0)
        pre_ref[...] = jnp.dot(
            hot_ref[:, :HID], stoch_ref[...], preferred_element_type=F32
        ) + jnp.dot(hot_ref[:, HID:], act_ref[...], preferred_element_type=F32)

        def finish(k, _, out_ref=out_ref):
            at = pl.ds(pl.multiple_of(k * PIECE, PIECE), PIECE)
            out_ref[at] = silu(row_norm(pre_ref[at])).astype(BF16)
            return 0

        lax.fori_loop(0, rows // PIECE, finish, 0)


def full_lanes(part):
    rows = part.shape[0]
    if rows < 256:
        part = jnp.concatenate([part, jnp.zeros((256 - rows, 128), F32)], axis=0)
    return jnp.transpose(part)


def lanes_from_row(row, rows):
    return jnp.transpose(jnp.broadcast_to(row, (128, row.shape[1])))[:rows]


def gates_kernel(emb_ref, x_ref, w_ref, g_ref, stat_ref, wbuf, sem):
    parts, depth, share = w_ref.shape
    chunks = depth // HID

    def fetch(c):
        at = pl.ds(pl.multiple_of(c * HID, HID), HID)
        return pltpu.make_async_copy(w_ref.at[:, at, :], wbuf.at[c], sem.at[c])

    for c in range(chunks):
        fetch(c).start()
    per = HID // share
    fetch(0).wait()
    for k in range(parts):
        g_ref[:, k * share : (k + 1) * share] = jnp.dot(
            emb_ref[...], wbuf[0, k], preferred_element_type=F32
        )

    def add(c, _):
        left = jnp.concatenate([x_ref[(c - 1) * per + q] for q in range(per)], axis=1)
        fetch(c).wait()
        for k in range(parts):
            g_ref[:, k * share : (k + 1) * share] += jnp.dot(
                left, wbuf[c, k], preferred_element_type=F32
            )
        return 0

    lax.fori_loop(1, chunks, add, 0)
    rows, width = g_ref.shape
    part = jnp.zeros((rows, 128), F32)
    part_sq = part
    for q in range(width // 128):
        piece = g_ref[:, q * 128 : (q + 1) * 128]
        part += piece
        part_sq += piece * piece
    sums = jnp.concatenate(
        [
            jnp.sum(full_lanes(part), axis=0, keepdims=True),
            jnp.sum(full_lanes(part_sq), axis=0, keepdims=True),
        ],
        axis=0,
    )
    for q in range(stat_ref.shape[0]):
        stat_ref[q] = sums


def update_kernel(entries, g_ref, stat_ref, carried_ref, live_ref, new_ref, low_ref):
    sums = jnp.sum(stat_ref[...], axis=0) / entries
    avg = sums[0:1]
    inv = lax.rsqrt(sums[1:2] - avg * avg + 1e-5)
    rows, share = carried_ref.shape
    avg_l = lanes_from_row(avg, rows)
    inv_l = lanes_from_row(inv, rows)
    live_l = lanes_from_row(live_ref[...], rows)
    for q in range(share // 128):
        def normed(part):
            at = part * share + q * 128
            return (g_ref[:, at : at + 128] - avg_l) * inv_l

        held = carried_ref[:, q * 128 : (q + 1) * 128]
        reset = sigmoid(normed(0))
        candidate = jnp.tanh(reset * normed(1))
        update = sigmoid(normed(2) - 1.0)
        renewed = update * candidate + (1.0 - update) * held
        renewed = jnp.where(live_l > 0, renewed, held)
        new_ref[:, q * 128 : (q + 1) * 128] = renewed
        low = renewed.astype(BF16)
        for k in range(low_ref.shape[0]):
            low_ref[k, :, q * 128 : (q + 1) * 128] = low


def two_parts(values):
    high = values.astype(BF16)
    return high, (values - high.astype(F32)).astype(BF16)


def prior_kernel(
    x_ref, w_ref, logit_ref, head_ref, picks_ref, live_ref, out_ref,
    wbuf, lbuf, pre_ref, hid_ref, parts_ref, sem,
):
    shards, rows, share = x_ref.shape
    chunks = w_ref.shape[0] // HID
    per = HID // share

    def fetch(c):
        at = pl.ds(pl.multiple_of(c * HID, HID), HID)
        return pltpu.make_async_copy(w_ref.at[at], wbuf.at[c], sem.at[c])

    for c in range(chunks):
        fetch(c).start()
    last = pltpu.make_async_copy(logit_ref, lbuf, sem.at[chunks])
    last.start()
    pre_ref[...] = jnp.zeros(pre_ref.shape, F32)

    def add(c, _):
        left = jnp.concatenate([x_ref[c * per + q] for q in range(per)], axis=1)
        fetch(c).wait()
        pre_ref[...] += jnp.dot(left, wbuf[c], preferred_element_type=F32)
        return 0

    lax.fori_loop(0, chunks, add, 0)

    def squash(k, _):
        at = pl.ds(pl.multiple_of(k * PIECE, PIECE), PIECE)
        hid_ref[at] = silu(row_norm(pre_ref[at])).astype(BF16)
        return 0

    lax.fori_loop(0, rows // PIECE, squash, 0)
    last.wait()
    across = (((1,), (1,)), ((), ()))
    heads = lax.dot_general(head_ref[...], hid_ref[...], across, preferred_element_type=F32)
    pre_ref[...] = jnp.dot(hid_ref[...], lbuf[...], preferred_element_type=F32)
    spread = spread_matrix()

    def classes(k, _):
        at = pl.ds(pl.multiple_of(k * PIECE, PIECE), PIECE)
        exponent = jnp.exp(5.0 * jnp.tanh(pre_ref[at] / 5.0))
        wanted = picks_ref[at, :GROUPS]
        chosen = jnp.where(chosen_mask(wanted, spread), exponent, 0.0)
        parts_ref[0, at], parts_ref[1, at] = two_parts(exponent)
        parts_ref[2, at], parts_ref[3, at] = two_parts(chosen)
        return 0

    lax.fori_loop(0, rows // PIECE, classes, 0)

    def over_groups(k):
        return lax.dot_general(
            spread, parts_ref[k], across, preferred_element_type=F32
        ) + lax.dot_general(spread, parts_ref[k + 1], across, preferred_element_type=F32)

    chances = 0.99 * over_groups(2) / over_groups(0) + 0.01 / CLASSES
    log_prob = jnp.sum(jnp.log(chances), axis=0, keepdims=True)
    live = live_ref[:, :rows]
    out_ref[...] = jnp.zeros(out_ref.shape, F32)
    out_ref[0:1, :rows] = log_prob * live
    out_ref[1:2, :rows] = heads[0:1] * live
    out_ref[2:3, :rows] = sigmoid(heads[1:2]) * live


def pick_kernel(at_ref, own_ref, other_ref, carried_ref, low_ref, *rest_ref):
    count, per_task, share = own_ref.shape
    done = carried_ref.shape[0] // per_task
    for i in range(count):
        at = at_ref[i]
        inner = at % count
        value = jnp.where(at < count, own_ref[inner], other_ref[inner])
        low = value.astype(BF16)
        rows = slice(i * per_task, (i + 1) * per_task)
        if i < done:
            carried_ref[rows] = value
            for k in range(low_ref.shape[0]):
                low_ref[k, rows] = low
        else:
            rest_ref[0][(i - done) * per_task : (i - done + 1) * per_task] = low


def settle_kernel(at_ref, got_ref, outs_ref, to_ref, final_ref, small_ref, buf, sem):
    count, per_task, share = buf.shape
    copies = []
    for i in range(count):
        at = pl.ds(pl.multiple_of(at_ref[1, i] * per_task, per_task), per_task)
        copy = pltpu.make_async_copy(got_ref.at[at_ref[0, i], at], buf.at[i], sem.at[i])
        copy.start()
        copies.append(copy)
    parts = side_by_side(outs_ref)
    for t in range(STEPS):
        values = jnp.dot(
            parts, selector(parts.shape[1], to_ref[t : t + 1]), preferred_element_type=F32
        )
        for k in range(3):
            at = t * 3 + k
            small_ref[k, t : t + 1, :] = values[at : at + 1] + values[12 + at : 13 + at]
    for i in range(count):
        copies[i].wait()
        final_ref[i * per_task : (i + 1) * per_task] = buf[i].astype(F32)


def params(mib):
    return pltpu.CompilerParams(vmem_limit_bytes=mib * 1024 * 1024)


WHOLE = pl.BlockSpec()
STAY = pl.BlockSpec(memory_space=pltpu.HBM)
SCALARS = pl.BlockSpec(memory_space=pltpu.SMEM)


def embed(at, everyone, stoch, act, rows):
    steps, _, depth = everyone.shape
    made = pl.pallas_call(
        embed_kernel,
        in_specs=[SCALARS, WHOLE, WHOLE, WHOLE],
        out_shape=[jax.ShapeDtypeStruct((rows, HID), BF16)] * steps
        + [jax.ShapeDtypeStruct((rows, depth), BF16)] * steps,
        scratch_shapes=[
            pltpu.VMEM((rows, HID + ACT_PAD), BF16),
            pltpu.VMEM((rows, HID), F32),
        ],
        compiler_params=params(20),
        name="embed",
    )(at, everyone, stoch, act)
    return made[:steps], made[steps:]


def gates(emb, x, w):
    shards, rows, share = x.shape
    parts, depth, _ = w.shape
    return pl.pallas_call(
        gates_kernel,
        in_specs=[WHOLE, WHOLE, STAY],
        out_shape=[
            jax.ShapeDtypeStruct((rows, parts * share), F32),
            jax.ShapeDtypeStruct((shards, 2, 256), F32),
        ],
        scratch_shapes=[
            pltpu.VMEM((depth // HID, parts, HID, share), BF16),
            pltpu.SemaphoreType.DMA((depth // HID,)),
        ],
        compiler_params=params(24),
        name="gates",
    )(emb, x, w)


def renew(g, stats, carried, live, entries):
    rows, share = carried.shape
    return pl.pallas_call(
        functools.partial(update_kernel, entries),
        out_shape=[
            jax.ShapeDtypeStruct((rows, share), F32),
            jax.ShapeDtypeStruct((stats.shape[0], rows, share), BF16),
        ],
        compiler_params=params(16),
        name="renew",
    )(g, stats, carried, live)


def prior(x, w, logit, head, picks, live):
    rows = x.shape[1]
    chunks = w.shape[0] // HID
    return pl.pallas_call(
        prior_kernel,
        in_specs=[WHOLE, STAY, STAY, WHOLE, WHOLE, WHOLE],
        out_shape=jax.ShapeDtypeStruct((8, 256), F32),
        scratch_shapes=[
            pltpu.VMEM((chunks, HID, HID), BF16),
            pltpu.VMEM((HID, HID), BF16),
            pltpu.VMEM((rows, HID), F32),
            pltpu.VMEM((rows, HID), BF16),
            pltpu.VMEM((4, rows, HID), BF16),
            pltpu.SemaphoreType.DMA((chunks + 1,)),
        ],
        compiler_params=params(28),
        name="prior",
    )(x, w, logit, head, picks, live)


def pick(at, own, other, rows, shards):
    count, per_task, share = own.shape
    left = count * per_task - rows
    shapes = [
        jax.ShapeDtypeStruct((rows, share), F32),
        jax.ShapeDtypeStruct((shards, rows, share), BF16),
    ]
    if left:
        shapes.append(jax.ShapeDtypeStruct((left, share), BF16))
    return pl.pallas_call(
        pick_kernel,
        in_specs=[SCALARS, WHOLE, WHOLE],
        out_shape=shapes,
        compiler_params=params(16),
        name="pick",
    )(at, own, other)


def settle(at, got, outs, to, count, per_task):
    share = got.shape[2]
    return pl.pallas_call(
        settle_kernel,
        in_specs=[SCALARS, pl.BlockSpec(memory_space=pl.ANY), WHOLE, WHOLE],
        out_shape=[
            jax.ShapeDtypeStruct((count * per_task, share), F32),
            jax.ShapeDtypeStruct((3, STEPS, to.shape[1]), F32),
        ],
        scratch_shapes=[
            pltpu.VMEM((count, per_task, share), BF16),
            pltpu.SemaphoreType.DMA((count,)),
        ],
        compiler_params=params(16),
        name="settle",
    )(at, got, outs, to)


def exchange(copies, axis):
    return lax.all_to_all(copies, axis, 0, 0, tiled=True)


def window(count, args, holders, shards):
    (
        deter, other, draws, actions, horizons, offsets, rank, local, from_task,
        stoch, act, w, prior_weight, logit, head,
    ) = args
    all_rows, share = deter.shape
    per_core = local.shape[0]
    per_task = all_rows // per_core
    rows = count * per_task
    entries = 3 * share * shards
    place = lax.axis_index("task")
    pair = 2 * per_core
    in_block = per_core // BLK_DEV

    carried, low, *rest = pick(
        from_task,
        deter.reshape(per_core, per_task, share),
        other.reshape(per_core, per_task, share),
        rows,
        shards,
    )
    x = exchange(low, "mp")

    sent = jnp.concatenate(
        [draws, actions[:, None], jnp.zeros((STEPS, DEPTH - GROUPS - 1, all_rows), I32)], axis=1
    ).astype(BF16)
    everyone = jnp.transpose(lax.all_gather(sent, "task"), (1, 0, 3, 2))
    everyone = everyone.reshape(STEPS, holders * all_rows, DEPTH)

    task = place // 2 * pair + local
    horizon = jnp.sum(
        jnp.where(task[:, None] == jnp.arange(TASKS, dtype=I32)[None, :], horizons[None, :], 0), axis=1
    )
    moments = WSTART + jnp.arange(STEPS, dtype=I32)
    living = jnp.repeat((horizon[None, :] > moments[:, None]).astype(F32), per_task, axis=1)

    running = jnp.cumsum(offsets, axis=0) % holders
    lane_block = task % per_core // in_block
    blocks = jnp.arange(BLK_DEV, dtype=I32)
    ahead_by = jnp.sum(
        jnp.where(lane_block[None, :, None] == blocks, running[:, None, :], 0), axis=2
    )
    slot = (task[None, :] // per_core + ahead_by) % holders
    source = slot * all_rows + (task % per_core)[None, :] * per_task
    emb, picks = embed(source, everyone, stoch, act, rows)
    x, emb, picks = lax.optimization_barrier((x, emb, picks))

    held = jnp.repeat((place - running) % holders, in_block, axis=1) * per_core
    held = held + jnp.arange(per_core, dtype=I32)[None, :]
    dealt = jnp.sum(
        jnp.where(held[:, :, None] == jnp.arange(TASKS, dtype=I32), rank.reshape(-1), 0), axis=2
    )
    core = held // pair * 2 + dealt % 2
    chunk = dealt // 2
    settle_at = jnp.stack([core[STEPS - 1], chunk[STEPS - 1]])
    to = jnp.where(chunk < count, core * 256 + chunk * per_task, -TASKS * 256)
    to = jnp.repeat(to, per_task, axis=1) + jnp.arange(all_rows, dtype=I32)[None, :] % per_task

    small = []
    for moment in range(STEPS):
        live = living[moment : moment + 1]
        g, stats = gates(emb[moment], x, w)
        stats = exchange(stats, "mp")
        small.append(prior(x, prior_weight, logit, head, picks[moment], live))
        stats, small = lax.optimization_barrier((stats, small))
        carried, low = renew(g, stats, carried, live, entries)
        if moment < STEPS - 1:
            x = exchange(low, "mp")

    outs = jnp.concatenate([s[:3] for s in small], axis=0)
    high, low_part = two_parts(outs)
    sent = jnp.concatenate([low[0], *rest, high, low_part, jnp.zeros((8, share), BF16)], axis=0)
    got = exchange(jnp.broadcast_to(sent[None], (holders, *sent.shape)), "task")
    outs = got[:, all_rows : all_rows + 24]
    return settle(settle_at, got, outs, to, per_core, per_task)


def on_device(
    deter,
    draws,
    actions,
    horizons,
    offsets,
    embed_stoch,
    embed_act,
    gru_weight,
    prior_weight,
    logit_weight,
    head_weight,
):
    holders = lax.axis_size("task")
    place = lax.axis_index("task")
    shards = lax.axis_size("mp")
    rows, share = deter.shape
    per_core = TASKS // holders
    pair = 2 * per_core

    other = lax.ppermute(deter, "task", [(i, i ^ 1) for i in range(holders)])
    w = jnp.transpose(gru_weight, (1, 0, 2))
    act = jnp.pad(embed_act, ((0, ACT_PAD - embed_act.shape[0]), (0, 0)))
    head = jnp.pad(jnp.transpose(head_weight), ((0, 6), (0, 0)))

    by_chip = horizons.reshape(TASKS // pair, pair)
    index = jnp.arange(pair, dtype=I32)
    ahead = (by_chip[:, None, :] > by_chip[:, :, None]) | (
        (by_chip[:, None, :] == by_chip[:, :, None]) & (index[None, None, :] < index[None, :, None])
    )
    rank = jnp.sum(ahead.astype(I32), axis=2)
    most = jnp.max(jnp.sum((by_chip > WSTART).astype(I32), axis=1))
    need = (most + 1) // 2
    level = sum((need > n).astype(I32) for n in LEVELS[:-1])

    chip = place // 2
    mine = 2 * jnp.arange(per_core, dtype=I32) + place % 2
    my_rank = jnp.sum(
        jnp.where(jnp.arange(TASKS // pair, dtype=I32)[:, None] == chip, rank, 0), axis=0
    )
    local = jnp.sum(jnp.where(my_rank[None, :] == mine[:, None], index[None, :], 0), axis=1)
    swapped = (local // per_core != place % 2).astype(I32)
    from_task = swapped * per_core + local % per_core
    operands = (
        deter, other, draws, actions, horizons, offsets, rank, local, from_task,
        embed_stoch, act, w, prior_weight, logit_weight, head,
    )
    branches = [lambda args, n=n: window(n, args, holders, shards) for n in LEVELS]
    final, small = lax.switch(level, branches, operands)
    return (small[0], small[1], small[2], final)


def solution(mesh):
    in_specs = (
        P("task", "mp"),
        P(None, None, "task"),
        P(None, "task"),
        P(),
        P(),
        P(),
        P(),
        P(None, None, "mp"),
        P(),
        P(),
        P(),
    )
    out_specs = (P(None, "task"), P(None, "task"), P(None, "task"), P("task", "mp"))
    return jax.shard_map(
        on_device, mesh=mesh, in_specs=in_specs, out_specs=out_specs, check_vma=False
    )
```

profile of v0, /device:TPU:1, one launch (start us, length us, event | category | flops | bytes accessed | tf_op | source)
XLA Modules:
  0.0 224.0 jit_solution(8939681321336374417)
XLA Ops:
  0.6 1.5 collective-permute-start
  2.1 0.7 reshape.543
  5.4 1.4 pad.8
  7.6 215.8 %conditional.1 = (f32[256,256]{1,0:T(8,128)}, f32[3,4,256]{2,1,0:T(4,128)}, f32[1,4,256]{2,1,0:T(4,128)}, f32[1,4,256]{2,1,0:T(4,128)}, f32[1,4,256]{2,1,0:T(4,1...) conditional(s32[]{:T(128)} %clamp.3, (s32[4,4]{1,0:T(4,128)}, ...), branch_computations={%region_5.10_spmd, %region_10.15_spmd, %region_15.20_spmd} | conditional | flops 928567 | bytes 60719288 | solution.py:523
  7.6 2.2 pick.3
  10.5 6.8 %all-to-all-start = ((bf16[16,160,256]{2,1,0:T(8,128)(2,1)}), bf16[16,160,256]{2,1,0:T(8,128)(2,1)S(1)}, u32[]{:S(2)}, u32[]{:S(2)}) async-start(bf16[16,160,256]{2,1,0:T(8,128)(2,1)} %get-tuple-element.107), calls=%async_computation | async-start | bytes 2621440 | tf_op jit(solution)/shard_map/cond/branch_0_fun/all_to_all | solution.py:395
  19.1 15.7 %all_gather.4 = bf16[8,4,40,256]{3,2,1,0:T(8,128)(2,1)} all-gather(bf16[1,4,40,256]{3,2,1,0:T(8,128)(2,1)S(1)} %maximum_maximum_fusion), channel_id=1, replica_groups=mesh['task'=8,'mp'=16] {'task'}, dimensions={0}, use_global_device_ids=true | all-gather | bytes 737280 | tf_op jit(solution)/shard_map/cond/branch_0_fun/all_gather | solution.py:424
  34.8 2.0 copy.63
  37.0 9.6 %embed.3 = (bf16[160,1024]{1,0:T(8,128)(2,1)S(1)}, bf16[160,1024]{1,0:T(8,128)(2,1)S(1)}, bf16[160,1024]{1,0:T(8,128)(2,1)S(1)}, bf16[160,1024]{1,0:T(8,128)(2,1...) custom-call(s32[4,8]{1,0:T(4,128)S(1)} %fusion.9.at_ref, ...), custom_call_target="tpu_custom_call" | custom-call | tf_op jit(solution)/shard_map/cond/branch_0_fun/embed/pallas_call | solution.py:291
  48.8 0.7 copy-done.17
  51.0 1.0 copy-done.18
  52.0 4.5 %gates.12 = (f32[160,768]{1,0:T(8,128)S(1)}, f32[16,2,256]{2,1,0:T(2,128)}) custom-call(bf16[160,1024]{1,0:T(8,128)(2,1)S(1)} %copy-done.18, bf16[16,160,256]{2,1,0:T(8,128)(2,1)S(1)} %all-to-all-done.x_ref, bf16[3,5120,256]{2,1,0:T(8,128)(2,1)} %get-tuple-element.126.w_ref), custom_call_target="tpu_custom_call" | custom-call | tf_op jit(solution)/shard_map/cond/branch_0_fun/gates/pallas_call | solution.py:309
  56.5 6.9 %all-to-all-start.1 = ((f32[16,2,256]{2,1,0:T(2,128)}), f32[16,2,256]{2,1,0:T(2,128)S(1)}, u32[]{:S(2)}, u32[]{:S(2)}) async-start(f32[16,2,256]{2,1,0:T(2,128)} %get-tuple-element.128), calls=%async_computation.1 | async-start | bytes 65536 | tf_op jit(solution)/shard_map/cond/branch_0_fun/all_to_all | solution.py:395
  63.6 6.7 %prior.12 = f32[8,256]{1,0:T(8,128)S(1)} custom-call(bf16[16,160,256]{2,1,0:T(8,128)(2,1)S(1)} %all-to-all-done.x_ref, bf16[4096,1024]{1,0:T(8,128)(2,1)} %get-tuple-element.129.w_ref, bf16[1024,1024]{1,0:T(8,128)(2,1)} %get-tuple-element.130.logit_ref, bf16[8,1024]{1,0:T(8,128)(2,1)S(1)} %get-tuple-element.131.head_ref, bf16[160,40]{1,0:T(8,128)(2,1)S(1)} %copy-done.48, ...), custom_call_target="tpu_custom_call" | custom-call | tf_op jit(solution)/shard_map/cond/branch_0_fun/prior/pallas_call | solution.py:341
  70.8 25.6 %all_to_all.108.x_ref = bf16[16,160,256]{2,1,0:T(8,128)(2,1)S(1)} all-to-all(bf16[16,160,256]{2,1,0:T(8,128)(2,1)S(1)} %get-tuple-element.136), channel_id=1, replica_groups=mesh['task'=8,'mp'=16] {'mp'}, dimensions={0} | all-to-all | bytes 2621440 | tf_op jit(solution)/shard_map/cond/branch_0_fun/all_to_all | solution.py:395
  96.4 4.5 %gates.13 = (f32[160,768]{1,0:T(8,128)S(1)}, f32[16,2,256]{2,1,0:T(2,128)}) custom-call(bf16[160,1024]{1,0:T(8,128)(2,1)S(1)} %copy-done.16, bf16[16,160,256]{2,1,0:T(8,128)(2,1)S(1)} %all_to_all.108.x_ref, bf16[3,5120,256]{2,1,0:T(8,128)(2,1)} %get-tuple-element.126.w_ref), custom_call_target="tpu_custom_call" | custom-call | tf_op jit(solution)/shard_map/cond/branch_0_fun/gates/pallas_call | solution.py:309
  101.0 3.5 %all-to-all-start.3 = ((f32[16,2,256]{2,1,0:T(2,128)}), f32[16,2,256]{2,1,0:T(2,128)S(1)}, u32[]{:S(2)}, u32[]{:S(2)}) async-start(f32[16,2,256]{2,1,0:T(2,128)} %get-tuple-element.138), calls=%async_computation.3 | async-start | bytes 65536 | tf_op jit(solution)/shard_map/cond/branch_0_fun/all_to_all | solution.py:395
  104.6 6.7 %prior.13 = f32[8,256]{1,0:T(8,128)S(1)} custom-call(bf16[16,160,256]{2,1,0:T(8,128)(2,1)S(1)} %all_to_all.108.x_ref, bf16[4096,1024]{1,0:T(8,128)(2,1)} %get-tuple-element.129.w_ref, bf16[1024,1024]{1,0:T(8,128)(2,1)} %get-tuple-element.130.logit_ref, bf16[8,1024]{1,0:T(8,128)(2,1)S(1)} %get-tuple-element.131.head_ref, bf16[160,40]{1,0:T(8,128)(2,1)S(1)} %copy-done.46, ...), custom_call_target="tpu_custom_call" | custom-call | tf_op jit(solution)/shard_map/cond/branch_0_fun/prior/pallas_call | solution.py:341
  111.8 24.2 %all_to_all.109.x_ref = bf16[16,160,256]{2,1,0:T(8,128)(2,1)S(1)} all-to-all(bf16[16,160,256]{2,1,0:T(8,128)(2,1)S(1)} %get-tuple-element.143), channel_id=1, replica_groups=mesh['task'=8,'mp'=16] {'mp'}, dimensions={0} | all-to-all | bytes 2621440 | tf_op jit(solution)/shard_map/cond/branch_0_fun/all_to_all | solution.py:395
  136.1 4.5 %gates.14 = (f32[160,768]{1,0:T(8,128)S(1)}, f32[16,2,256]{2,1,0:T(2,128)}) custom-call(bf16[160,1024]{1,0:T(8,128)(2,1)S(1)} %copy-done.14, bf16[16,160,256]{2,1,0:T(8,128)(2,1)S(1)} %all_to_all.109.x_ref, bf16[3,5120,256]{2,1,0:T(8,128)(2,1)} %get-tuple-element.126.w_ref), custom_call_target="tpu_custom_call" | custom-call | tf_op jit(solution)/shard_map/cond/branch_0_fun/gates/pallas_call | solution.py:309
  140.6 3.7 %all-to-all-start.5 = ((f32[16,2,256]{2,1,0:T(2,128)}), f32[16,2,256]{2,1,0:T(2,128)S(1)}, u32[]{:S(2)}, u32[]{:S(2)}) async-start(f32[16,2,256]{2,1,0:T(2,128)} %get-tuple-element.145), calls=%async_computation.5 | async-start | bytes 65536 | tf_op jit(solution)/shard_map/cond/branch_0_fun/all_to_all | solution.py:395
  144.4 6.7 %prior.14 = f32[8,256]{1,0:T(8,128)S(1)} custom-call(bf16[16,160,256]{2,1,0:T(8,128)(2,1)S(1)} %all_to_all.109.x_ref, bf16[4096,1024]{1,0:T(8,128)(2,1)} %get-tuple-element.129.w_ref, bf16[1024,1024]{1,0:T(8,128)(2,1)} %get-tuple-element.130.logit_ref, bf16[8,1024]{1,0:T(8,128)(2,1)S(1)} %get-tuple-element.131.head_ref, ...), custom_call_target="tpu_custom_call" | custom-call | tf_op jit(solution)/shard_map/cond/branch_0_fun/prior/pallas_call | solution.py:341
  151.6 22.3 %all_to_all.110.x_ref = bf16[16,160,256]{2,1,0:T(8,128)(2,1)S(1)} all-to-all(bf16[16,160,256]{2,1,0:T(8,128)(2,1)S(1)} %get-tuple-element.151), channel_id=1, replica_groups=mesh['task'=8,'mp'=16] {'mp'}, dimensions={0} | all-to-all | bytes 2621440 | tf_op jit(solution)/shard_map/cond/branch_0_fun/all_to_all | solution.py:395
  174.0 4.5 %gates.15 = (f32[160,768]{1,0:T(8,128)S(1)}, f32[16,2,256]{2,1,0:T(2,128)}) custom-call(bf16[160,1024]{1,0:T(8,128)(2,1)S(1)} %copy-done.12, bf16[16,160,256]{2,1,0:T(8,128)(2,1)S(1)} %all_to_all.110.x_ref, bf16[3,5120,256]{2,1,0:T(8,128)(2,1)} %get-tuple-element.126.w_ref), custom_call_target="tpu_custom_call" | custom-call | tf_op jit(solution)/shard_map/cond/branch_0_fun/gates/pallas_call | solution.py:309
  178.5 3.5 %all-to-all-start.7 = ((f32[16,2,256]{2,1,0:T(2,128)}), f32[16,2,256]{2,1,0:T(2,128)S(1)}, u32[]{:S(2)}, u32[]{:S(2)}) async-start(f32[16,2,256]{2,1,0:T(2,128)} %get-tuple-element.153), calls=%async_computation.7 | async-start | bytes 65536 | tf_op jit(solution)/shard_map/cond/branch_0_fun/all_to_all | solution.py:395
  182.2 6.7 %prior.15 = f32[8,256]{1,0:T(8,128)S(1)} custom-call(bf16[16,160,256]{2,1,0:T(8,128)(2,1)S(1)} %all_to_all.110.x_ref, bf16[4096,1024]{1,0:T(8,128)(2,1)} %get-tuple-element.129.w_ref, bf16[1024,1024]{1,0:T(8,128)(2,1)} %get-tuple-element.130.logit_ref, bf16[8,1024]{1,0:T(8,128)(2,1)S(1)} %get-tuple-element.131.head_ref, ...), custom_call_target="tpu_custom_call" | custom-call | tf_op jit(solution)/shard_map/cond/branch_0_fun/prior/pallas_call | solution.py:341
  188.9 1.1 renew.15
  190.3 1.1 broadcast_in_dim.221
  191.4 9.7 %all-to-all-start.8 = ((bf16[8,288,256]{2,1,0:T(8,128)(2,1)}), bf16[8,288,256]{2,1,0:T(8,128)(2,1)S(1)}, u32[]{:S(2)}, u32[]{:S(2)}) async-start(bf16[8,288,256]{2,1,0:T(8,128)(2,1)} %broadcast_in_dim.221), calls=%async_computation.8 | async-start | bytes 2359296 | tf_op jit(solution)/shard_map/cond/branch_0_fun/all_to_all | solution.py:395
  201.7 15.9 %all-to-all-done.8.got_ref = bf16[8,288,256]{2,1,0:T(8,128)(2,1)S(1)} async-done(((bf16[8,288,256]{2,1,0:T(8,128)(2,1)}), bf16[8,288,256]{2,1,0:T(8,128)(2,1)S(1)}, u32[]{:S(2)}, u32[]{:S(2)}) %all-to-all-start.8) | async-done | bytes 1179680 | tf_op jit(solution)/shard_map/cond/branch_0_fun/all_to_all | solution.py:395
  217.6 2.4 %settle.3 = (f32[256,256]{1,0:T(8,128)}, f32[3,4,256]{2,1,0:T(4,128)}) custom-call(s32[2,8]{1,0:T(2,128)S(1)} %pad_add_fusion.at_ref, bf16[8,288,256]{2,1,0:T(8,128)(2,1)S(1)} %all-to-all-done.8.got_ref, bf16[8,24,256]{2,1,0:T(8,128)(2,1)S(1)} %slice.186.outs_ref, s32[4,256]{1,0:T(4,128)S(1)} %broadcast_add_fusion.to_ref), custom_call_target="tpu_custom_call" | custom-call | tf_op jit(solution)/shard_map/cond/branch_0_fun/settle/pallas_call | solution.py:378
  220.0 1.3 fusion.40
  (124 shorter events, 14.3 us)
Async XLA Ops:
  0.6 6.9 %collective-permute-start = (f32[256,256]{1,0:T(8,128)}, f32[256,256]{1,0:T(8,128)S(1)}, u32[]{:S(2)}, u32[]{:S(2)}) collective-permute-start(f32[256,256]{1,0:T(8,128)} %param.14), channel_id=1, source_target_pairs={{0,16},{16,0},{32,48},{48,32},{64,80},{80,64},{96,112},{112,96},{1... | collective-permute-start | bytes 786440 | tf_op jit(solution)/shard_map/ppermute | solution.py:495
  3.1 0.6 copy-start.58
  7.6 11.4 %copy-start.72 = (s32[8]{0:T(128)}, s32[8]{0:T(128)S(1)}, u32[]{:S(2)}) copy-start(s32[8]{0:T(128)S(1)} %get-tuple-element.108) | copy-start | bytes 100 | tf_op jit(solution)/shard_map/cond
  7.6 9.8 %copy-start.65 = (s32[4,4]{1,0:T(4,128)S(1)}, s32[4,4]{1,0:T(4,128)}, u32[]{:S(2)}) copy-start(s32[4,4]{1,0:T(4,128)} %get-tuple-element.446) | copy-start | bytes 196 | tf_op jit(solution)/shard_map/cond
  7.6 11.3 %copy-start.62 = (s32[4,256]{1,0:T(4,128)S(1)}, s32[4,256]{1,0:T(4,128)}, u32[]{:S(2)}) copy-start(s32[4,256]{1,0:T(4,128)} %get-tuple-element.110) | copy-start | bytes 12292 | tf_op jit(solution)/shard_map/cond
  7.6 11.3 %copy-start.54 = (s32[4,32,256]{2,1,0:T(8,128)S(1)}, s32[4,32,256]{2,1,0:T(8,128)}, u32[]{:S(2)}) copy-start(s32[4,32,256]{2,1,0:T(8,128)} %get-tuple-element.109) | copy-start | bytes 393220 | tf_op jit(solution)/shard_map/cond
  9.8 0.7 copy-start.29
  10.5 40.5 %all-to-all-start = ((bf16[16,160,256]{2,1,0:T(8,128)(2,1)}), bf16[16,160,256]{2,1,0:T(8,128)(2,1)S(1)}, u32[]{:S(2)}, u32[]{:S(2)}) async-start(bf16[16,160,256]{2,1,0:T(8,128)(2,1)} %get-tuple-element.107), calls=%async_computation | async-start | bytes 2621440 | tf_op jit(solution)/shard_map/cond/branch_0_fun/all_to_all | solution.py:395
  34.8 2.0 copy-start.73
  34.8 2.1 copy-start.70
  37.0 13.7 %copy-start.83 = (s32[64]{0:T(128)S(1)}, s32[64]{0:T(128)}, u32[]{:S(2)}) copy-start(s32[64]{0:T(128)} %get-tuple-element.133) | copy-start | bytes 772 | tf_op jit(solution)/shard_map/cond
  46.6 0.7 copy-start.11
  47.3 0.7 copy-start.13
  48.0 0.7 copy-start.15
  48.8 0.7 copy-start.17
  49.5 0.6 copy-start.45
  50.1 0.6 copy-start.47
  51.0 1.0 copy-start.18
  52.0 11.6 %copy-start.48 = (bf16[160,40]{1,0:T(8,128)(2,1)S(1)}, bf16[160,40]{1,0:T(8,128)(2,1)}, u32[]{:S(2)}) copy-start(bf16[160,40]{1,0:T(8,128)(2,1)} %copy-done.47) | copy-start | bytes 38404 | tf_op jit(solution)/shard_map/cond
  56.5 13.8 %all-to-all-start.1 = ((f32[16,2,256]{2,1,0:T(2,128)}), f32[16,2,256]{2,1,0:T(2,128)S(1)}, u32[]{:S(2)}, u32[]{:S(2)}) async-start(f32[16,2,256]{2,1,0:T(2,128)} %get-tuple-element.128), calls=%async_computation.1 | async-start | bytes 65536 | tf_op jit(solution)/shard_map/cond/branch_0_fun/all_to_all | solution.py:395
  63.6 6.7 %copy-start.30 = (f32[160,256]{1,0:T(8,128)S(1)}, f32[160,256]{1,0:T(8,128)}, u32[]{:S(2)}) copy-start(f32[160,256]{1,0:T(8,128)} %copy-done.29) | copy-start | bytes 491524 | tf_op jit(solution)/shard_map/cond
  70.3 26.1 %copy-start.16 = (bf16[160,1024]{1,0:T(8,128)(2,1)S(1)}, bf16[160,1024]{1,0:T(8,128)(2,1)}, u32[]{:S(2)}) copy-start(bf16[160,1024]{1,0:T(8,128)(2,1)} %copy-done.15) | copy-start | bytes 983044 | tf_op jit(solution)/shard_map/cond
  96.4 8.2 %copy-start.46 = (bf16[160,40]{1,0:T(8,128)(2,1)S(1)}, bf16[160,40]{1,0:T(8,128)(2,1)}, u32[]{:S(2)}) copy-start(bf16[160,40]{1,0:T(8,128)(2,1)} %copy-done.45) | copy-start | bytes 38404 | tf_op jit(solution)/shard_map/cond
  101.0 10.4 %all-to-all-start.3 = ((f32[16,2,256]{2,1,0:T(2,128)}), f32[16,2,256]{2,1,0:T(2,128)S(1)}, u32[]{:S(2)}, u32[]{:S(2)}) async-start(f32[16,2,256]{2,1,0:T(2,128)} %get-tuple-element.138), calls=%async_computation.3 | async-start | bytes 65536 | tf_op jit(solution)/shard_map/cond/branch_0_fun/all_to_all | solution.py:395
  111.3 24.7 %copy-start.14 = (bf16[160,1024]{1,0:T(8,128)(2,1)S(1)}, bf16[160,1024]{1,0:T(8,128)(2,1)}, u32[]{:S(2)}) copy-start(bf16[160,1024]{1,0:T(8,128)(2,1)} %copy-done.13) | copy-start | bytes 983044 | tf_op jit(solution)/shard_map/cond
  140.6 10.5 %all-to-all-start.5 = ((f32[16,2,256]{2,1,0:T(2,128)}), f32[16,2,256]{2,1,0:T(2,128)S(1)}, u32[]{:S(2)}, u32[]{:S(2)}) async-start(f32[16,2,256]{2,1,0:T(2,128)} %get-tuple-element.145), calls=%async_computation.5 | async-start | bytes 65536 | tf_op jit(solution)/shard_map/cond/branch_0_fun/all_to_all | solution.py:395
  151.1 22.8 %copy-start.12 = (bf16[160,1024]{1,0:T(8,128)(2,1)S(1)}, bf16[160,1024]{1,0:T(8,128)(2,1)}, u32[]{:S(2)}) copy-start(bf16[160,1024]{1,0:T(8,128)(2,1)} %copy-done.11) | copy-start | bytes 983044 | tf_op jit(solution)/shard_map/cond
  178.5 10.4 %all-to-all-start.7 = ((f32[16,2,256]{2,1,0:T(2,128)}), f32[16,2,256]{2,1,0:T(2,128)S(1)}, u32[]{:S(2)}, u32[]{:S(2)}) async-start(f32[16,2,256]{2,1,0:T(2,128)} %get-tuple-element.153), calls=%async_computation.7 | async-start | bytes 65536 | tf_op jit(solution)/shard_map/cond/branch_0_fun/all_to_all | solution.py:395
  190.3 10.8 %copy-start.59 = (s32[4,16]{1,0:T(4,128)S(1)}, s32[4,16]{1,0:T(4,128)}, u32[]{:S(2)}) copy-start(s32[4,16]{1,0:T(4,128)} %get-tuple-element.103) | copy-start | bytes 772 | tf_op jit(solution)/shard_map/cond
  190.3 10.9 %copy-start.69 = (s32[4,4]{0,1:T(4,128)S(1)}, s32[4,4]{0,1:T(4,128)}, u32[]{:S(2)}) copy-start(s32[4,4]{0,1:T(4,128)} %get-tuple-element.497) | copy-start | bytes 196 | tf_op jit(solution)/shard_map/cond
  191.4 26.2 %all-to-all-start.8 = ((bf16[8,288,256]{2,1,0:T(8,128)(2,1)}), bf16[8,288,256]{2,1,0:T(8,128)(2,1)S(1)}, u32[]{:S(2)}, u32[]{:S(2)}) async-start(bf16[8,288,256]{2,1,0:T(8,128)(2,1)} %broadcast_in_dim.221), calls=%async_computation.8 | async-start | bytes 2359296 | tf_op jit(solution)/shard_map/cond/branch_0_fun/all_to_all | solution.py:395
  223.4 0.6 copy-start.78
  (2 other events, 1.2 us)
where the time goes:
time: 225 us; the launch traced here: 224 us
  blocking collectives  87.8 us (39%)
  Pallas kernels  61.7 us (27%)
  starting transfers between devices  35.7 us (16%)
  local copies, waits for them, and re-layouts  18.3 us (8%)
  waiting for transfers between devices  15.9 us (7%)
  other arithmetic  2.83 us (1%)
    all_to_all x3, blocking collectives, exchange(): return lax.all_to_all(copies, axis, 0, 0, tiled=True)  72.1 us
    all_to_all x6, starting transfers between devices, exchange(): return lax.all_to_all(copies, axis, 0, 0, tiled=True)  34.2 us
    pallas_call x4, Pallas kernels, prior(): pl.pallas_call(prior_kernel, in_specs=[WHOLE, STAY, STAY, WHOLE, WHOLE, W...  26.7 us
    pallas_call x4, Pallas kernels, gates(): pl.pallas_call(gates_kernel, in_specs=[WHOLE, WHOLE, STAY], out_shape=[ja...  18.1 us
    all_to_all x6, waiting for transfers between devices, exchange(): return lax.all_to_all(copies, axis, 0, 0, tiled=True)  15.9 us
    all_gather x1, blocking collectives, window(): everyone = jnp.transpose(lax.all_gather(sent, 'task'), (1, 0, 3, 2))  15.7 us
    pallas_call x1, Pallas kernels, embed(): pl.pallas_call(embed_kernel, in_specs=[SCALARS, WHOLE, WHOLE, WHOLE], out...  9.6 us
    cond x49, local copies, waits for them, and re-layouts  7.88 us
  transfers between devices with their start and end apart: 7, of which 1 were waited for; matrix products, arithmetic and copies ran while one was open for 4% of the time, Pallas kernels for 16%

commit v1 on v0

--- a/solution.py
+++ b/solution.py
@@ -14,10 +14,10 @@
 BLK_DEV = 4
 STEPS = 4
 WSTART = 16
-ACT_PAD = 32
 DEPTH = 40
-LEVELS = (5, 6, 8)
+LEVELS = (6, 8)
 PIECE = 32
+ROLLED = (8,)
 F32 = jnp.float32
 BF16 = jnp.bfloat16
 I32 = jnp.int32
@@ -59,35 +59,62 @@
     return jnp.concatenate([ref[q] for q in range(ref.shape[0])], axis=1)
 
 
-def embed_kernel(at_ref, ev_ref, stoch_ref, act_ref, *refs):
-    steps = ev_ref.shape[0]
-    outs, all_picks, (hot_ref, pre_ref) = refs[:steps], refs[steps : 2 * steps], refs[2 * steps :]
-    rows = pre_ref.shape[0]
+def embed_kernel(
+    at_ref, ev_hbm, stoch_hbm, act_ref, out_hbm, hot_hbm,
+    picks_ref, stoch_ref, hot_ref, out_ref, sem, done_sem,
+):
+    steps, rows, _ = hot_ref.shape
+    count = rows // PIECE
+
+    def fetch(step, k):
+        at = pl.ds(pl.multiple_of(at_ref[step, k], PIECE), PIECE)
+        to = pl.ds(k * PIECE, PIECE)
+        return pltpu.make_async_copy(ev_hbm.at[step, at], picks_ref.at[step, to], sem.at[step, k])
+
+    def give(step, q):
+        ref, hbm = ((hot_ref, hot_hbm), (out_ref, out_hbm))[q]
+        return pltpu.make_async_copy(ref.at[step], hbm.at[step], done_sem.at[q, step])
+
+    def start(step, _):
+        for k in range(count):
+            fetch(step, k).start()
+        return 0
+
+    lax.fori_loop(0, steps, start, 0)
+    table = pltpu.make_async_copy(stoch_hbm, stoch_ref, done_sem.at[2, 0])
+    table.start()
     spread = spread_matrix()
-    ids = lax.broadcasted_iota(I32, (PIECE, ACT_PAD), 1).astype(F32)
-    for step in range(steps):
-        picks_ref, out_ref = all_picks[step], outs[step]
-
-        def mark(k, _, step=step, picks_ref=picks_ref):
-            at = pl.ds(pl.multiple_of(k * PIECE, PIECE), PIECE)
-            wanted = ev_ref[step, pl.ds(pl.multiple_of(at_ref[step, k], PIECE), PIECE)]
-            picks_ref[at] = wanted
-            hot_ref[at, :HID] = chosen_mask(wanted[:, :GROUPS], spread).astype(F32).astype(BF16)
-            action = wanted[:, GROUPS : GROUPS + 1].astype(F32)
-            hot_ref[at, HID:] = (ids == action).astype(F32).astype(BF16)
-            return 0
-
-        lax.fori_loop(0, rows // PIECE, mark, 0)
-        pre_ref[...] = jnp.dot(
-            hot_ref[:, :HID], stoch_ref[...], preferred_element_type=F32
-        ) + jnp.dot(hot_ref[:, HID:], act_ref[...], preferred_element_type=F32)
-
-        def finish(k, _, out_ref=out_ref):
-            at = pl.ds(pl.multiple_of(k * PIECE, PIECE), PIECE)
-            out_ref[at] = silu(row_norm(pre_ref[at])).astype(BF16)
-            return 0
-
-        lax.fori_loop(0, rows // PIECE, finish, 0)
+    ids = lax.broadcasted_iota(I32, (rows, act_ref.shape[0]), 1).astype(F32)
+
+    def make(step, _):
+        for k in range(count):
+            fetch(step, k).wait()
+        wanted = picks_ref[step]
+        hot = chosen_mask(wanted[:, :GROUPS], spread).astype(F32).astype(BF16)
+        hot_ref[step] = hot
+        give(step, 0).start()
+
+        @pl.when(step == 0)
+        def _():
+            table.wait()
+
+        action = wanted[:, GROUPS : GROUPS + 1].astype(F32)
+        act_hot = (ids == action).astype(F32).astype(BF16)
+        pre = jnp.dot(hot, stoch_ref[...], preferred_element_type=F32) + jnp.dot(
+            act_hot, act_ref[...], preferred_element_type=F32
+        )
+        out_ref[step] = silu(row_norm(pre)).astype(BF16)
+        give(step, 1).start()
+        return 0
+
+    lax.fori_loop(0, steps, make, 0)
+
+    def finish(step, _):
+        give(step, 0).wait()
+        give(step, 1).wait()
+        return 0
+
+    lax.fori_loop(0, steps, finish, 0)
 
 
 def full_lanes(part):
@@ -101,7 +128,7 @@
     return jnp.transpose(jnp.broadcast_to(row, (128, row.shape[1])))[:rows]
 
 
-def gates_kernel(emb_ref, x_ref, w_ref, g_ref, stat_ref, wbuf, sem):
+def gates_kernel(step, emb_hbm, x_ref, w_ref, g_hbm, stat_ref, g_ref, wbuf, emb_ref, sem):
     parts, depth, share = w_ref.shape
     chunks = depth // HID
 
@@ -109,9 +136,12 @@
         at = pl.ds(pl.multiple_of(c * HID, HID), HID)
         return pltpu.make_async_copy(w_ref.at[:, at, :], wbuf.at[c], sem.at[c])
 
+    emb = pltpu.make_async_copy(emb_hbm.at[step], emb_ref, sem.at[chunks])
+    emb.start()
     for c in range(chunks):
         fetch(c).start()
     per = HID // share
+    emb.wait()
     fetch(0).wait()
     for k in range(parts):
         g_ref[:, k * share : (k + 1) * share] = jnp.dot(
@@ -128,6 +158,8 @@
         return 0
 
     lax.fori_loop(1, chunks, add, 0)
+    out = pltpu.make_async_copy(g_ref, g_hbm, sem.at[chunks])
+    out.start()
     rows, width = g_ref.shape
     part = jnp.zeros((rows, 128), F32)
     part_sq = part
@@ -144,16 +176,28 @@
     )
     for q in range(stat_ref.shape[0]):
         stat_ref[q] = sums
-
-
-def update_kernel(entries, g_ref, stat_ref, carried_ref, live_ref, new_ref, low_ref):
+    out.wait()
+
+
+def update_kernel(
+    entries, step, g_hbm, stat_ref, carried_hbm, live_ref, new_hbm, low_ref,
+    g_ref, carried_ref, new_ref, sem,
+):
+    copies = [
+        pltpu.make_async_copy(g_hbm, g_ref, sem.at[0]),
+        pltpu.make_async_copy(carried_hbm, carried_ref, sem.at[1]),
+    ]
+    for copy in copies:
+        copy.start()
     sums = jnp.sum(stat_ref[...], axis=0) / entries
     avg = sums[0:1]
     inv = lax.rsqrt(sums[1:2] - avg * avg + 1e-5)
     rows, share = carried_ref.shape
     avg_l = lanes_from_row(avg, rows)
     inv_l = lanes_from_row(inv, rows)
-    live_l = lanes_from_row(live_ref[...], rows)
+    live_l = lanes_from_row(live_ref[pl.ds(step, 1), :], rows)
+    for copy in copies:
+        copy.wait()
     for q in range(share // 128):
         def normed(part):
             at = part * share + q * 128
@@ -169,6 +213,9 @@
         low = renewed.astype(BF16)
         for k in range(low_ref.shape[0]):
             low_ref[k, :, q * 128 : (q + 1) * 128] = low
+    out = pltpu.make_async_copy(new_ref, new_hbm, sem.at[2])
+    out.start()
+    out.wait()
 
 
 def two_parts(values):
@@ -177,8 +224,8 @@
 
 
 def prior_kernel(
-    x_ref, w_ref, logit_ref, head_ref, picks_ref, live_ref, out_ref,
-    wbuf, lbuf, pre_ref, hid_ref, parts_ref, sem,
+    step, x_hbm, w_ref, logit_ref, head_ref, hot_hbm, live_ref, out_ref,
+    x_ref, wbuf, lbuf, pre_ref, hid_ref, hot_ref, parts_ref, sem,
 ):
     shards, rows, share = x_ref.shape
     chunks = w_ref.shape[0] // HID
@@ -188,11 +235,16 @@
         at = pl.ds(pl.multiple_of(c * HID, HID), HID)
         return pltpu.make_async_copy(w_ref.at[at], wbuf.at[c], sem.at[c])
 
+    state = pltpu.make_async_copy(x_hbm, x_ref, sem.at[chunks + 2])
+    state.start()
     for c in range(chunks):
         fetch(c).start()
     last = pltpu.make_async_copy(logit_ref, lbuf, sem.at[chunks])
     last.start()
+    marks = pltpu.make_async_copy(hot_hbm.at[step], hot_ref, sem.at[chunks + 1])
+    marks.start()
     pre_ref[...] = jnp.zeros(pre_ref.shape, F32)
+    state.wait()
 
     def add(c, _):
         left = jnp.concatenate([x_ref[c * per + q] for q in range(per)], axis=1)
@@ -209,6 +261,7 @@
 
     lax.fori_loop(0, rows // PIECE, squash, 0)
     last.wait()
+    marks.wait()
     across = (((1,), (1,)), ((), ()))
     heads = lax.dot_general(head_ref[...], hid_ref[...], across, preferred_element_type=F32)
     pre_ref[...] = jnp.dot(hid_ref[...], lbuf[...], preferred_element_type=F32)
@@ -216,11 +269,12 @@
 
     def classes(k, _):
         at = pl.ds(pl.multiple_of(k * PIECE, PIECE), PIECE)
-        exponent = jnp.exp(5.0 * jnp.tanh(pre_ref[at] / 5.0))
-        wanted = picks_ref[at, :GROUPS]
-        chosen = jnp.where(chosen_mask(wanted, spread), exponent, 0.0)
-        parts_ref[0, at], parts_ref[1, at] = two_parts(exponent)
-        parts_ref[2, at], parts_ref[3, at] = two_parts(chosen)
+        high, low = two_parts(jnp.exp(5.0 * jnp.tanh(pre_ref[at] / 5.0)))
+        hot = hot_ref[at]
+        parts_ref[0, at] = high
+        parts_ref[1, at] = low
+        parts_ref[2, at] = high * hot
+        parts_ref[3, at] = low * hot
         return 0
 
     lax.fori_loop(0, rows // PIECE, classes, 0)
@@ -232,7 +286,7 @@
 
     chances = 0.99 * over_groups(2) / over_groups(0) + 0.01 / CLASSES
     log_prob = jnp.sum(jnp.log(chances), axis=0, keepdims=True)
-    live = live_ref[:, :rows]
+    live = live_ref[pl.ds(step, 1), :rows]
     out_ref[...] = jnp.zeros(out_ref.shape, F32)
     out_ref[0:1, :rows] = log_prob * live
     out_ref[1:2, :rows] = heads[0:1] * live
@@ -256,7 +310,9 @@
             rest_ref[0][(i - done) * per_task : (i - done + 1) * per_task] = low
 
 
-def settle_kernel(at_ref, got_ref, outs_ref, to_ref, final_ref, small_ref, buf, sem):
+def settle_kernel(
+    at_ref, got_ref, outs_ref, to_ref, log_ref, reward_ref, cont_ref, final_ref, buf, sem
+):
     count, per_task, share = buf.shape
     copies = []
     for i in range(count):
@@ -269,9 +325,9 @@
         values = jnp.dot(
             parts, selector(parts.shape[1], to_ref[t : t + 1]), preferred_element_type=F32
         )
-        for k in range(3):
+        for k, ref in enumerate((log_ref, reward_ref, cont_ref)):
             at = t * 3 + k
-            small_ref[k, t : t + 1, :] = values[at : at + 1] + values[12 + at : 13 + at]
+            ref[t : t + 1] = values[at : at + 1] + values[12 + at : 13 + at]
     for i in range(count):
         copies[i].wait()
         final_ref[i * per_task : (i + 1) * per_task] = buf[i].astype(F32)
@@ -286,73 +342,117 @@
 SCALARS = pl.BlockSpec(memory_space=pltpu.SMEM)
 
 
+def placed(specs, operands):
+    return tuple(
+        pltpu.with_memory_space_constraint(o, pltpu.HBM) if s is STAY else o
+        for s, o in zip(specs, operands, strict=True)
+    )
+
+
 def embed(at, everyone, stoch, act, rows):
     steps, _, depth = everyone.shape
-    made = pl.pallas_call(
+    return pl.pallas_call(
         embed_kernel,
-        in_specs=[SCALARS, WHOLE, WHOLE, WHOLE],
-        out_shape=[jax.ShapeDtypeStruct((rows, HID), BF16)] * steps
-        + [jax.ShapeDtypeStruct((rows, depth), BF16)] * steps,
+        in_specs=[SCALARS, STAY, STAY, WHOLE],
+        out_specs=[STAY, STAY],
+        out_shape=[pltpu.HBM((steps, rows, HID), BF16)] * 2,
         scratch_shapes=[
-            pltpu.VMEM((rows, HID + ACT_PAD), BF16),
-            pltpu.VMEM((rows, HID), F32),
-        ],
-        compiler_params=params(20),
+            pltpu.VMEM((steps, rows, depth), BF16),
+            pltpu.VMEM(stoch.shape, BF16),
+            pltpu.VMEM((steps, rows, HID), BF16),
+            pltpu.VMEM((steps, rows, HID), BF16),
+            pltpu.SemaphoreType.DMA((steps, rows // PIECE)),
+            pltpu.SemaphoreType.DMA((3, steps)),
+        ],
+        compiler_params=params(24),
         name="embed",
-    )(at, everyone, stoch, act)
-    return made[:steps], made[steps:]
-
-
-def gates(emb, x, w):
+    )(*placed([SCALARS, STAY, STAY, WHOLE], (at, everyone, stoch, act)))
+
+
+def stepped(kernel, moment, specs, operands):
+    operands = placed(specs, operands)
+    if isinstance(moment, int):
+        return functools.partial(kernel, moment), specs, operands
+
+    def with_scalar(step_ref, *refs):
+        kernel(step_ref[0], *refs)
+
+    return with_scalar, [SCALARS, *specs], (jnp.full((1,), moment, I32), *operands)
+
+
+def gates(moment, emb, x, w):
+    kernel, specs, operands = stepped(gates_kernel, moment, [STAY, WHOLE, STAY], (emb, x, w))
     shards, rows, share = x.shape
     parts, depth, _ = w.shape
     return pl.pallas_call(
-        gates_kernel,
-        in_specs=[WHOLE, WHOLE, STAY],
+        kernel,
+        in_specs=specs,
         out_shape=[
-            jax.ShapeDtypeStruct((rows, parts * share), F32),
+            pltpu.HBM((rows, parts * share), F32),
             jax.ShapeDtypeStruct((shards, 2, 256), F32),
         ],
+        out_specs=[STAY, WHOLE],
         scratch_shapes=[
+            pltpu.VMEM((rows, parts * share), F32),
             pltpu.VMEM((depth // HID, parts, HID, share), BF16),
-            pltpu.SemaphoreType.DMA((depth // HID,)),
+            pltpu.VMEM((rows, HID), BF16),
+            pltpu.SemaphoreType.DMA((depth // HID + 1,)),
         ],
         compiler_params=params(24),
         name="gates",
-    )(emb, x, w)
-
-
-def renew(g, stats, carried, live, entries):
+    )(*operands)
+
+
+def renew(moment, g, stats, carried, live, entries):
+    kernel, specs, operands = stepped(
+        functools.partial(update_kernel, entries), moment, [STAY, WHOLE, STAY, WHOLE], (g, stats, carried, live)
+    )
     rows, share = carried.shape
     return pl.pallas_call(
-        functools.partial(update_kernel, entries),
+        kernel,
+        in_specs=specs,
         out_shape=[
-            jax.ShapeDtypeStruct((rows, share), F32),
+            pltpu.HBM((rows, share), F32),
             jax.ShapeDtypeStruct((stats.shape[0], rows, share), BF16),
+        ],
+        out_specs=[STAY, WHOLE],
+        scratch_shapes=[
+            pltpu.VMEM(g.shape, F32),
+            pltpu.VMEM((rows, share), F32),
+            pltpu.VMEM((rows, share), F32),
+            pltpu.SemaphoreType.DMA((3,)),
         ],
         compiler_params=params(16),
         name="renew",
-    )(g, stats, carried, live)
-
-
-def prior(x, w, logit, head, picks, live):
+    )(*operands)
+
+
+def prior(moment, x, w, logit, head, hot, live):
+    kernel, specs, operands = stepped(
+        prior_kernel,
+        moment,
+        [STAY, STAY, STAY, WHOLE, STAY, WHOLE],
+        (x, w, logit, head, hot, live),
+    )
     rows = x.shape[1]
     chunks = w.shape[0] // HID
     return pl.pallas_call(
-        prior_kernel,
-        in_specs=[WHOLE, STAY, STAY, WHOLE, WHOLE, WHOLE],
+        kernel,
+        in_specs=specs,
         out_shape=jax.ShapeDtypeStruct((8, 256), F32),
         scratch_shapes=[
+            pltpu.VMEM(x.shape, BF16),
             pltpu.VMEM((chunks, HID, HID), BF16),
             pltpu.VMEM((HID, HID), BF16),
             pltpu.VMEM((rows, HID), F32),
             pltpu.VMEM((rows, HID), BF16),
+            pltpu.VMEM((rows, HID), BF16),
             pltpu.VMEM((4, rows, HID), BF16),
-            pltpu.SemaphoreType.DMA((chunks + 1,)),
+            pltpu.SemaphoreType.DMA((chunks + 3,)),
         ],
         compiler_params=params(28),
         name="prior",
-    )(x, w, logit, head, picks, live)
+    )(*operands)
 
 
 def pick(at, own, other, rows, shards):
@@ -378,10 +478,8 @@
     return pl.pallas_call(
         settle_kernel,
         in_specs=[SCALARS, pl.BlockSpec(memory_space=pl.ANY), WHOLE, WHOLE],
-        out_shape=[
-            jax.ShapeDtypeStruct((count * per_task, share), F32),
-            jax.ShapeDtypeStruct((3, STEPS, to.shape[1]), F32),
-        ],
+        out_shape=[jax.ShapeDtypeStruct(to.shape, F32)] * 3
+        + [jax.ShapeDtypeStruct((count * per_task, share), F32)],
         scratch_shapes=[
             pltpu.VMEM((count, per_task, share), BF16),
             pltpu.SemaphoreType.DMA((count,)),
@@ -439,8 +537,8 @@
     )
     slot = (task[None, :] // per_core + ahead_by) % holders
     source = slot * all_rows + (task % per_core)[None, :] * per_task
-    emb, picks = embed(source, everyone, stoch, act, rows)
-    x, emb, picks = lax.optimization_barrier((x, emb, picks))
+    emb, hot = embed(source, everyone, stoch, act, rows)
+    x, emb, hot = lax.optimization_barrier((x, emb, hot))
 
     held = jnp.repeat((place - running) % holders, in_block, axis=1) * per_core
     held = held + jnp.arange(per_core, dtype=I32)[None, :]
@@ -453,18 +551,31 @@
     to = jnp.where(chunk < count, core * 256 + chunk * per_task, -TASKS * 256)
     to = jnp.repeat(to, per_task, axis=1) + jnp.arange(all_rows, dtype=I32)[None, :] % per_task
 
+    def one_step(moment, x, carried):
+        g, stats = gates(moment, emb, x, w)
+        stats = exchange(stats, "mp")
+        small = prior(moment, x, prior_weight, logit, head, hot, living)
+        stats, small = lax.optimization_barrier((stats, small))
+        carried, low = renew(moment, g, stats, carried, living, entries)
+        return low, carried, small[:3]
+
     small = []
-    for moment in range(STEPS):
-        live = living[moment : moment + 1]
-        g, stats = gates(emb[moment], x, w)
-        stats = exchange(stats, "mp")
-        small.append(prior(x, prior_weight, logit, head, picks[moment], live))
-        stats, small = lax.optimization_barrier((stats, small))
-        carried, low = renew(g, stats, carried, live, entries)
-        if moment < STEPS - 1:
+    if count in ROLLED:
+
+        def body(state, moment):
+            low, carried, out = one_step(moment, *state)
+            return (exchange(low, "mp"), carried), out
+
+        (x, carried), outs = lax.scan(body, (x, carried), jnp.arange(STEPS - 1, dtype=I32))
+        small.append(outs.reshape(-1, outs.shape[2]))
+    else:
+        for moment in range(STEPS - 1):
+            low, carried, out = one_step(moment, x, carried)
+            small.append(out)
             x = exchange(low, "mp")
-
-    outs = jnp.concatenate([s[:3] for s in small], axis=0)
+    low, _, out = one_step(STEPS - 1, x, carried)
+
+    outs = jnp.concatenate([*small, out], axis=0)
     high, low_part = two_parts(outs)
     sent = jnp.concatenate([low[0], *rest, high, low_part, jnp.zeros((8, share), BF16)], axis=0)
     got = exchange(jnp.broadcast_to(sent[None], (holders, *sent.shape)), "task")
@@ -494,8 +605,7 @@
 
     other = lax.ppermute(deter, "task", [(i, i ^ 1) for i in range(holders)])
     w = jnp.transpose(gru_weight, (1, 0, 2))
-    act = jnp.pad(embed_act, ((0, ACT_PAD - embed_act.shape[0]), (0, 0)))
-    head = jnp.pad(jnp.transpose(head_weight), ((0, 6), (0, 0)))
+    head = jnp.transpose(head_weight)
 
     by_chip = horizons.reshape(TASKS // pair, pair)
     index = jnp.arange(pair, dtype=I32)
@@ -517,11 +627,10 @@
     from_task = swapped * per_core + local % per_core
     operands = (
         deter, other, draws, actions, horizons, offsets, rank, local, from_task,
-        embed_stoch, act, w, prior_weight, logit_weight, head,
+        embed_stoch, embed_act, w, prior_weight, logit_weight, head,
     )
     branches = [lambda args, n=n: window(n, args, holders, shards) for n in LEVELS]
-    final, small = lax.switch(level, branches, operands)
-    return (small[0], small[1], small[2], final)
+    return tuple(lax.switch(level, branches, operands))
 
 
 def solution(mesh):

time: 225 us -> 231 us (1.027)
  local copies, waits for them, and re-layouts: 18.3 us -> 5.28 us
  Pallas kernels: 61.7 us -> 74.4 us
  blocking collectives: 87.8 us -> 95.6 us
    pallas_call x13, Pallas kernels: 57 us -> 69.6 us  [the longest x4 28.4 us: prior(): pl.pallas_call(kernel, in_specs=specs, out_shape=jax.ShapeDtypeStruct((8,...]
    all_to_all x3, blocking collectives: 72.1 us -> 80.9 us  [exchange(): return lax.all_to_all(copies, axis, 0, 0, tiled=True)]
    cond x49 -> x22, local copies, waits for them, and re-layouts: 7.88 us -> 0.73 us
  transfers between devices with their start and end apart: 7 -> 7, of which waited for: 1 -> 1; matrix products, arithmetic and copies ran while one was open for 4% -> 2% of each run, Pallas kernels for 16% -> 16%
where the time goes in v1:
time: 231 us
  blocking collectives  95.6 us (41%)
  Pallas kernels  74.4 us (32%)
  starting transfers between devices  35 us (15%)
  waiting for transfers between devices  15.9 us (7%)
  local copies, waits for them, and re-layouts  5.28 us (2%)
    all_to_all x3, blocking collectives, exchange(): return lax.all_to_all(copies, axis, 0, 0, tiled=True)  80.9 us
    all_to_all x6, starting transfers between devices, exchange(): return lax.all_to_all(copies, axis, 0, 0, tiled=True)  33.5 us
    pallas_call x4, Pallas kernels, prior(): pl.pallas_call(kernel, in_specs=specs, out_shape=jax.ShapeDtypeStruct((8,...  28.4 us
    pallas_call x4, Pallas kernels, gates(): pl.pallas_call(kernel, in_specs=specs, out_shape=[pltpu.HBM((rows, parts...  24.3 us
    all_to_all x6, waiting for transfers between devices, exchange(): return lax.all_to_all(copies, axis, 0, 0, tiled=True)  15.9 us
    all_gather x1, blocking collectives, window(): everyone = jnp.transpose(lax.all_gather(sent, 'task'), (1, 0, 3, 2))  14.6 us
    pallas_call x4, Pallas kernels, renew(): pl.pallas_call(kernel, in_specs=specs, out_shape=[pltpu.HBM((rows, share)...  8.77 us
    pallas_call x1, Pallas kernels, embed(): pl.pallas_call(embed_kernel, in_specs=[SCALARS, STAY, STAY, WHOLE], out_s...  8.2 us
  transfers between devices with their start and end apart: 7, of which 1 were waited for; matrix products, arithmetic and copies ran while one was open for 2% of the time, Pallas kernels for 16%

profile of v1, /device:TPU:1, one launch (start us, length us, event | category | flops | bytes accessed | tf_op | source)
XLA Modules:
  0.0 230.7 jit_solution(15334815278600935367)
XLA Ops:
  0.6 1.5 collective-permute-start
  2.2 0.7 reshape.342
  4.9 225.6 %conditional.1 = ((f32[4,256]{1,0:T(4,128)}, f32[4,256]{1,0:T(4,128)}, f32[4,256]{1,0:T(4,128)}, f32[256,256]{1,0:T(8,128)})) conditional(s32[]{:T(128)} %clamp.3, (s32[4,4]{1,0:T(4,128)}, s32[4,16]{1,0:T(4,128)S(1)}, f32[256,256]{1,0:T(8,128)}, f32[256,256]{1,0:T(8,128)S(1)}, s32[8]{0:T(128)S(1)}, /*index=5*/s32[8]{0:T(128)S(1)}, ...), branch_computations={%region_5.10_spmd, %region_10.17_spmd} | conditional | flops 910137 | bytes 49271632 | solution.py:633
  4.9 2.4 %pick.2 = (f32[192,256]{1,0:T(8,128)S(1)}, bf16[16,192,256]{2,1,0:T(8,128)(2,1)}, bf16[64,256]{1,0:T(8,128)(2,1)S(1)}) custom-call(s32[8]{0:T(128)S(1)} %get-tuple-element.110.at_ref, f32[8,32,256]{2,1,0:T(8,128)} %bitcast.34, f32[8,32,256]{2,1,0:T(8,128)S(1)} %bitcast.36), custom_call_target="tpu_custom_call" | custom-call | tf_op jit(solution)/shard_map/cond/branch_0_fun/pick/pallas_call | solution.py:467
  7.3 0.7 copy-done.4
  8.0 6.8 %all-to-all-start = ((bf16[16,192,256]{2,1,0:T(8,128)(2,1)}), bf16[16,192,256]{2,1,0:T(8,128)(2,1)S(1)}, u32[]{:S(2)}, u32[]{:S(2)}) async-start(bf16[16,192,256]{2,1,0:T(8,128)(2,1)} %get-tuple-element.113), calls=%async_computation | async-start | bytes 3145728 | tf_op jit(solution)/shard_map/cond/branch_0_fun/all_to_all | solution.py:493
  15.5 14.6 %all_gather.4 = bf16[8,4,40,256]{3,2,1,0:T(8,128)(2,1)S(1)} all-gather(bf16[1,4,40,256]{3,2,1,0:T(8,128)(2,1)S(1)} %maximum_maximum_fusion), channel_id=1, replica_groups=mesh['task'=8,'mp'=16] {'task'}, dimensions={0}, use_global_device_ids=true | all-gather | bytes 737280 | tf_op jit(solution)/shard_map/cond/branch_0_fun/all_gather | solution.py:522
  30.1 1.8 copy.56
  32.0 8.2 %embed.2 = (bf16[4,192,1024]{2,1,0:T(8,128)(2,1)}, bf16[4,192,1024]{2,1,0:T(8,128)(2,1)}) custom-call(s32[4,8]{1,0:T(4,128)S(1)} %fusion.11.at_ref, bf16[4,2048,40]{2,1,0:T(8,128)(2,1)} %bitcast.30, bf16[1024,1024]{1,0:T(8,128)(2,1)} %get-tuple-element.117.stoch_hbm, bf16[18,1024]{1,0:T(8,128)(2,1)S(1)} %copy-done.12), custom_call_target="tpu_custom_call" | custom-call | tf_op jit(solution)/shard_map/cond/branch_0_fun/embed/pallas_call | solution.py:354
  40.4 6.1 %gates.6 = (f32[192,768]{1,0:T(8,128)}, f32[16,2,256]{2,1,0:T(2,128)}) custom-call(bf16[4,192,1024]{2,1,0:T(8,128)(2,1)} %get-tuple-element.121.emb_hbm, bf16[16,192,256]{2,1,0:T(8,128)(2,1)S(1)} %all-to-all-done.x_ref.x_hbm, bf16[3,5120,256]{2,1,0:T(8,128)(2,1)} %get-tuple-element.123.w_ref), custom_call_target="tpu_custom_call" | custom-call | tf_op jit(solution)/shard_map/cond/branch_0_fun/gates/pallas_call | solution.py:387
  46.5 7.0 %all-to-all-start.1 = ((f32[16,2,256]{2,1,0:T(2,128)}), f32[16,2,256]{2,1,0:T(2,128)S(1)}, u32[]{:S(2)}, u32[]{:S(2)}) async-start(f32[16,2,256]{2,1,0:T(2,128)} %get-tuple-element.125), calls=%async_computation.1 | async-start | bytes 65536 | tf_op jit(solution)/shard_map/cond/branch_0_fun/all_to_all | solution.py:493
  53.7 7.1 %prior.6 = f32[8,256]{1,0:T(8,128)S(1)} custom-call(bf16[16,192,256]{2,1,0:T(8,128)(2,1)} %copy-done, bf16[4096,1024]{1,0:T(8,128)(2,1)} %get-tuple-element.126.w_ref, bf16[1024,1024]{1,0:T(8,128)(2,1)} %get-tuple-element.127.logit_ref, bf16[2,1024]{1,0:T(2,128)(2,1)S(1)} %copy-done.10, bf16[4,192,1024]{2,1,0:T(8,128)(2,1)} %get-tuple-element.129.hot_hbm, ...), custom_call_target="tpu_custom_call" | custom-call | tf_op jit(solution)/shard_map/cond/branch_0_fun/prior/pallas_call | solution.py:439
  60.8 2.2 renew.6
  63.0 28.3 %all_to_all.62.x_ref.x_hbm = bf16[16,192,256]{2,1,0:T(8,128)(2,1)S(1)} all-to-all(bf16[16,192,256]{2,1,0:T(8,128)(2,1)S(1)} %get-tuple-element.133), channel_id=1, replica_groups=mesh['task'=8,'mp'=16] {'mp'}, dimensions={0} | all-to-all | bytes 3145728 | tf_op jit(solution)/shard_map/cond/branch_0_fun/all_to_all | solution.py:493
  91.3 6.1 %gates.7 = (f32[192,768]{1,0:T(8,128)}, f32[16,2,256]{2,1,0:T(2,128)}) custom-call(bf16[4,192,1024]{2,1,0:T(8,128)(2,1)} %get-tuple-element.121.emb_hbm, bf16[16,192,256]{2,1,0:T(8,128)(2,1)S(1)} %all_to_all.62.x_ref.x_hbm, bf16[3,5120,256]{2,1,0:T(8,128)(2,1)} %get-tuple-element.123.w_ref), custom_call_target="tpu_custom_call" | custom-call | tf_op jit(solution)/shard_map/cond/branch_0_fun/gates/pallas_call | solution.py:387
  97.4 3.5 %all-to-all-start.3 = ((f32[16,2,256]{2,1,0:T(2,128)}), f32[16,2,256]{2,1,0:T(2,128)S(1)}, u32[]{:S(2)}, u32[]{:S(2)}) async-start(f32[16,2,256]{2,1,0:T(2,128)} %get-tuple-element.135), calls=%async_computation.3 | async-start | bytes 65536 | tf_op jit(solution)/shard_map/cond/branch_0_fun/all_to_all | solution.py:493
  100.9 7.1 %prior.7 = f32[8,256]{1,0:T(8,128)S(1)} custom-call(bf16[16,192,256]{2,1,0:T(8,128)(2,1)} %copy-done.2, bf16[4096,1024]{1,0:T(8,128)(2,1)} %get-tuple-element.126.w_ref, bf16[1024,1024]{1,0:T(8,128)(2,1)} %get-tuple-element.127.logit_ref, bf16[2,1024]{1,0:T(2,128)(2,1)S(1)} %copy-done.10, bf16[4,192,1024]{2,1,0:T(8,128)(2,1)} %get-tuple-element.129.hot_hbm, ...), custom_call_target="tpu_custom_call" | custom-call | tf_op jit(solution)/shard_map/cond/branch_0_fun/prior/pallas_call | solution.py:439
  108.1 2.2 renew.7
  110.2 27.5 %all_to_all.63.x_ref.x_hbm = bf16[16,192,256]{2,1,0:T(8,128)(2,1)S(1)} all-to-all(bf16[16,192,256]{2,1,0:T(8,128)(2,1)S(1)} %get-tuple-element.138), channel_id=1, replica_groups=mesh['task'=8,'mp'=16] {'mp'}, dimensions={0} | all-to-all | bytes 3145728 | tf_op jit(solution)/shard_map/cond/branch_0_fun/all_to_all | solution.py:493
  137.7 6.1 %gates.8 = (f32[192,768]{1,0:T(8,128)}, f32[16,2,256]{2,1,0:T(2,128)}) custom-call(bf16[4,192,1024]{2,1,0:T(8,128)(2,1)} %get-tuple-element.121.emb_hbm, bf16[16,192,256]{2,1,0:T(8,128)(2,1)S(1)} %all_to_all.63.x_ref.x_hbm, bf16[3,5120,256]{2,1,0:T(8,128)(2,1)} %get-tuple-element.123.w_ref), custom_call_target="tpu_custom_call" | custom-call | tf_op jit(solution)/shard_map/cond/branch_0_fun/gates/pallas_call | solution.py:387
  143.8 3.7 %all-to-all-start.5 = ((f32[16,2,256]{2,1,0:T(2,128)}), f32[16,2,256]{2,1,0:T(2,128)S(1)}, u32[]{:S(2)}, u32[]{:S(2)}) async-start(f32[16,2,256]{2,1,0:T(2,128)} %get-tuple-element.140), calls=%async_computation.5 | async-start | bytes 65536 | tf_op jit(solution)/shard_map/cond/branch_0_fun/all_to_all | solution.py:493
  147.5 7.1 %prior.8 = f32[8,256]{1,0:T(8,128)S(1)} custom-call(bf16[16,192,256]{2,1,0:T(8,128)(2,1)} %copy-done.3, bf16[4096,1024]{1,0:T(8,128)(2,1)} %get-tuple-element.126.w_ref, bf16[1024,1024]{1,0:T(8,128)(2,1)} %get-tuple-element.127.logit_ref, bf16[2,1024]{1,0:T(2,128)(2,1)S(1)} %copy-done.10, bf16[4,192,1024]{2,1,0:T(8,128)(2,1)} %get-tuple-element.129.hot_hbm, ...), custom_call_target="tpu_custom_call" | custom-call | tf_op jit(solution)/shard_map/cond/branch_0_fun/prior/pallas_call | solution.py:439
  154.6 2.2 renew.8
  156.8 25.1 %all_to_all.64.x_ref.x_hbm = bf16[16,192,256]{2,1,0:T(8,128)(2,1)S(1)} all-to-all(bf16[16,192,256]{2,1,0:T(8,128)(2,1)S(1)} %get-tuple-element.143), channel_id=1, replica_groups=mesh['task'=8,'mp'=16] {'mp'}, dimensions={0} | all-to-all | bytes 3145728 | tf_op jit(solution)/shard_map/cond/branch_0_fun/all_to_all | solution.py:493
  182.0 6.1 %gates.9 = (f32[192,768]{1,0:T(8,128)}, f32[16,2,256]{2,1,0:T(2,128)}) custom-call(bf16[4,192,1024]{2,1,0:T(8,128)(2,1)} %get-tuple-element.121.emb_hbm, bf16[16,192,256]{2,1,0:T(8,128)(2,1)S(1)} %all_to_all.64.x_ref.x_hbm, bf16[3,5120,256]{2,1,0:T(8,128)(2,1)} %get-tuple-element.123.w_ref), custom_call_target="tpu_custom_call" | custom-call | tf_op jit(solution)/shard_map/cond/branch_0_fun/gates/pallas_call | solution.py:387
  188.1 3.5 %all-to-all-start.7 = ((f32[16,2,256]{2,1,0:T(2,128)}), f32[16,2,256]{2,1,0:T(2,128)S(1)}, u32[]{:S(2)}, u32[]{:S(2)}) async-start(f32[16,2,256]{2,1,0:T(2,128)} %get-tuple-element.145), calls=%async_computation.7 | async-start | bytes 65536 | tf_op jit(solution)/shard_map/cond/branch_0_fun/all_to_all | solution.py:493
  191.6 7.1 %prior.9 = f32[8,256]{1,0:T(8,128)S(1)} custom-call(bf16[16,192,256]{2,1,0:T(8,128)(2,1)} %copy-done.1, bf16[4096,1024]{1,0:T(8,128)(2,1)} %get-tuple-element.126.w_ref, bf16[1024,1024]{1,0:T(8,128)(2,1)} %get-tuple-element.127.logit_ref, bf16[2,1024]{1,0:T(2,128)(2,1)S(1)} %copy-done.10, bf16[4,192,1024]{2,1,0:T(8,128)(2,1)} %get-tuple-element.129.hot_hbm, ...), custom_call_target="tpu_custom_call" | custom-call | tf_op jit(solution)/shard_map/cond/branch_0_fun/prior/pallas_call | solution.py:439
  198.8 2.2 renew.9
  201.2 1.1 broadcast_in_dim.123
  202.3 9.0 %all-to-all-start.8 = ((bf16[8,288,256]{2,1,0:T(8,128)(2,1)}), bf16[8,288,256]{2,1,0:T(8,128)(2,1)S(1)}, u32[]{:S(2)}, u32[]{:S(2)}) async-start(bf16[8,288,256]{2,1,0:T(8,128)(2,1)} %broadcast_in_dim.123), calls=%async_computation.8 | async-start | bytes 2359296 | tf_op jit(solution)/shard_map/cond/branch_0_fun/all_to_all | solution.py:493
  211.9 15.9 %all-to-all-done.8.got_ref = bf16[8,288,256]{2,1,0:T(8,128)(2,1)S(1)} async-done(((bf16[8,288,256]{2,1,0:T(8,128)(2,1)}), bf16[8,288,256]{2,1,0:T(8,128)(2,1)S(1)}, u32[]{:S(2)}, u32[]{:S(2)}) %all-to-all-start.8) | async-done | bytes 1179680 | tf_op jit(solution)/shard_map/cond/branch_0_fun/all_to_all | solution.py:493
  227.8 2.4 %settle.2 = (f32[4,256]{1,0:T(4,128)}, f32[4,256]{1,0:T(4,128)}, f32[4,256]{1,0:T(4,128)}, f32[256,256]{1,0:T(8,128)}) custom-call(s32[2,8]{1,0:T(2,128)S(1)} %pad_add_fusion.at_ref, bf16[8,288,256]{2,1,0:T(8,128)(2,1)S(1)} %all-to-all-done.8.got_ref, bf16[8,24,256]{2,1,0:T(8,128)(2,1)S(1)} %slice.43.outs_ref, s32[4,256]{1,0:T(4,128)S(1)} %broadcast_add_fusion.to_ref), custom_call_target="tpu_custom_call" | custom-call | tf_op jit(solution)/shard_map/cond/branch_0_fun/settle/pallas_call | solution.py:478
  (79 shorter events, 3.3 us)
Async XLA Ops:
  0.6 4.2 %collective-permute-start = (f32[256,256]{1,0:T(8,128)}, f32[256,256]{1,0:T(8,128)S(1)}, u32[]{:S(2)}, u32[]{:S(2)}) collective-permute-start(f32[256,256]{1,0:T(8,128)} %param.15), channel_id=1, source_target_pairs={{0,16},{16,0},{32,48},{48,32},{64,80},{80,64},{96,112},{112,96},{1... | collective-permute-start | bytes 786440 | tf_op jit(solution)/shard_map/ppermute | solution.py:606
  4.9 10.0 %copy-start.15 = (s32[4,4]{1,0:T(4,128)S(1)}, s32[4,4]{1,0:T(4,128)}, u32[]{:S(2)}) copy-start(s32[4,4]{1,0:T(4,128)} %get-tuple-element.342) | copy-start | bytes 196 | tf_op jit(solution)/shard_map/cond
  4.9 10.3 %copy-start.9 = (s32[4,32,256]{2,1,0:T(8,128)S(1)}, s32[4,32,256]{2,1,0:T(8,128)}, u32[]{:S(2)}) copy-start(s32[4,32,256]{2,1,0:T(8,128)} %get-tuple-element.115) | copy-start | bytes 393220 | tf_op jit(solution)/shard_map/cond
  4.9 10.3 %copy-start.14 = (s32[4,256]{1,0:T(4,128)S(1)}, s32[4,256]{1,0:T(4,128)}, u32[]{:S(2)}) copy-start(s32[4,256]{1,0:T(4,128)} %get-tuple-element.116) | copy-start | bytes 12292 | tf_op jit(solution)/shard_map/cond
  7.3 0.7 copy-start.4
  8.0 32.4 %all-to-all-start = ((bf16[16,192,256]{2,1,0:T(8,128)(2,1)}), bf16[16,192,256]{2,1,0:T(8,128)(2,1)S(1)}, u32[]{:S(2)}, u32[]{:S(2)}) async-start(bf16[16,192,256]{2,1,0:T(8,128)(2,1)} %get-tuple-element.113), calls=%async_computation | async-start | bytes 3145728 | tf_op jit(solution)/shard_map/cond/branch_0_fun/all_to_all | solution.py:493
  14.8 17.2 %copy-start.12 = (bf16[18,1024]{1,0:T(8,128)(2,1)S(1)}, bf16[18,1024]{1,0:T(8,128)(2,1)}, u32[]{:S(2)}) copy-start(bf16[18,1024]{1,0:T(8,128)(2,1)} %get-tuple-element.118.act_ref) | copy-start | bytes 110596 | tf_op jit(solution)/shard_map/cond
  32.0 8.2 %copy-start.16 = (s32[64]{0:T(128)S(1)}, s32[64]{0:T(128)}, u32[]{:S(2)}) copy-start(s32[64]{0:T(128)} %get-tuple-element.130) | copy-start | bytes 772 | tf_op jit(solution)/shard_map/cond
  40.4 6.1 %copy-start = (bf16[16,192,256]{2,1,0:T(8,128)(2,1)}, bf16[16,192,256]{2,1,0:T(8,128)(2,1)S(1)}, u32[]{:S(2)}) copy-start(bf16[16,192,256]{2,1,0:T(8,128)(2,1)S(1)} %all-to-all-done.x_ref.x_hbm) | copy-start | bytes 4718596 | tf_op jit(solution)/shard_map/cond
  40.4 13.3 %copy-start.10 = (bf16[2,1024]{1,0:T(2,128)(2,1)S(1)}, bf16[2,1024]{1,0:T(2,128)(2,1)}, u32[]{:S(2)}) copy-start(bf16[2,1024]{1,0:T(2,128)(2,1)} %get-tuple-element.128.head_ref) | copy-start | bytes 12292 | tf_op jit(solution)/shard_map/cond
  46.5 14.3 %all-to-all-start.1 = ((f32[16,2,256]{2,1,0:T(2,128)}), f32[16,2,256]{2,1,0:T(2,128)S(1)}, u32[]{:S(2)}, u32[]{:S(2)}) async-start(f32[16,2,256]{2,1,0:T(2,128)} %get-tuple-element.125), calls=%async_computation.1 | async-start | bytes 65536 | tf_op jit(solution)/shard_map/cond/branch_0_fun/all_to_all | solution.py:493
  91.3 6.1 %copy-start.2 = (bf16[16,192,256]{2,1,0:T(8,128)(2,1)}, bf16[16,192,256]{2,1,0:T(8,128)(2,1)S(1)}, u32[]{:S(2)}) copy-start(bf16[16,192,256]{2,1,0:T(8,128)(2,1)S(1)} %all_to_all.62.x_ref.x_hbm) | copy-start | bytes 4718596 | tf_op jit(solution)/shard_map/cond
  97.4 10.6 %all-to-all-start.3 = ((f32[16,2,256]{2,1,0:T(2,128)}), f32[16,2,256]{2,1,0:T(2,128)S(1)}, u32[]{:S(2)}, u32[]{:S(2)}) async-start(f32[16,2,256]{2,1,0:T(2,128)} %get-tuple-element.135), calls=%async_computation.3 | async-start | bytes 65536 | tf_op jit(solution)/shard_map/cond/branch_0_fun/all_to_all | solution.py:493
  137.7 6.1 %copy-start.3 = (bf16[16,192,256]{2,1,0:T(8,128)(2,1)}, bf16[16,192,256]{2,1,0:T(8,128)(2,1)S(1)}, u32[]{:S(2)}) copy-start(bf16[16,192,256]{2,1,0:T(8,128)(2,1)S(1)} %all_to_all.63.x_ref.x_hbm) | copy-start | bytes 4718596 | tf_op jit(solution)/shard_map/cond
  143.8 10.8 %all-to-all-start.5 = ((f32[16,2,256]{2,1,0:T(2,128)}), f32[16,2,256]{2,1,0:T(2,128)S(1)}, u32[]{:S(2)}, u32[]{:S(2)}) async-start(f32[16,2,256]{2,1,0:T(2,128)} %get-tuple-element.140), calls=%async_computation.5 | async-start | bytes 65536 | tf_op jit(solution)/shard_map/cond/branch_0_fun/all_to_all | solution.py:493
  182.0 6.1 %copy-start.1 = (bf16[16,192,256]{2,1,0:T(8,128)(2,1)}, bf16[16,192,256]{2,1,0:T(8,128)(2,1)S(1)}, u32[]{:S(2)}) copy-start(bf16[16,192,256]{2,1,0:T(8,128)(2,1)S(1)} %all_to_all.64.x_ref.x_hbm) | copy-start | bytes 4718596 | tf_op jit(solution)/shard_map/cond
  188.1 10.7 %all-to-all-start.7 = ((f32[16,2,256]{2,1,0:T(2,128)}), f32[16,2,256]{2,1,0:T(2,128)S(1)}, u32[]{:S(2)}, u32[]{:S(2)}) async-start(f32[16,2,256]{2,1,0:T(2,128)} %get-tuple-element.145), calls=%async_computation.7 | async-start | bytes 65536 | tf_op jit(solution)/shard_map/cond/branch_0_fun/all_to_all | solution.py:493
  202.3 25.5 %all-to-all-start.8 = ((bf16[8,288,256]{2,1,0:T(8,128)(2,1)}), bf16[8,288,256]{2,1,0:T(8,128)(2,1)S(1)}, u32[]{:S(2)}, u32[]{:S(2)}) async-start(bf16[8,288,256]{2,1,0:T(8,128)(2,1)} %broadcast_in_dim.123), calls=%async_computation.8 | async-start | bytes 2359296 | tf_op jit(solution)/shard_map/cond/branch_0_fun/all_to_all | solution.py:493

commit v2 on v1

--- a/solution.py
+++ b/solution.py
@@ -24,11 +24,11 @@
 
 
 def silu(v):
-    return v / (1.0 + jnp.exp(-v))
+    return v * sigmoid(v)
 
 
 def sigmoid(v):
-    return 1.0 / (1.0 + jnp.exp(-v))
+    return 0.5 + 0.5 * jnp.tanh(0.5 * v)
 
 
 def row_norm(pre):
@@ -60,16 +60,18 @@
 
 
 def embed_kernel(
-    at_ref, ev_hbm, stoch_hbm, act_ref, out_hbm, hot_hbm,
+    first, at_ref, ev_hbm, stoch_hbm, act_ref, out_hbm, hot_hbm,
     picks_ref, stoch_ref, hot_ref, out_ref, sem, done_sem,
 ):
     steps, rows, _ = hot_ref.shape
     count = rows // PIECE
 
     def fetch(step, k):
-        at = pl.ds(pl.multiple_of(at_ref[step, k], PIECE), PIECE)
+        at = pl.ds(pl.multiple_of(at_ref[first + step, k], PIECE), PIECE)
         to = pl.ds(k * PIECE, PIECE)
-        return pltpu.make_async_copy(ev_hbm.at[step, at], picks_ref.at[step, to], sem.at[step, k])
+        return pltpu.make_async_copy(
+            ev_hbm.at[first + step, at], picks_ref.at[step, to], sem.at[step, k]
+        )
 
     def give(step, q):
         ref, hbm = ((hot_ref, hot_hbm), (out_ref, out_hbm))[q]
@@ -128,7 +130,7 @@
     return jnp.transpose(jnp.broadcast_to(row, (128, row.shape[1])))[:rows]
 
 
-def gates_kernel(step, emb_hbm, x_ref, w_ref, g_hbm, stat_ref, g_ref, wbuf, emb_ref, sem):
+def gates_kernel(step, emb_hbm, x_hbm, w_ref, g_ref, stat_ref, x_ref, wbuf, emb_ref, sem):
     parts, depth, share = w_ref.shape
     chunks = depth // HID
 
@@ -137,10 +139,17 @@
         return pltpu.make_async_copy(w_ref.at[:, at, :], wbuf.at[c], sem.at[c])
 
     emb = pltpu.make_async_copy(emb_hbm.at[step], emb_ref, sem.at[chunks])
+    per = HID // share
+
+    def fetch_x(c):
+        at = pl.ds((c - 1) * per, per)
+        return pltpu.make_async_copy(x_hbm.at[at], x_ref.at[at], sem.at[chunks + c])
+
     emb.start()
-    for c in range(chunks):
+    fetch(0).start()
+    for c in range(1, chunks):
+        fetch_x(c).start()
         fetch(c).start()
-    per = HID // share
     emb.wait()
     fetch(0).wait()
     for k in range(parts):
@@ -149,6 +158,7 @@
         )
 
     def add(c, _):
+        fetch_x(c).wait()
         left = jnp.concatenate([x_ref[(c - 1) * per + q] for q in range(per)], axis=1)
         fetch(c).wait()
         for k in range(parts):
@@ -158,8 +168,6 @@
         return 0
 
     lax.fori_loop(1, chunks, add, 0)
-    out = pltpu.make_async_copy(g_ref, g_hbm, sem.at[chunks])
-    out.start()
     rows, width = g_ref.shape
     part = jnp.zeros((rows, 128), F32)
     part_sq = part
@@ -176,19 +184,9 @@
     )
     for q in range(stat_ref.shape[0]):
         stat_ref[q] = sums
-    out.wait()
-
-
-def update_kernel(
-    entries, step, g_hbm, stat_ref, carried_hbm, live_ref, new_hbm, low_ref,
-    g_ref, carried_ref, new_ref, sem,
-):
-    copies = [
-        pltpu.make_async_copy(g_hbm, g_ref, sem.at[0]),
-        pltpu.make_async_copy(carried_hbm, carried_ref, sem.at[1]),
-    ]
-    for copy in copies:
-        copy.start()
+
+
+def update_kernel(entries, step, g_ref, stat_ref, carried_ref, live_ref, new_ref, low_ref):
     sums = jnp.sum(stat_ref[...], axis=0) / entries
     avg = sums[0:1]
     inv = lax.rsqrt(sums[1:2] - avg * avg + 1e-5)
@@ -196,8 +194,6 @@
     avg_l = lanes_from_row(avg, rows)
     inv_l = lanes_from_row(inv, rows)
     live_l = lanes_from_row(live_ref[pl.ds(step, 1), :], rows)
-    for copy in copies:
-        copy.wait()
     for q in range(share // 128):
         def normed(part):
             at = part * share + q * 128
@@ -213,9 +209,6 @@
         low = renewed.astype(BF16)
         for k in range(low_ref.shape[0]):
             low_ref[k, :, q * 128 : (q + 1) * 128] = low
-    out = pltpu.make_async_copy(new_ref, new_hbm, sem.at[2])
-    out.start()
-    out.wait()
 
 
 def two_parts(values):
@@ -224,7 +217,7 @@
 
 
 def prior_kernel(
-    step, x_hbm, w_ref, logit_ref, head_ref, hot_hbm, live_ref, out_ref,
+    at_step, step, x_hbm, w_ref, logit_ref, head_ref, hot_hbm, live_ref, out_ref,
     x_ref, wbuf, lbuf, pre_ref, hid_ref, hot_ref, parts_ref, sem,
 ):
     shards, rows, share = x_ref.shape
@@ -241,7 +234,7 @@
         fetch(c).start()
     last = pltpu.make_async_copy(logit_ref, lbuf, sem.at[chunks])
     last.start()
-    marks = pltpu.make_async_copy(hot_hbm.at[step], hot_ref, sem.at[chunks + 1])
+    marks = pltpu.make_async_copy(hot_hbm.at[at_step], hot_ref, sem.at[chunks + 1])
     marks.start()
     pre_ref[...] = jnp.zeros(pre_ref.shape, F32)
     state.wait()
@@ -311,15 +304,22 @@
 
 
 def settle_kernel(
-    at_ref, got_ref, outs_ref, to_ref, log_ref, reward_ref, cont_ref, final_ref, buf, sem
+    rows, at_ref, got_ref, left_ref, outs_ref, to_ref, log_ref, reward_ref, cont_ref, final_ref, buf, sem
 ):
     count, per_task, share = buf.shape
-    copies = []
+    done = rows // per_task
     for i in range(count):
-        at = pl.ds(pl.multiple_of(at_ref[1, i] * per_task, per_task), per_task)
-        copy = pltpu.make_async_copy(got_ref.at[at_ref[0, i], at], buf.at[i], sem.at[i])
-        copy.start()
-        copies.append(copy)
+        chunk = at_ref[1, i]
+
+        def bring(ref, chunk, i=i):
+            at = pl.ds(pl.multiple_of(chunk * per_task, per_task), per_task)
+            pltpu.make_async_copy(ref.at[at_ref[0, i], at], buf.at[i], sem.at[i]).start()
+
+        if done == count:
+            bring(got_ref, chunk)
+        else:
+            pl.when(chunk < done)(functools.partial(bring, got_ref, chunk))
+            pl.when(chunk >= done)(functools.partial(bring, left_ref, chunk - done))
     parts = side_by_side(outs_ref)
     for t in range(STEPS):
         values = jnp.dot(
@@ -329,7 +329,7 @@
             at = t * 3 + k
             ref[t : t + 1] = values[at : at + 1] + values[12 + at : 13 + at]
     for i in range(count):
-        copies[i].wait()
+        pltpu.make_async_copy(got_ref.at[0, pl.ds(0, per_task)], buf.at[i], sem.at[i]).wait()
         final_ref[i * per_task : (i + 1) * per_task] = buf[i].astype(F32)
 
 
@@ -339,6 +339,7 @@
 
 WHOLE = pl.BlockSpec()
 STAY = pl.BlockSpec(memory_space=pltpu.HBM)
+EITHER = pl.BlockSpec(memory_space=pl.ANY)
 SCALARS = pl.BlockSpec(memory_space=pltpu.SMEM)
 
 
@@ -349,10 +350,10 @@
     )
 
 
-def embed(at, everyone, stoch, act, rows):
-    steps, _, depth = everyone.shape
+def embed(first, steps, at, everyone, stoch, act, rows):
+    depth = everyone.shape[2]
     return pl.pallas_call(
-        embed_kernel,
+        functools.partial(embed_kernel, first),
         in_specs=[SCALARS, STAY, STAY, WHOLE],
         out_specs=[STAY, STAY],
         out_shape=[pltpu.HBM((steps, rows, HID), BF16)] * 2,
@@ -369,34 +370,33 @@
     )(*placed([SCALARS, STAY, STAY, WHOLE], (at, everyone, stoch, act)))
 
 
-def stepped(kernel, moment, specs, operands):
+def stepped(kernel, steps, specs, operands):
     operands = placed(specs, operands)
-    if isinstance(moment, int):
-        return functools.partial(kernel, moment), specs, operands
-
-    def with_scalar(step_ref, *refs):
-        kernel(step_ref[0], *refs)
-
-    return with_scalar, [SCALARS, *specs], (jnp.full((1,), moment, I32), *operands)
-
-
-def gates(moment, emb, x, w):
-    kernel, specs, operands = stepped(gates_kernel, moment, [STAY, WHOLE, STAY], (emb, x, w))
+    if all(isinstance(step, int) for step in steps):
+        return functools.partial(kernel, *steps), specs, operands
+
+    def with_scalars(step_ref, *refs):
+        kernel(*(step_ref[k] for k in range(len(steps))), *refs)
+
+    return with_scalars, [SCALARS, *specs], (jnp.stack(steps), *operands)
+
+
+def gates(at, emb, x, w):
+    kernel, specs, operands = stepped(gates_kernel, (at,), [STAY, EITHER, STAY], (emb, x, w))
     shards, rows, share = x.shape
     parts, depth, _ = w.shape
     return pl.pallas_call(
         kernel,
         in_specs=specs,
         out_shape=[
-            pltpu.HBM((rows, parts * share), F32),
+            jax.ShapeDtypeStruct((rows, parts * share), F32),
             jax.ShapeDtypeStruct((shards, 2, 256), F32),
         ],
-        out_specs=[STAY, WHOLE],
         scratch_shapes=[
-            pltpu.VMEM((rows, parts * share), F32),
+            pltpu.VMEM(x.shape, BF16),
             pltpu.VMEM((depth // HID, parts, HID, share), BF16),
             pltpu.VMEM((rows, HID), BF16),
-            pltpu.SemaphoreType.DMA((depth // HID + 1,)),
+            pltpu.SemaphoreType.DMA((2 * (depth // HID),)),
         ],
         compiler_params=params(24),
         name="gates",
@@ -405,32 +405,25 @@
 
 def renew(moment, g, stats, carried, live, entries):
     kernel, specs, operands = stepped(
-        functools.partial(update_kernel, entries), moment, [STAY, WHOLE, STAY, WHOLE], (g, stats, carried, live)
+        functools.partial(update_kernel, entries), (moment,), [WHOLE] * 4, (g, stats, carried, live)
     )
     rows, share = carried.shape
     return pl.pallas_call(
         kernel,
         in_specs=specs,
         out_shape=[
-            pltpu.HBM((rows, share), F32),
+            jax.ShapeDtypeStruct((rows, share), F32),
             jax.ShapeDtypeStruct((stats.shape[0], rows, share), BF16),
-        ],
-        out_specs=[STAY, WHOLE],
-        scratch_shapes=[
-            pltpu.VMEM(g.shape, F32),
-            pltpu.VMEM((rows, share), F32),
-            pltpu.VMEM((rows, share), F32),
-            pltpu.SemaphoreType.DMA((3,)),
         ],
         compiler_params=params(16),
         name="renew",
     )(*operands)
 
 
-def prior(moment, x, w, logit, head, hot, live):
+def prior(at, moment, x, w, logit, head, hot, live):
     kernel, specs, operands = stepped(
         prior_kernel,
-        moment,
+        (at, moment),
         [STAY, STAY, STAY, WHOLE, STAY, WHOLE],
         (x, w, logit, head, hot, live),
     )
@@ -473,11 +466,11 @@
     )(at, own, other)
 
 
-def settle(at, got, outs, to, count, per_task):
+def settle(at, got, left, outs, to, rows, count, per_task):
     share = got.shape[2]
     return pl.pallas_call(
-        settle_kernel,
-        in_specs=[SCALARS, pl.BlockSpec(memory_space=pl.ANY), WHOLE, WHOLE],
+        functools.partial(settle_kernel, rows),
+        in_specs=[SCALARS, EITHER, EITHER, WHOLE, WHOLE],
         out_shape=[jax.ShapeDtypeStruct(to.shape, F32)] * 3
         + [jax.ShapeDtypeStruct((count * per_task, share), F32)],
         scratch_shapes=[
@@ -486,7 +479,7 @@
         ],
         compiler_params=params(16),
         name="settle",
-    )(at, got, outs, to)
+    )(at, got, left, outs, to)
 
 
 def exchange(copies, axis):
@@ -519,8 +512,11 @@
     sent = jnp.concatenate(
         [draws, actions[:, None], jnp.zeros((STEPS, DEPTH - GROUPS - 1, all_rows), I32)], axis=1
     ).astype(BF16)
-    everyone = jnp.transpose(lax.all_gather(sent, "task"), (1, 0, 3, 2))
-    everyone = everyone.reshape(STEPS, holders * all_rows, DEPTH)
+    sent = jnp.concatenate([sent.reshape(STEPS * DEPTH, all_rows), *rest], axis=0)
+    everyone = lax.all_gather(sent, "task")
+    left = everyone[:, STEPS * DEPTH :]
+    everyone = everyone[:, : STEPS * DEPTH].reshape(holders, STEPS, DEPTH, all_rows)
+    everyone = jnp.transpose(everyone, (1, 0, 3, 2)).reshape(STEPS, holders * all_rows, DEPTH)
 
     task = place // 2 * pair + local
     horizon = jnp.sum(
@@ -537,7 +533,8 @@
     )
     slot = (task[None, :] // per_core + ahead_by) % holders
     source = slot * all_rows + (task % per_core)[None, :] * per_task
-    emb, hot = embed(source, everyone, stoch, act, rows)
+    first = STEPS if count in ROLLED else 1
+    emb, hot = embed(0, first, source, everyone, stoch, act, rows)
     x, emb, hot = lax.optimization_barrier((x, emb, hot))
 
     held = jnp.repeat((place - running) % holders, in_block, axis=1) * per_core
@@ -551,36 +548,53 @@
     to = jnp.where(chunk < count, core * 256 + chunk * per_task, -TASKS * 256)
     to = jnp.repeat(to, per_task, axis=1) + jnp.arange(all_rows, dtype=I32)[None, :] % per_task
 
-    def one_step(moment, x, carried):
-        g, stats = gates(moment, emb, x, w)
+    def likely(at, moment, x, hot):
+        return prior(at, moment, x, prior_weight, logit, head, hot, living)[:3]
+
+    def gated(at, moment, x, emb, carried):
+        g, stats = gates(at, emb, x, w)
         stats = exchange(stats, "mp")
-        small = prior(moment, x, prior_weight, logit, head, hot, living)
-        stats, small = lax.optimization_barrier((stats, small))
-        carried, low = renew(moment, g, stats, carried, living, entries)
-        return low, carried, small[:3]
+        return renew(moment, g, stats, carried, living, entries)
 
     small = []
     if count in ROLLED:
 
         def body(state, moment):
-            low, carried, out = one_step(moment, *state)
-            return (exchange(low, "mp"), carried), out
+            x, carried = state
+            carried, low = gated(moment, moment, x, emb, carried)
+            out = likely(moment, moment, x, hot)
+            x, out = lax.optimization_barrier((exchange(low, "mp"), out))
+            return (x, carried), out
 
         (x, carried), outs = lax.scan(body, (x, carried), jnp.arange(STEPS - 1, dtype=I32))
         small.append(outs.reshape(-1, outs.shape[2]))
+        at = STEPS - 1
     else:
+        at = 0
         for moment in range(STEPS - 1):
-            low, carried, out = one_step(moment, x, carried)
+            carried, low = gated(at, moment, x, emb, carried)
+            out = likely(at, moment, x, hot)
+            if moment == 0:
+                emb, hot = embed(1, STEPS - 1, source, everyone, stoch, act, rows)
+            x = exchange(low, "mp")
+            x, out, emb, hot = lax.optimization_barrier((x, out, emb, hot))
             small.append(out)
-            x = exchange(low, "mp")
-    low, _, out = one_step(STEPS - 1, x, carried)
+            at = moment
+
+    g, stats = gates(at, emb, x, w)
+    stats = exchange(stats, "mp")
+    out = likely(at, STEPS - 1, x, hot)
+    stats, small, out = lax.optimization_barrier((stats, small, out))
+    _, low = renew(STEPS - 1, g, stats, carried, living, entries)
 
     outs = jnp.concatenate([*small, out], axis=0)
     high, low_part = two_parts(outs)
-    sent = jnp.concatenate([low[0], *rest, high, low_part, jnp.zeros((8, share), BF16)], axis=0)
+    sent = jnp.concatenate([low[0], high, low_part, jnp.zeros((8, share), BF16)], axis=0)
     got = exchange(jnp.broadcast_to(sent[None], (holders, *sent.shape)), "task")
-    outs = got[:, all_rows : all_rows + 24]
-    return settle(settle_at, got, outs, to, per_core, per_task)
+    outs = got[:, rows : rows + 24]
+    if not rest:
+        left = got
+    return settle(settle_at, got, left, outs, to, rows, per_core, per_task)
 
 
 def on_device(

time: 231 us -> 212 us (0.918)
  blocking collectives: 95.6 us -> 39.4 us
  waiting for transfers between devices: 15.9 us -> 55 us
  Pallas kernels: 74.4 us -> 70.8 us
    all_to_all x3 -> x2, blocking collectives: 80.9 us -> 24.4 us  [exchange(): return lax.all_to_all(copies, axis, 0, 0, tiled=True)]
    all_to_all x6 -> x7, waiting for transfers between devices: 15.9 us -> 55 us  [exchange(): return lax.all_to_all(copies, axis, 0, 0, tiled=True)]
    pallas_call x10 -> x11, Pallas kernels: 43.7 us -> 40.4 us  [the longest x4 20.7 us: gates(): pl.pallas_call(kernel, in_specs=specs, out_shape=[jax.ShapeDtypeStruct((r...]
    all_to_all x6 -> x7, starting transfers between devices: 33.5 us -> 33.6 us  [exchange(): return lax.all_to_all(copies, axis, 0, 0, tiled=True)]
  transfers between devices with their start and end apart: 7 -> 8, of which waited for: 1 -> 6; matrix products, arithmetic and copies ran while one was open for 2% -> 3% of each run, Pallas kernels for 16% -> 18%
where the time goes in v2:
time: 212 us; the launch traced here: 211 us
  Pallas kernels  70.8 us (33%)
  waiting for transfers between devices  55 us (26%)
  blocking collectives  39.4 us (19%)
  starting transfers between devices  35.1 us (17%)
  local copies, waits for them, and re-layouts  6.43 us (3%)
  other arithmetic  2.36 us (1%)
    all_to_all x7, waiting for transfers between devices, exchange(): return lax.all_to_all(copies, axis, 0, 0, tiled=True)  55 us
    all_to_all x7, starting transfers between devices, exchange(): return lax.all_to_all(copies, axis, 0, 0, tiled=True)  33.6 us
    pallas_call x4, Pallas kernels, prior(): pl.pallas_call(kernel, in_specs=specs, out_shape=jax.ShapeDtypeStruct((8,...  28.1 us
    all_to_all x2, blocking collectives, exchange(): return lax.all_to_all(copies, axis, 0, 0, tiled=True)  24.4 us
    pallas_call x4, Pallas kernels, gates(): pl.pallas_call(kernel, in_specs=specs, out_shape=[jax.ShapeDtypeStruct((r...  20.7 us
    all_gather x1, blocking collectives, window(): everyone = lax.all_gather(sent, 'task')  14.9 us
    pallas_call x2, Pallas kernels, embed(): pl.pallas_call(functools.partial(embed_kernel, first), in_specs=[SCALARS,...  10.8 us
    pallas_call x4, Pallas kernels, renew(): pl.pallas_call(kernel, in_specs=specs, out_shape=[jax.ShapeDtypeStruct((r...  6.45 us
  transfers between devices with their start and end apart: 8, of which 6 were waited for; matrix products, arithmetic and copies ran while one was open for 3% of the time, Pallas kernels for 18%

profile of v2, /device:TPU:1, one launch (start us, length us, event | category | flops | bytes accessed | tf_op | source)
XLA Modules:
  0.0 211.3 jit_solution(9544623903158826604)
XLA Ops:
  4.9 206.3 %conditional.1 = ((f32[4,256]{1,0:T(4,128)}, f32[4,256]{1,0:T(4,128)}, f32[4,256]{1,0:T(4,128)}, f32[256,256]{1,0:T(8,128)})) conditional(s32[]{:T(128)} %clamp.3, (s32[4,4]{1,0:T(4,128)}, s32[4,16]{1,0:T(4,128)S(1)}, f32[256,256]{1,0:T(8,128)}, f32[256,256]{1,0:T(8,128)S(1)}, s32[8]{0:T(128)S(1)}, /*index=5*/s32[8]{0:T(128)S(1)}, ...), branch_computations={%region_5.10_spmd, %region_10.17_spmd} | conditional | flops 1026871 | bytes 58013452 | solution.py:647
  4.9 2.3 %pick.2 = (f32[192,256]{1,0:T(8,128)S(1)}, bf16[16,192,256]{2,1,0:T(8,128)(2,1)}, bf16[64,256]{1,0:T(8,128)(2,1)S(1)}) custom-call(s32[8]{0:T(128)S(1)} %get-tuple-element.110.at_ref, f32[8,32,256]{2,1,0:T(8,128)} %bitcast.40, f32[8,32,256]{2,1,0:T(8,128)S(1)} %bitcast.42), custom_call_target="tpu_custom_call" | custom-call | tf_op jit(solution)/shard_map/cond/branch_0_fun/pick/pallas_call | solution.py:460
  7.2 6.8 %all-to-all-start = ((bf16[16,192,256]{2,1,0:T(8,128)(2,1)}), bf16[16,192,256]{2,1,0:T(8,128)(2,1)S(1)}, u32[]{:S(2)}, u32[]{:S(2)}) async-start(bf16[16,192,256]{2,1,0:T(8,128)(2,1)} %get-tuple-element.113), calls=%async_computation | async-start | bytes 3145728 | tf_op jit(solution)/shard_map/cond/branch_0_fun/all_to_all | solution.py:486
  14.7 14.9 %all-gather = bf16[1792,256]{1,0:T(8,128)(2,1)S(1)} all-gather(bf16[224,256]{1,0:T(8,128)(2,1)S(1)} %pad_maximum_fusion), channel_id=2, replica_groups=mesh['task'=8,'mp'=16] {'task'}, dimensions={0}, use_global_device_ids=true | all-gather | bytes 1032192 | tf_op jit(solution)/shard_map/cond/branch_0_fun/all_gather | solution.py:516
  30.7 1.8 copy.55
  32.6 4.0 %embed.3 = (bf16[1,192,1024]{2,1,0:T(8,128)(2,1)}, bf16[1,192,1024]{2,1,0:T(8,128)(2,1)}) custom-call(s32[4,8]{1,0:T(4,128)S(1)} %fusion.11.at_ref, bf16[4,2048,40]{2,1,0:T(8,128)(2,1)} %bitcast.33, bf16[1024,1024]{1,0:T(8,128)(2,1)} %get-tuple-element.118.stoch_hbm, bf16[18,1024]{1,0:T(8,128)(2,1)S(1)} %copy-done.8), custom_call_target="tpu_custom_call" | custom-call | tf_op jit(solution)/shard_map/cond/branch_0_fun/embed/pallas_call | solution.py:355
  36.9 2.6 %all-to-all-done.x_hbm = bf16[16,192,256]{2,1,0:T(8,128)(2,1)S(1)} async-done(((bf16[16,192,256]{2,1,0:T(8,128)(2,1)}), bf16[16,192,256]{2,1,0:T(8,128)(2,1)S(1)}, u32[]{:S(2)}, u32[]{:S(2)}) %all-to-all-start) | async-done | bytes 1572896 | tf_op jit(solution)/shard_map/cond/branch_0_fun/all_to_all | solution.py:486
  39.5 5.5 %gates.6 = (f32[192,768]{1,0:T(8,128)S(1)}, f32[16,2,256]{2,1,0:T(2,128)}) custom-call(bf16[1,192,1024]{2,1,0:T(8,128)(2,1)} %get-tuple-element.122.emb_hbm, bf16[16,192,256]{2,1,0:T(8,128)(2,1)S(1)} %all-to-all-done.x_hbm, bf16[3,5120,256]{2,1,0:T(8,128)(2,1)} %get-tuple-element.124.w_ref), custom_call_target="tpu_custom_call" | custom-call | tf_op jit(solution)/shard_map/cond/branch_0_fun/gates/pallas_call | solution.py:388
  45.0 4.4 %all-to-all-start.1 = ((f32[16,2,256]{2,1,0:T(2,128)}), f32[16,2,256]{2,1,0:T(2,128)S(1)}, u32[]{:S(2)}, u32[]{:S(2)}) async-start(f32[16,2,256]{2,1,0:T(2,128)} %get-tuple-element.126), calls=%async_computation.1 | async-start | bytes 65536 | tf_op jit(solution)/shard_map/cond/branch_0_fun/all_to_all | solution.py:486
  49.6 6.2 %all-to-all-done.1.stat_ref = f32[16,2,256]{2,1,0:T(2,128)S(1)} async-done(((f32[16,2,256]{2,1,0:T(2,128)}), f32[16,2,256]{2,1,0:T(2,128)S(1)}, u32[]{:S(2)}, u32[]{:S(2)}) %all-to-all-start.1) | async-done | bytes 32800 | tf_op jit(solution)/shard_map/cond/branch_0_fun/all_to_all | solution.py:486
  57.5 3.7 %all-to-all-start.2 = ((bf16[16,192,256]{2,1,0:T(8,128)(2,1)}), bf16[16,192,256]{2,1,0:T(8,128)(2,1)S(1)}, u32[]{:S(2)}, u32[]{:S(2)}) async-start(bf16[16,192,256]{2,1,0:T(8,128)(2,1)} %get-tuple-element.129), calls=%async_computation.2 | async-start | bytes 3145728 | tf_op jit(solution)/shard_map/cond/branch_0_fun/all_to_all | solution.py:486
  61.3 6.8 %embed.4 = (bf16[3,192,1024]{2,1,0:T(8,128)(2,1)}, bf16[3,192,1024]{2,1,0:T(8,128)(2,1)}) custom-call(s32[4,8]{1,0:T(4,128)S(1)} %fusion.11.at_ref, bf16[4,2048,40]{2,1,0:T(8,128)(2,1)} %bitcast.34, bf16[1024,1024]{1,0:T(8,128)(2,1)} %get-tuple-element.118.stoch_hbm, bf16[18,1024]{1,0:T(8,128)(2,1)S(1)} %copy-done.8), custom_call_target="tpu_custom_call" | custom-call | tf_op jit(solution)/shard_map/cond/branch_0_fun/embed/pallas_call | solution.py:355
  68.0 7.0 %prior.6 = f32[8,256]{1,0:T(8,128)S(1)} custom-call(bf16[16,192,256]{2,1,0:T(8,128)(2,1)} %copy-done, bf16[4096,1024]{1,0:T(8,128)(2,1)} %get-tuple-element.130.w_ref, bf16[1024,1024]{1,0:T(8,128)(2,1)} %get-tuple-element.131.logit_ref, bf16[2,1024]{1,0:T(2,128)(2,1)S(1)} %copy-done.10, bf16[1,192,1024]{2,1,0:T(8,128)(2,1)} %get-tuple-element.133.hot_hbm, ...), custom_call_target="tpu_custom_call" | custom-call | tf_op jit(solution)/shard_map/cond/branch_0_fun/prior/pallas_call | solution.py:432
  75.1 7.1 %all-to-all-done.2.x_hbm = bf16[16,192,256]{2,1,0:T(8,128)(2,1)S(1)} async-done(((bf16[16,192,256]{2,1,0:T(8,128)(2,1)}), bf16[16,192,256]{2,1,0:T(8,128)(2,1)S(1)}, u32[]{:S(2)}, u32[]{:S(2)}) %all-to-all-start.2) | async-done | bytes 1572896 | tf_op jit(solution)/shard_map/cond/branch_0_fun/all_to_all | solution.py:486
  82.2 4.9 %gates.7 = (f32[192,768]{1,0:T(8,128)S(1)}, f32[16,2,256]{2,1,0:T(2,128)S(1)}) custom-call(bf16[3,192,1024]{2,1,0:T(8,128)(2,1)} %get-tuple-element.150.emb_hbm, bf16[16,192,256]{2,1,0:T(8,128)(2,1)S(1)} %all-to-all-done.2.x_hbm, bf16[3,5120,256]{2,1,0:T(8,128)(2,1)} %get-tuple-element.124.w_ref), custom_call_target="tpu_custom_call" | custom-call | tf_op jit(solution)/shard_map/cond/branch_0_fun/gates/pallas_call | solution.py:388
  87.1 12.5 %all_to_all.62.stat_ref = f32[16,2,256]{2,1,0:T(2,128)S(1)} all-to-all(f32[16,2,256]{2,1,0:T(2,128)S(1)} %get-tuple-element.139), channel_id=1, replica_groups=mesh['task'=8,'mp'=16] {'mp'}, dimensions={0} | all-to-all | bytes 65536 | tf_op jit(solution)/shard_map/cond/branch_0_fun/all_to_all | solution.py:486
  99.6 1.7 renew.7
  101.3 3.7 %all-to-all-start.4 = ((bf16[16,192,256]{2,1,0:T(8,128)(2,1)}), bf16[16,192,256]{2,1,0:T(8,128)(2,1)S(1)}, u32[]{:S(2)}, u32[]{:S(2)}) async-start(bf16[16,192,256]{2,1,0:T(8,128)(2,1)} %get-tuple-element.141), calls=%async_computation.4 | async-start | bytes 3145728 | tf_op jit(solution)/shard_map/cond/branch_0_fun/all_to_all | solution.py:486
  105.0 7.0 %prior.7 = f32[8,256]{1,0:T(8,128)S(1)} custom-call(bf16[16,192,256]{2,1,0:T(8,128)(2,1)} %copy-done.1, bf16[4096,1024]{1,0:T(8,128)(2,1)} %get-tuple-element.130.w_ref, bf16[1024,1024]{1,0:T(8,128)(2,1)} %get-tuple-element.131.logit_ref, bf16[2,1024]{1,0:T(2,128)(2,1)S(1)} %copy-done.10, bf16[3,192,1024]{2,1,0:T(8,128)(2,1)} %get-tuple-element.157.hot_hbm, ...), custom_call_target="tpu_custom_call" | custom-call | tf_op jit(solution)/shard_map/cond/branch_0_fun/prior/pallas_call | solution.py:432
  112.1 13.5 %all-to-all-done.4.x_hbm = bf16[16,192,256]{2,1,0:T(8,128)(2,1)S(1)} async-done(((bf16[16,192,256]{2,1,0:T(8,128)(2,1)}), bf16[16,192,256]{2,1,0:T(8,128)(2,1)S(1)}, u32[]{:S(2)}, u32[]{:S(2)}) %all-to-all-start.4) | async-done | bytes 1572896 | tf_op jit(solution)/shard_map/cond/branch_0_fun/all_to_all | solution.py:486
  125.6 4.8 %gates.8 = (f32[192,768]{1,0:T(8,128)S(1)}, f32[16,2,256]{2,1,0:T(2,128)S(1)}) custom-call(bf16[3,192,1024]{2,1,0:T(8,128)(2,1)} %get-tuple-element.150.emb_hbm, bf16[16,192,256]{2,1,0:T(8,128)(2,1)S(1)} %all-to-all-done.4.x_hbm, bf16[3,5120,256]{2,1,0:T(8,128)(2,1)} %get-tuple-element.124.w_ref), custom_call_target="tpu_custom_call" | custom-call | tf_op jit(solution)/shard_map/cond/branch_0_fun/gates/pallas_call | solution.py:388
  130.5 11.9 %all_to_all.63.stat_ref = f32[16,2,256]{2,1,0:T(2,128)S(1)} all-to-all(f32[16,2,256]{2,1,0:T(2,128)S(1)} %get-tuple-element.146), channel_id=1, replica_groups=mesh['task'=8,'mp'=16] {'mp'}, dimensions={0} | all-to-all | bytes 65536 | tf_op jit(solution)/shard_map/cond/branch_0_fun/all_to_all | solution.py:486
  142.4 1.7 renew.8
  144.2 3.7 %all-to-all-start.6 = ((bf16[16,192,256]{2,1,0:T(8,128)(2,1)}), bf16[16,192,256]{2,1,0:T(8,128)(2,1)S(1)}, u32[]{:S(2)}, u32[]{:S(2)}) async-start(bf16[16,192,256]{2,1,0:T(8,128)(2,1)} %get-tuple-element.148), calls=%async_computation.6 | async-start | bytes 3145728 | tf_op jit(solution)/shard_map/cond/branch_0_fun/all_to_all | solution.py:486
  147.9 7.0 %prior.8 = f32[8,256]{1,0:T(8,128)S(1)} custom-call(bf16[16,192,256]{2,1,0:T(8,128)(2,1)} %copy-done.3, bf16[4096,1024]{1,0:T(8,128)(2,1)} %get-tuple-element.130.w_ref, bf16[1024,1024]{1,0:T(8,128)(2,1)} %get-tuple-element.131.logit_ref, bf16[2,1024]{1,0:T(2,128)(2,1)S(1)} %copy-done.10, bf16[3,192,1024]{2,1,0:T(8,128)(2,1)} %get-tuple-element.157.hot_hbm, ...), custom_call_target="tpu_custom_call" | custom-call | tf_op jit(solution)/shard_map/cond/branch_0_fun/prior/pallas_call | solution.py:432
  154.9 13.4 %all-to-all-done.6.x_hbm = bf16[16,192,256]{2,1,0:T(8,128)(2,1)S(1)} async-done(((bf16[16,192,256]{2,1,0:T(8,128)(2,1)}), bf16[16,192,256]{2,1,0:T(8,128)(2,1)S(1)}, u32[]{:S(2)}, u32[]{:S(2)}) %all-to-all-start.6) | async-done | bytes 1572896 | tf_op jit(solution)/shard_map/cond/branch_0_fun/all_to_all | solution.py:486
  168.3 5.5 %gates.9 = (f32[192,768]{1,0:T(8,128)S(1)}, f32[16,2,256]{2,1,0:T(2,128)}) custom-call(bf16[3,192,1024]{2,1,0:T(8,128)(2,1)} %get-tuple-element.150.emb_hbm, bf16[16,192,256]{2,1,0:T(8,128)(2,1)S(1)} %all-to-all-done.6.x_hbm, bf16[3,5120,256]{2,1,0:T(8,128)(2,1)} %get-tuple-element.124.w_ref), custom_call_target="tpu_custom_call" | custom-call | tf_op jit(solution)/shard_map/cond/branch_0_fun/gates/pallas_call | solution.py:388
  173.8 5.5 %all-to-all-start.7 = ((f32[16,2,256]{2,1,0:T(2,128)}), f32[16,2,256]{2,1,0:T(2,128)S(1)}, u32[]{:S(2)}, u32[]{:S(2)}) async-start(f32[16,2,256]{2,1,0:T(2,128)} %get-tuple-element.153), calls=%async_computation.7 | async-start | bytes 65536 | tf_op jit(solution)/shard_map/cond/branch_0_fun/all_to_all | solution.py:486
  179.4 7.0 %prior.9 = f32[8,256]{1,0:T(8,128)S(1)} custom-call(bf16[16,192,256]{2,1,0:T(8,128)(2,1)} %copy-done.2, bf16[4096,1024]{1,0:T(8,128)(2,1)} %get-tuple-element.130.w_ref, bf16[1024,1024]{1,0:T(8,128)(2,1)} %get-tuple-element.131.logit_ref, bf16[2,1024]{1,0:T(2,128)(2,1)S(1)} %copy-done.10, bf16[3,192,1024]{2,1,0:T(8,128)(2,1)} %get-tuple-element.157.hot_hbm, ...), custom_call_target="tpu_custom_call" | custom-call | tf_op jit(solution)/shard_map/cond/branch_0_fun/prior/pallas_call | solution.py:432
  188.8 5.8 %all-to-all-start.8 = ((bf16[8,224,256]{2,1,0:T(8,128)(2,1)}), bf16[8,224,256]{2,1,0:T(8,128)(2,1)S(1)}, u32[]{:S(2)}, u32[]{:S(2)}) async-start(bf16[8,224,256]{2,1,0:T(8,128)(2,1)} %broadcast_in_dim.153), calls=%async_computation.8 | async-start | bytes 1835008 | tf_op jit(solution)/shard_map/cond/branch_0_fun/all_to_all | solution.py:486
  196.2 12.2 %all-to-all-done.8.got_ref = bf16[8,224,256]{2,1,0:T(8,128)(2,1)S(1)} async-done(((bf16[8,224,256]{2,1,0:T(8,128)(2,1)}), bf16[8,224,256]{2,1,0:T(8,128)(2,1)S(1)}, u32[]{:S(2)}, u32[]{:S(2)}) %all-to-all-start.8) | async-done | bytes 917536 | tf_op jit(solution)/shard_map/cond/branch_0_fun/all_to_all | solution.py:486
  208.4 2.5 %settle.2 = (f32[4,256]{1,0:T(4,128)}, f32[4,256]{1,0:T(4,128)}, f32[4,256]{1,0:T(4,128)}, f32[256,256]{1,0:T(8,128)}) custom-call(s32[2,8]{1,0:T(2,128)S(1)} %pad_add_fusion.at_ref, bf16[8,224,256]{2,1,0:T(8,128)(2,1)S(1)} %all-to-all-done.8.got_ref, bf16[8,64,256]{2,1,0:T(8,128)(2,1)S(1)} %slice.54.left_ref, bf16[8,24,256]{2,1,0:T(8,128)(2,1)S(1)} %slice.55.outs_ref, ...), custom_call_target="tpu_custom_call" | custom-call | tf_op jit(solution)/shard_map/cond/branch_0_fun/settle/pallas_call | solution.py:471
  (85 shorter events, 11.5 us)
Async XLA Ops:
  0.6 4.2 %collective-permute-start = (f32[256,256]{1,0:T(8,128)}, f32[256,256]{1,0:T(8,128)S(1)}, u32[]{:S(2)}, u32[]{:S(2)}) collective-permute-start(f32[256,256]{1,0:T(8,128)} %param.15), channel_id=1, source_target_pairs={{0,16},{16,0},{32,48},{48,32},{64,80},{80,64},{96,112},{112,96},{1... | collective-permute-start | bytes 786440 | tf_op jit(solution)/shard_map/ppermute | solution.py:620
  4.9 9.2 %copy-start.12 = (s32[4,256]{1,0:T(4,128)S(1)}, s32[4,256]{1,0:T(4,128)}, u32[]{:S(2)}) copy-start(s32[4,256]{1,0:T(4,128)} %get-tuple-element.116) | copy-start | bytes 12292 | tf_op jit(solution)/shard_map/cond
  4.9 9.2 %copy-start.13 = (s32[4,4]{1,0:T(4,128)S(1)}, s32[4,4]{1,0:T(4,128)}, u32[]{:S(2)}) copy-start(s32[4,4]{1,0:T(4,128)} %get-tuple-element.354) | copy-start | bytes 196 | tf_op jit(solution)/shard_map/cond
  4.9 9.6 %copy-start.7 = (s32[4,32,256]{2,1,0:T(8,128)S(1)}, s32[4,32,256]{2,1,0:T(8,128)}, u32[]{:S(2)}) copy-start(s32[4,32,256]{2,1,0:T(8,128)} %get-tuple-element.115) | copy-start | bytes 393220 | tf_op jit(solution)/shard_map/cond
  7.2 32.2 %all-to-all-start = ((bf16[16,192,256]{2,1,0:T(8,128)(2,1)}), bf16[16,192,256]{2,1,0:T(8,128)(2,1)S(1)}, u32[]{:S(2)}, u32[]{:S(2)}) async-start(bf16[16,192,256]{2,1,0:T(8,128)(2,1)} %get-tuple-element.113), calls=%async_computation | async-start | bytes 3145728 | tf_op jit(solution)/shard_map/cond/branch_0_fun/all_to_all | solution.py:486
  29.7 1.0 copy-start.6
  29.7 3.0 %copy-start.8 = (bf16[18,1024]{1,0:T(8,128)(2,1)S(1)}, bf16[18,1024]{1,0:T(8,128)(2,1)}, u32[]{:S(2)}) copy-start(bf16[18,1024]{1,0:T(8,128)(2,1)} %get-tuple-element.119.act_ref) | copy-start | bytes 110596 | tf_op jit(solution)/shard_map/cond
  32.6 4.1 %copy-start.14 = (s32[64]{0:T(128)S(1)}, s32[64]{0:T(128)}, u32[]{:S(2)}) copy-start(s32[64]{0:T(128)} %get-tuple-element.128) | copy-start | bytes 772 | tf_op jit(solution)/shard_map/cond
  39.5 5.5 %copy-start = (bf16[16,192,256]{2,1,0:T(8,128)(2,1)}, bf16[16,192,256]{2,1,0:T(8,128)(2,1)S(1)}, u32[]{:S(2)}) copy-start(bf16[16,192,256]{2,1,0:T(8,128)(2,1)S(1)} %all-to-all-done.x_hbm) | copy-start | bytes 4718596 | tf_op jit(solution)/shard_map/cond
  45.0 10.8 %all-to-all-start.1 = ((f32[16,2,256]{2,1,0:T(2,128)}), f32[16,2,256]{2,1,0:T(2,128)S(1)}, u32[]{:S(2)}, u32[]{:S(2)}) async-start(f32[16,2,256]{2,1,0:T(2,128)} %get-tuple-element.126), calls=%async_computation.1 | async-start | bytes 65536 | tf_op jit(solution)/shard_map/cond/branch_0_fun/all_to_all | solution.py:486
  57.5 24.6 %all-to-all-start.2 = ((bf16[16,192,256]{2,1,0:T(8,128)(2,1)}), bf16[16,192,256]{2,1,0:T(8,128)(2,1)S(1)}, u32[]{:S(2)}, u32[]{:S(2)}) async-start(bf16[16,192,256]{2,1,0:T(8,128)(2,1)} %get-tuple-element.129), calls=%async_computation.2 | async-start | bytes 3145728 | tf_op jit(solution)/shard_map/cond/branch_0_fun/all_to_all | solution.py:486
  61.2 6.8 %copy-start.10 = (bf16[2,1024]{1,0:T(2,128)(2,1)S(1)}, bf16[2,1024]{1,0:T(2,128)(2,1)}, u32[]{:S(2)}) copy-start(bf16[2,1024]{1,0:T(2,128)(2,1)} %get-tuple-element.132.head_ref) | copy-start | bytes 12292 | tf_op jit(solution)/shard_map/cond
  82.2 4.9 %copy-start.1 = (bf16[16,192,256]{2,1,0:T(8,128)(2,1)}, bf16[16,192,256]{2,1,0:T(8,128)(2,1)S(1)}, u32[]{:S(2)}) copy-start(bf16[16,192,256]{2,1,0:T(8,128)(2,1)S(1)} %all-to-all-done.2.x_hbm) | copy-start | bytes 4718596 | tf_op jit(solution)/shard_map/cond
  101.3 24.3 %all-to-all-start.4 = ((bf16[16,192,256]{2,1,0:T(8,128)(2,1)}), bf16[16,192,256]{2,1,0:T(8,128)(2,1)S(1)}, u32[]{:S(2)}, u32[]{:S(2)}) async-start(bf16[16,192,256]{2,1,0:T(8,128)(2,1)} %get-tuple-element.141), calls=%async_computation.4 | async-start | bytes 3145728 | tf_op jit(solution)/shard_map/cond/branch_0_fun/all_to_all | solution.py:486
  125.6 4.9 %copy-start.3 = (bf16[16,192,256]{2,1,0:T(8,128)(2,1)}, bf16[16,192,256]{2,1,0:T(8,128)(2,1)S(1)}, u32[]{:S(2)}) copy-start(bf16[16,192,256]{2,1,0:T(8,128)(2,1)S(1)} %all-to-all-done.4.x_hbm) | copy-start | bytes 4718596 | tf_op jit(solution)/shard_map/cond
  144.2 24.1 %all-to-all-start.6 = ((bf16[16,192,256]{2,1,0:T(8,128)(2,1)}), bf16[16,192,256]{2,1,0:T(8,128)(2,1)S(1)}, u32[]{:S(2)}, u32[]{:S(2)}) async-start(bf16[16,192,256]{2,1,0:T(8,128)(2,1)} %get-tuple-element.148), calls=%async_computation.6 | async-start | bytes 3145728 | tf_op jit(solution)/shard_map/cond/branch_0_fun/all_to_all | solution.py:486
  168.3 5.5 %copy-start.2 = (bf16[16,192,256]{2,1,0:T(8,128)(2,1)}, bf16[16,192,256]{2,1,0:T(8,128)(2,1)S(1)}, u32[]{:S(2)}) copy-start(bf16[16,192,256]{2,1,0:T(8,128)(2,1)S(1)} %all-to-all-done.6.x_hbm) | copy-start | bytes 4718596 | tf_op jit(solution)/shard_map/cond
  173.8 12.7 %all-to-all-start.7 = ((f32[16,2,256]{2,1,0:T(2,128)}), f32[16,2,256]{2,1,0:T(2,128)S(1)}, u32[]{:S(2)}, u32[]{:S(2)}) async-start(f32[16,2,256]{2,1,0:T(2,128)} %get-tuple-element.153), calls=%async_computation.7 | async-start | bytes 65536 | tf_op jit(solution)/shard_map/cond/branch_0_fun/all_to_all | solution.py:486
  188.8 19.5 %all-to-all-start.8 = ((bf16[8,224,256]{2,1,0:T(8,128)(2,1)}), bf16[8,224,256]{2,1,0:T(8,128)(2,1)S(1)}, u32[]{:S(2)}, u32[]{:S(2)}) async-start(bf16[8,224,256]{2,1,0:T(8,128)(2,1)} %broadcast_in_dim.153), calls=%async_computation.8 | async-start | bytes 1835008 | tf_op jit(solution)/shard_map/cond/branch_0_fun/all_to_all | solution.py:486

commit v3 on v2

--- a/solution.py
+++ b/solution.py
@@ -14,7 +14,7 @@
 BLK_DEV = 4
 STEPS = 4
 WSTART = 16
-DEPTH = 40
+DEPTH = GROUPS + 1
 LEVELS = (6, 8)
 PIECE = 32
 ROLLED = (8,)
@@ -50,18 +50,9 @@
     return wide == (entry % CLASSES).astype(F32)
 
 
-def selector(length, at):
-    place = lax.broadcasted_iota(I32, (length, at.shape[1]), 0)
-    return (place == at).astype(F32).astype(BF16)
-
-
-def side_by_side(ref):
-    return jnp.concatenate([ref[q] for q in range(ref.shape[0])], axis=1)
-
-
 def embed_kernel(
-    first, at_ref, ev_hbm, stoch_hbm, act_ref, out_hbm, hot_hbm,
-    picks_ref, stoch_ref, hot_ref, out_ref, sem, done_sem,
+    first, at_ref, ev_hbm, stoch_hbm, act_ref, w_hbm, out_hbm, hot_hbm,
+    picks_ref, stoch_ref, wbuf, hot_ref, out_ref, sem, done_sem,
 ):
     steps, rows, _ = hot_ref.shape
     count = rows // PIECE
@@ -85,6 +76,8 @@
     lax.fori_loop(0, steps, start, 0)
     table = pltpu.make_async_copy(stoch_hbm, stoch_ref, done_sem.at[2, 0])
     table.start()
+    weights = pltpu.make_async_copy(w_hbm.at[:, pl.ds(0, HID), :], wbuf, done_sem.at[2, 1])
+    weights.start()
     spread = spread_matrix()
     ids = lax.broadcasted_iota(I32, (rows, act_ref.shape[0]), 1).astype(F32)
 
@@ -105,7 +98,17 @@
         pre = jnp.dot(hot, stoch_ref[...], preferred_element_type=F32) + jnp.dot(
             act_hot, act_ref[...], preferred_element_type=F32
         )
-        out_ref[step] = silu(row_norm(pre)).astype(BF16)
+        embedded = silu(row_norm(pre)).astype(BF16)
+
+        @pl.when(step == 0)
+        def _():
+            weights.wait()
+
+        share = wbuf.shape[2]
+        for k in range(wbuf.shape[0]):
+            out_ref[step, :, k * share : (k + 1) * share] = jnp.dot(
+                embedded, wbuf[k], preferred_element_type=F32
+            )
         give(step, 1).start()
         return 0
 
@@ -130,36 +133,31 @@
     return jnp.transpose(jnp.broadcast_to(row, (128, row.shape[1])))[:rows]
 
 
-def gates_kernel(step, emb_hbm, x_hbm, w_ref, g_ref, stat_ref, x_ref, wbuf, emb_ref, sem):
+def gates_kernel(step, emb_hbm, x_hbm, w_ref, g_ref, stat_ref, x_ref, wbuf, sem):
     parts, depth, share = w_ref.shape
-    chunks = depth // HID
+    chunks = depth // HID - 1
+    per = HID // share
 
     def fetch(c):
-        at = pl.ds(pl.multiple_of(c * HID, HID), HID)
+        at = pl.ds(pl.multiple_of((c + 1) * HID, HID), HID)
         return pltpu.make_async_copy(w_ref.at[:, at, :], wbuf.at[c], sem.at[c])
 
-    emb = pltpu.make_async_copy(emb_hbm.at[step], emb_ref, sem.at[chunks])
-    per = HID // share
-
     def fetch_x(c):
-        at = pl.ds((c - 1) * per, per)
+        at = pl.ds(c * per, per)
         return pltpu.make_async_copy(x_hbm.at[at], x_ref.at[at], sem.at[chunks + c])
 
+    emb = pltpu.make_async_copy(emb_hbm.at[step], g_ref, sem.at[2 * chunks])
+    fetch_x(0).start()
+    fetch(0).start()
     emb.start()
-    fetch(0).start()
     for c in range(1, chunks):
         fetch_x(c).start()
         fetch(c).start()
     emb.wait()
-    fetch(0).wait()
-    for k in range(parts):
-        g_ref[:, k * share : (k + 1) * share] = jnp.dot(
-            emb_ref[...], wbuf[0, k], preferred_element_type=F32
-        )
 
     def add(c, _):
         fetch_x(c).wait()
-        left = jnp.concatenate([x_ref[(c - 1) * per + q] for q in range(per)], axis=1)
+        left = jnp.concatenate([x_ref[c * per + q] for q in range(per)], axis=1)
         fetch(c).wait()
         for k in range(parts):
             g_ref[:, k * share : (k + 1) * share] += jnp.dot(
@@ -167,7 +165,7 @@
             )
         return 0
 
-    lax.fori_loop(1, chunks, add, 0)
+    lax.fori_loop(0, chunks, add, 0)
     rows, width = g_ref.shape
     part = jnp.zeros((rows, 128), F32)
     part_sq = part
@@ -184,6 +182,11 @@
     )
     for q in range(stat_ref.shape[0]):
         stat_ref[q] = sums
+
+
+def spread_copies(low_ref, low_hbm, rows, sem):
+    for k in range(low_hbm.shape[0]):
+        pltpu.make_async_copy(low_ref.at[rows], low_hbm.at[k, rows], sem.at[k]).start()
 
 
 def update_kernel(entries, step, g_ref, stat_ref, carried_ref, live_ref, new_ref, low_ref):
@@ -286,7 +289,8 @@
     out_ref[2:3, :rows] = sigmoid(heads[1:2]) * live
 
 
-def pick_kernel(at_ref, own_ref, other_ref, carried_ref, low_ref, *rest_ref):
+def pick_kernel(at_ref, own_ref, other_ref, carried_ref, low_hbm, *refs):
+    *rest, low_ref, sem = refs
     count, per_task, share = own_ref.shape
     done = carried_ref.shape[0] // per_task
     for i in range(count):
@@ -297,14 +301,18 @@
         rows = slice(i * per_task, (i + 1) * per_task)
         if i < done:
             carried_ref[rows] = value
-            for k in range(low_ref.shape[0]):
-                low_ref[k, rows] = low
+            low_ref[rows] = low
         else:
-            rest_ref[0][(i - done) * per_task : (i - done + 1) * per_task] = low
+            rest[0][(i - done) * per_task : (i - done + 1) * per_task] = low
+        if i == done - 1:
+            spread_copies(low_ref, low_hbm, pl.ds(0, done * per_task), sem)
+    for k in range(low_hbm.shape[0]):
+        pltpu.make_async_copy(low_ref, low_hbm.at[k], sem.at[k]).wait()
 
 
 def settle_kernel(
-    rows, at_ref, got_ref, left_ref, outs_ref, to_ref, log_ref, reward_ref, cont_ref, final_ref, buf, sem
+    rows, at_ref, to_ref, got_ref, left_ref, outs_ref,
+    log_ref, reward_ref, cont_ref, final_ref, buf, tall_ref, mine_ref, sem,
 ):
     count, per_task, share = buf.shape
     done = rows // per_task
@@ -320,14 +328,20 @@
         else:
             pl.when(chunk < done)(functools.partial(bring, got_ref, chunk))
             pl.when(chunk >= done)(functools.partial(bring, left_ref, chunk - done))
-    parts = side_by_side(outs_ref)
+
+    holders, depth, lanes = outs_ref.shape
+    half = depth // 2
+    for d in range(holders):
+        both = outs_ref[d].astype(F32)
+        tall_ref[d * lanes : (d + 1) * lanes] = jnp.transpose(both[:half] + both[half:])
     for t in range(STEPS):
-        values = jnp.dot(
-            parts, selector(parts.shape[1], to_ref[t : t + 1]), preferred_element_type=F32
-        )
+        for i in range(count):
+            at = to_ref[t, i]
+            from_rows = pl.ds(pl.multiple_of(jnp.maximum(at, 0), per_task), per_task)
+            mine_ref[i * per_task : (i + 1) * per_task] = jnp.where(at >= 0, tall_ref[from_rows], 0.0)
+        flat = jnp.transpose(mine_ref[...])
         for k, ref in enumerate((log_ref, reward_ref, cont_ref)):
-            at = t * 3 + k
-            ref[t : t + 1] = values[at : at + 1] + values[12 + at : 13 + at]
+            ref[t : t + 1] = flat[t * 3 + k : t * 3 + k + 1]
     for i in range(count):
         pltpu.make_async_copy(got_ref.at[0, pl.ds(0, per_task)], buf.at[i], sem.at[i]).wait()
         final_ref[i * per_task : (i + 1) * per_task] = buf[i].astype(F32)
@@ -350,24 +364,30 @@
     )
 
 
-def embed(first, steps, at, everyone, stoch, act, rows):
+def embed(first, steps, at, everyone, stoch, act, w, rows):
     depth = everyone.shape[2]
+    parts, _, share = w.shape
+    specs = [SCALARS, STAY, STAY, WHOLE, STAY]
     return pl.pallas_call(
         functools.partial(embed_kernel, first),
-        in_specs=[SCALARS, STAY, STAY, WHOLE],
+        in_specs=specs,
         out_specs=[STAY, STAY],
-        out_shape=[pltpu.HBM((steps, rows, HID), BF16)] * 2,
+        out_shape=[
+            pltpu.HBM((steps, rows, parts * share), F32),
+            pltpu.HBM((steps, rows, HID), BF16),
+        ],
         scratch_shapes=[
             pltpu.VMEM((steps, rows, depth), BF16),
             pltpu.VMEM(stoch.shape, BF16),
+            pltpu.VMEM((parts, HID, share), BF16),
             pltpu.VMEM((steps, rows, HID), BF16),
-            pltpu.VMEM((steps, rows, HID), BF16),
+            pltpu.VMEM((steps, rows, parts * share), F32),
             pltpu.SemaphoreType.DMA((steps, rows // PIECE)),
-            pltpu.SemaphoreType.DMA((3, steps)),
+            pltpu.SemaphoreType.DMA((3, max(steps, 2))),
         ],
         compiler_params=params(24),
         name="embed",
-    )(*placed([SCALARS, STAY, STAY, WHOLE], (at, everyone, stoch, act)))
+    )(*placed(specs, (at, everyone, stoch, act, w)))
 
 
 def stepped(kernel, steps, specs, operands):
@@ -394,16 +414,15 @@
         ],
         scratch_shapes=[
             pltpu.VMEM(x.shape, BF16),
-            pltpu.VMEM((depth // HID, parts, HID, share), BF16),
-            pltpu.VMEM((rows, HID), BF16),
-            pltpu.SemaphoreType.DMA((2 * (depth // HID),)),
+            pltpu.VMEM((depth // HID - 1, parts, HID, share), BF16),
+            pltpu.SemaphoreType.DMA((2 * (depth // HID) - 1,)),
         ],
         compiler_params=params(24),
         name="gates",
     )(*operands)
 
 
-def renew(moment, g, stats, carried, live, entries):
+def renew(moment, g, stats, carried, live, entries, copies):
     kernel, specs, operands = stepped(
         functools.partial(update_kernel, entries), (moment,), [WHOLE] * 4, (g, stats, carried, live)
     )
@@ -413,7 +432,7 @@
         in_specs=specs,
         out_shape=[
             jax.ShapeDtypeStruct((rows, share), F32),
-            jax.ShapeDtypeStruct((stats.shape[0], rows, share), BF16),
+            jax.ShapeDtypeStruct((copies, rows, share), BF16),
         ],
         compiler_params=params(16),
         name="renew",
@@ -453,7 +472,7 @@
     left = count * per_task - rows
     shapes = [
         jax.ShapeDtypeStruct((rows, share), F32),
-        jax.ShapeDtypeStruct((shards, rows, share), BF16),
+        pltpu.HBM((shards, rows, share), BF16),
     ]
     if left:
         shapes.append(jax.ShapeDtypeStruct((left, share), BF16))
@@ -461,25 +480,30 @@
         pick_kernel,
         in_specs=[SCALARS, WHOLE, WHOLE],
         out_shape=shapes,
+        out_specs=[WHOLE, STAY] + [WHOLE] * (len(shapes) - 2),
+        scratch_shapes=[pltpu.VMEM((rows, share), BF16), pltpu.SemaphoreType.DMA((shards,))],
         compiler_params=params(16),
         name="pick",
     )(at, own, other)
 
 
-def settle(at, got, left, outs, to, rows, count, per_task):
+def settle(at, to, got, left, outs, rows, count, per_task):
     share = got.shape[2]
+    holders, depth, lanes = outs.shape
     return pl.pallas_call(
         functools.partial(settle_kernel, rows),
-        in_specs=[SCALARS, EITHER, EITHER, WHOLE, WHOLE],
-        out_shape=[jax.ShapeDtypeStruct(to.shape, F32)] * 3
+        in_specs=[SCALARS, SCALARS, EITHER, EITHER, WHOLE],
+        out_shape=[jax.ShapeDtypeStruct((STEPS, count * per_task), F32)] * 3
         + [jax.ShapeDtypeStruct((count * per_task, share), F32)],
         scratch_shapes=[
             pltpu.VMEM((count, per_task, share), BF16),
+            pltpu.VMEM((holders * lanes, depth // 2), F32),
+            pltpu.VMEM((count * per_task, depth // 2), F32),
             pltpu.SemaphoreType.DMA((count,)),
         ],
         compiler_params=params(16),
         name="settle",
-    )(at, got, left, outs, to)
+    )(at, to, got, left, outs)
 
 
 def exchange(copies, axis):
@@ -509,9 +533,7 @@
     )
     x = exchange(low, "mp")
 
-    sent = jnp.concatenate(
-        [draws, actions[:, None], jnp.zeros((STEPS, DEPTH - GROUPS - 1, all_rows), I32)], axis=1
-    ).astype(BF16)
+    sent = jnp.concatenate([draws, actions[:, None]], axis=1).astype(BF16)
     sent = jnp.concatenate([sent.reshape(STEPS * DEPTH, all_rows), *rest], axis=0)
     everyone = lax.all_gather(sent, "task")
     left = everyone[:, STEPS * DEPTH :]
@@ -534,7 +556,7 @@
     slot = (task[None, :] // per_core + ahead_by) % holders
     source = slot * all_rows + (task % per_core)[None, :] * per_task
     first = STEPS if count in ROLLED else 1
-    emb, hot = embed(0, first, source, everyone, stoch, act, rows)
+    emb, hot = embed(0, first, source, everyone, stoch, act, w, rows)
     x, emb, hot = lax.optimization_barrier((x, emb, hot))
 
     held = jnp.repeat((place - running) % holders, in_block, axis=1) * per_core
@@ -545,8 +567,7 @@
     core = held // pair * 2 + dealt % 2
     chunk = dealt // 2
     settle_at = jnp.stack([core[STEPS - 1], chunk[STEPS - 1]])
-    to = jnp.where(chunk < count, core * 256 + chunk * per_task, -TASKS * 256)
-    to = jnp.repeat(to, per_task, axis=1) + jnp.arange(all_rows, dtype=I32)[None, :] % per_task
+    to = jnp.where(chunk < count, core * share + chunk * per_task, -1)
 
     def likely(at, moment, x, hot):
         return prior(at, moment, x, prior_weight, logit, head, hot, living)[:3]
@@ -554,7 +575,7 @@
     def gated(at, moment, x, emb, carried):
         g, stats = gates(at, emb, x, w)
         stats = exchange(stats, "mp")
-        return renew(moment, g, stats, carried, living, entries)
+        return renew(moment, g, stats, carried, living, entries, shards)
 
     small = []
     if count in ROLLED:
@@ -575,7 +596,7 @@
             carried, low = gated(at, moment, x, emb, carried)
             out = likely(at, moment, x, hot)
             if moment == 0:
-                emb, hot = embed(1, STEPS - 1, source, everyone, stoch, act, rows)
+                emb, hot = embed(1, STEPS - 1, source, everyone, stoch, act, w, rows)
             x = exchange(low, "mp")
             x, out, emb, hot = lax.optimization_barrier((x, out, emb, hot))
             small.append(out)
@@ -585,16 +606,17 @@
     stats = exchange(stats, "mp")
     out = likely(at, STEPS - 1, x, hot)
     stats, small, out = lax.optimization_barrier((stats, small, out))
-    _, low = renew(STEPS - 1, g, stats, carried, living, entries)
+    _, low = renew(STEPS - 1, g, stats, carried, living, entries, 1)
 
     outs = jnp.concatenate([*small, out], axis=0)
     high, low_part = two_parts(outs)
-    sent = jnp.concatenate([low[0], high, low_part, jnp.zeros((8, share), BF16)], axis=0)
+    pad = jnp.zeros((16 - high.shape[0], share), BF16)
+    sent = jnp.concatenate([low[0], high, pad, low_part, pad], axis=0)
     got = exchange(jnp.broadcast_to(sent[None], (holders, *sent.shape)), "task")
-    outs = got[:, rows : rows + 24]
+    outs = got[:, rows:]
     if not rest:
         left = got
-    return settle(settle_at, got, left, outs, to, rows, per_core, per_task)
+    return settle(settle_at, to, got, left, outs, rows, per_core, per_task)
 
 
 def on_device(

time: 212 us -> 211 us (level)
  waiting for transfers between devices: 55 us -> 52.3 us
    pallas_call x2, Pallas kernels: 10.8 us -> 13.5 us  [embed(): pl.pallas_call(functools.partial(embed_kernel, first), in_specs=specs, ou...]
    all_to_all x7, waiting for transfers between devices: 55 us -> 52.3 us  [exchange(): return lax.all_to_all(copies, axis, 0, 0, tiled=True)]
  transfers between devices with their start and end apart: 8 -> 8, of which waited for: 6 -> 6; matrix products, arithmetic and copies ran while one was open for 3% -> 3% of each run, Pallas kernels for 18% -> 20%
where the time goes in v3:
time: 211 us; the launch traced here: 210 us
  Pallas kernels  71.1 us (34%)
  waiting for transfers between devices  52.3 us (25%)
  blocking collectives  39.2 us (19%)
  starting transfers between devices  36.3 us (17%)
  local copies, waits for them, and re-layouts  6.47 us (3%)
  other arithmetic  2.21 us (1%)
    all_to_all x7, waiting for transfers between devices, exchange(): return lax.all_to_all(copies, axis, 0, 0, tiled=True)  52.3 us
    all_to_all x7, starting transfers between devices, exchange(): return lax.all_to_all(copies, axis, 0, 0, tiled=True)  34.8 us
    pallas_call x4, Pallas kernels, prior(): pl.pallas_call(kernel, in_specs=specs, out_shape=jax.ShapeDtypeStruct((8,...  28.1 us
    all_to_all x2, blocking collectives, exchange(): return lax.all_to_all(copies, axis, 0, 0, tiled=True)  24.4 us
    pallas_call x4, Pallas kernels, gates(): pl.pallas_call(kernel, in_specs=specs, out_shape=[jax.ShapeDtypeStruct((r...  18.8 us
    all_gather x1, blocking collectives, window(): everyone = lax.all_gather(sent, 'task')  14.8 us
    pallas_call x2, Pallas kernels, embed(): pl.pallas_call(functools.partial(embed_kernel, first), in_specs=specs, ou...  13.5 us
    pallas_call x4, Pallas kernels, renew(): pl.pallas_call(kernel, in_specs=specs, out_shape=[jax.ShapeDtypeStruct((r...  6.15 us
  transfers between devices with their start and end apart: 8, of which 6 were waited for; matrix products, arithmetic and copies ran while one was open for 3% of the time, Pallas kernels for 20%

profile of v3, /device:TPU:1, one launch (start us, length us, event | category | flops | bytes accessed | tf_op | source)
XLA Modules:
  0.0 209.8 jit_solution(13147274223015194336)
XLA Ops:
  4.9 204.7 %conditional.1 = ((f32[4,256]{1,0:T(4,128)}, f32[4,256]{1,0:T(4,128)}, f32[4,256]{1,0:T(4,128)}, f32[256,256]{1,0:T(8,128)})) conditional(s32[]{:T(128)} %clamp.3, (s32[4,4]{1,0:T(4,128)}, s32[4,16]{1,0:T(4,128)S(1)}, f32[256,256]{1,0:T(8,128)}, f32[256,256]{1,0:T(8,128)S(1)}, s32[8]{0:T(128)S(1)}, /*index=5*/s32[8]{0:T(128)S(1)}, ...), branch_computations={%region_5.10_spmd, %region_10.17_spmd} | conditional | flops 426391 | bytes 57992060 | solution.py:669
  5.0 2.3 %pick.2 = (f32[192,256]{1,0:T(8,128)S(1)}, bf16[16,192,256]{2,1,0:T(8,128)(2,1)}, bf16[64,256]{1,0:T(8,128)(2,1)S(1)}) custom-call(s32[8]{0:T(128)S(1)} %get-tuple-element.624.at_ref, f32[8,32,256]{2,1,0:T(8,128)} %bitcast.37, f32[8,32,256]{2,1,0:T(8,128)S(1)} %bitcast.39), custom_call_target="tpu_custom_call" | custom-call | tf_op jit(solution)/shard_map/cond/branch_0_fun/pick/pallas_call | solution.py:479
  7.3 6.8 %all-to-all-start = ((bf16[16,192,256]{2,1,0:T(8,128)(2,1)}), bf16[16,192,256]{2,1,0:T(8,128)(2,1)S(1)}, u32[]{:S(2)}, u32[]{:S(2)}) async-start(bf16[16,192,256]{2,1,0:T(8,128)(2,1)} %get-tuple-element.113), calls=%async_computation | async-start | bytes 3145728 | tf_op jit(solution)/shard_map/cond/branch_0_fun/all_to_all | solution.py:510
  14.7 14.8 %all-gather.1 = bf16[8,196,256]{2,1,0:T(8,128)(2,1)S(1)} all-gather(bf16[1,196,256]{2,1,0:T(8,128)(2,1)S(1)} %maximum_bitcast_fusion), channel_id=2, replica_groups=mesh['task'=8,'mp'=16] {'task'}, dimensions={0}, use_global_device_ids=true | all-gather | bytes 903168 | tf_op jit(solution)/shard_map/cond/branch_0_fun/all_gather | solution.py:538
  30.6 1.9 copy.74
  32.7 4.8 %embed.3 = (f32[1,192,768]{2,1,0:T(8,128)}, bf16[1,192,1024]{2,1,0:T(8,128)(2,1)}) custom-call(s32[4,8]{1,0:T(4,128)S(1)} %fusion.11.at_ref, bf16[4,2048,33]{2,1,0:T(8,128)(2,1)} %bitcast.32, bf16[1024,1024]{1,0:T(8,128)(2,1)} %get-tuple-element.267.stoch_hbm, bf16[18,1024]{1,0:T(8,128)(2,1)S(1)} %copy-done.9, ...), custom_call_target="tpu_custom_call" | custom-call | tf_op jit(solution)/shard_map/cond/branch_0_fun/embed/pallas_call | solution.py:371
  37.7 1.9 all-to-all-done.x_hbm
  39.6 5.0 %gates.6 = (f32[192,768]{1,0:T(8,128)S(1)}, f32[16,2,256]{2,1,0:T(2,128)}) custom-call(f32[1,192,768]{2,1,0:T(8,128)} %get-tuple-element.123.emb_hbm, bf16[16,192,256]{2,1,0:T(8,128)(2,1)S(1)} %all-to-all-done.x_hbm, bf16[3,5120,256]{2,1,0:T(8,128)(2,1)} %get-tuple-element.120.w_hbm.w_ref), custom_call_target="tpu_custom_call" | custom-call | tf_op jit(solution)/shard_map/cond/branch_0_fun/gates/pallas_call | solution.py:408
  44.6 5.1 %all-to-all-start.1 = ((f32[16,2,256]{2,1,0:T(2,128)}), f32[16,2,256]{2,1,0:T(2,128)S(1)}, u32[]{:S(2)}, u32[]{:S(2)}) async-start(f32[16,2,256]{2,1,0:T(2,128)} %get-tuple-element.126), calls=%async_computation.1 | async-start | bytes 65536 | tf_op jit(solution)/shard_map/cond/branch_0_fun/all_to_all | solution.py:510
  49.9 6.2 %all-to-all-done.1.stat_ref = f32[16,2,256]{2,1,0:T(2,128)S(1)} async-done(((f32[16,2,256]{2,1,0:T(2,128)}), f32[16,2,256]{2,1,0:T(2,128)S(1)}, u32[]{:S(2)}, u32[]{:S(2)}) %all-to-all-start.1) | async-done | bytes 32800 | tf_op jit(solution)/shard_map/cond/branch_0_fun/all_to_all | solution.py:510
  57.8 3.7 %all-to-all-start.2 = ((bf16[16,192,256]{2,1,0:T(8,128)(2,1)}), bf16[16,192,256]{2,1,0:T(8,128)(2,1)S(1)}, u32[]{:S(2)}, u32[]{:S(2)}) async-start(bf16[16,192,256]{2,1,0:T(8,128)(2,1)} %get-tuple-element.129), calls=%async_computation.2 | async-start | bytes 3145728 | tf_op jit(solution)/shard_map/cond/branch_0_fun/all_to_all | solution.py:510
  61.6 8.7 %embed.4 = (f32[3,192,768]{2,1,0:T(8,128)}, bf16[3,192,1024]{2,1,0:T(8,128)(2,1)}) custom-call(s32[4,8]{1,0:T(4,128)S(1)} %fusion.11.at_ref, bf16[4,2048,33]{2,1,0:T(8,128)(2,1)} %bitcast.33, bf16[1024,1024]{1,0:T(8,128)(2,1)} %get-tuple-element.267.stoch_hbm, bf16[18,1024]{1,0:T(8,128)(2,1)S(1)} %copy-done.9, ...), custom_call_target="tpu_custom_call" | custom-call | tf_op jit(solution)/shard_map/cond/branch_0_fun/embed/pallas_call | solution.py:371
  70.3 7.0 %prior.6 = f32[8,256]{1,0:T(8,128)S(1)} custom-call(bf16[16,192,256]{2,1,0:T(8,128)(2,1)} %copy-done, bf16[4096,1024]{1,0:T(8,128)(2,1)} %get-tuple-element.271.w_ref, bf16[1024,1024]{1,0:T(8,128)(2,1)} %get-tuple-element.273.logit_ref, bf16[2,1024]{1,0:T(2,128)(2,1)S(1)} %copy-done.11, bf16[1,192,1024]{2,1,0:T(8,128)(2,1)} %get-tuple-element.133.hot_hbm, ...), custom_call_target="tpu_custom_call" | custom-call | tf_op jit(solution)/shard_map/cond/branch_0_fun/prior/pallas_call | solution.py:451
  77.4 5.1 %all-to-all-done.2.x_hbm = bf16[16,192,256]{2,1,0:T(8,128)(2,1)S(1)} async-done(((bf16[16,192,256]{2,1,0:T(8,128)(2,1)}), bf16[16,192,256]{2,1,0:T(8,128)(2,1)S(1)}, u32[]{:S(2)}, u32[]{:S(2)}) %all-to-all-start.2) | async-done | bytes 1572896 | tf_op jit(solution)/shard_map/cond/branch_0_fun/all_to_all | solution.py:510
  82.5 4.4 %gates.7 = (f32[192,768]{1,0:T(8,128)S(1)}, f32[16,2,256]{2,1,0:T(2,128)S(1)}) custom-call(f32[3,192,768]{2,1,0:T(8,128)} %get-tuple-element.150.emb_hbm, bf16[16,192,256]{2,1,0:T(8,128)(2,1)S(1)} %all-to-all-done.2.x_hbm, bf16[3,5120,256]{2,1,0:T(8,128)(2,1)} %get-tuple-element.120.w_hbm.w_ref), custom_call_target="tpu_custom_call" | custom-call | tf_op jit(solution)/shard_map/cond/branch_0_fun/gates/pallas_call | solution.py:408
  86.9 12.5 %all_to_all.62.stat_ref = f32[16,2,256]{2,1,0:T(2,128)S(1)} all-to-all(f32[16,2,256]{2,1,0:T(2,128)S(1)} %get-tuple-element.139), channel_id=1, replica_groups=mesh['task'=8,'mp'=16] {'mp'}, dimensions={0} | all-to-all | bytes 65536 | tf_op jit(solution)/shard_map/cond/branch_0_fun/all_to_all | solution.py:510
  99.4 1.7 renew.7
  101.1 3.7 %all-to-all-start.4 = ((bf16[16,192,256]{2,1,0:T(8,128)(2,1)}), bf16[16,192,256]{2,1,0:T(8,128)(2,1)S(1)}, u32[]{:S(2)}, u32[]{:S(2)}) async-start(bf16[16,192,256]{2,1,0:T(8,128)(2,1)} %get-tuple-element.141), calls=%async_computation.4 | async-start | bytes 3145728 | tf_op jit(solution)/shard_map/cond/branch_0_fun/all_to_all | solution.py:510
  104.8 7.0 %prior.7 = f32[8,256]{1,0:T(8,128)S(1)} custom-call(bf16[16,192,256]{2,1,0:T(8,128)(2,1)} %copy-done.1, bf16[4096,1024]{1,0:T(8,128)(2,1)} %get-tuple-element.271.w_ref, bf16[1024,1024]{1,0:T(8,128)(2,1)} %get-tuple-element.273.logit_ref, bf16[2,1024]{1,0:T(2,128)(2,1)S(1)} %copy-done.11, bf16[3,192,1024]{2,1,0:T(8,128)(2,1)} %get-tuple-element.157.hot_hbm, ...), custom_call_target="tpu_custom_call" | custom-call | tf_op jit(solution)/shard_map/cond/branch_0_fun/prior/pallas_call | solution.py:451
  111.9 13.6 %all-to-all-done.4.x_hbm = bf16[16,192,256]{2,1,0:T(8,128)(2,1)S(1)} async-done(((bf16[16,192,256]{2,1,0:T(8,128)(2,1)}), bf16[16,192,256]{2,1,0:T(8,128)(2,1)S(1)}, u32[]{:S(2)}, u32[]{:S(2)}) %all-to-all-start.4) | async-done | bytes 1572896 | tf_op jit(solution)/shard_map/cond/branch_0_fun/all_to_all | solution.py:510
  125.4 4.4 %gates.8 = (f32[192,768]{1,0:T(8,128)S(1)}, f32[16,2,256]{2,1,0:T(2,128)S(1)}) custom-call(f32[3,192,768]{2,1,0:T(8,128)} %get-tuple-element.150.emb_hbm, bf16[16,192,256]{2,1,0:T(8,128)(2,1)S(1)} %all-to-all-done.4.x_hbm, bf16[3,5120,256]{2,1,0:T(8,128)(2,1)} %get-tuple-element.120.w_hbm.w_ref), custom_call_target="tpu_custom_call" | custom-call | tf_op jit(solution)/shard_map/cond/branch_0_fun/gates/pallas_call | solution.py:408
  129.8 11.9 %all_to_all.63.stat_ref = f32[16,2,256]{2,1,0:T(2,128)S(1)} all-to-all(f32[16,2,256]{2,1,0:T(2,128)S(1)} %get-tuple-element.146), channel_id=1, replica_groups=mesh['task'=8,'mp'=16] {'mp'}, dimensions={0} | all-to-all | bytes 65536 | tf_op jit(solution)/shard_map/cond/branch_0_fun/all_to_all | solution.py:510
  141.7 1.7 renew.8
  143.5 3.7 %all-to-all-start.6 = ((bf16[16,192,256]{2,1,0:T(8,128)(2,1)}), bf16[16,192,256]{2,1,0:T(8,128)(2,1)S(1)}, u32[]{:S(2)}, u32[]{:S(2)}) async-start(bf16[16,192,256]{2,1,0:T(8,128)(2,1)} %get-tuple-element.148), calls=%async_computation.6 | async-start | bytes 3145728 | tf_op jit(solution)/shard_map/cond/branch_0_fun/all_to_all | solution.py:510
  147.2 7.0 %prior.8 = f32[8,256]{1,0:T(8,128)S(1)} custom-call(bf16[16,192,256]{2,1,0:T(8,128)(2,1)} %copy-done.2, bf16[4096,1024]{1,0:T(8,128)(2,1)} %get-tuple-element.271.w_ref, bf16[1024,1024]{1,0:T(8,128)(2,1)} %get-tuple-element.273.logit_ref, bf16[2,1024]{1,0:T(2,128)(2,1)S(1)} %copy-done.11, bf16[3,192,1024]{2,1,0:T(8,128)(2,1)} %get-tuple-element.157.hot_hbm, ...), custom_call_target="tpu_custom_call" | custom-call | tf_op jit(solution)/shard_map/cond/branch_0_fun/prior/pallas_call | solution.py:451
  154.2 13.3 %all-to-all-done.6.x_hbm = bf16[16,192,256]{2,1,0:T(8,128)(2,1)S(1)} async-done(((bf16[16,192,256]{2,1,0:T(8,128)(2,1)}), bf16[16,192,256]{2,1,0:T(8,128)(2,1)S(1)}, u32[]{:S(2)}, u32[]{:S(2)}) %all-to-all-start.6) | async-done | bytes 1572896 | tf_op jit(solution)/shard_map/cond/branch_0_fun/all_to_all | solution.py:510
  167.6 5.0 %gates.9 = (f32[192,768]{1,0:T(8,128)S(1)}, f32[16,2,256]{2,1,0:T(2,128)}) custom-call(f32[3,192,768]{2,1,0:T(8,128)} %get-tuple-element.150.emb_hbm, bf16[16,192,256]{2,1,0:T(8,128)(2,1)S(1)} %all-to-all-done.6.x_hbm, bf16[3,5120,256]{2,1,0:T(8,128)(2,1)} %get-tuple-element.120.w_hbm.w_ref), custom_call_target="tpu_custom_call" | custom-call | tf_op jit(solution)/shard_map/cond/branch_0_fun/gates/pallas_call | solution.py:408
  172.6 5.5 %all-to-all-start.7 = ((f32[16,2,256]{2,1,0:T(2,128)}), f32[16,2,256]{2,1,0:T(2,128)S(1)}, u32[]{:S(2)}, u32[]{:S(2)}) async-start(f32[16,2,256]{2,1,0:T(2,128)} %get-tuple-element.153), calls=%async_computation.7 | async-start | bytes 65536 | tf_op jit(solution)/shard_map/cond/branch_0_fun/all_to_all | solution.py:510
  178.1 7.0 %prior.9 = f32[8,256]{1,0:T(8,128)S(1)} custom-call(bf16[16,192,256]{2,1,0:T(8,128)(2,1)} %copy-done.3, bf16[4096,1024]{1,0:T(8,128)(2,1)} %get-tuple-element.271.w_ref, bf16[1024,1024]{1,0:T(8,128)(2,1)} %get-tuple-element.273.logit_ref, bf16[2,1024]{1,0:T(2,128)(2,1)S(1)} %copy-done.11, bf16[3,192,1024]{2,1,0:T(8,128)(2,1)} %get-tuple-element.157.hot_hbm, ...), custom_call_target="tpu_custom_call" | custom-call | tf_op jit(solution)/shard_map/cond/branch_0_fun/prior/pallas_call | solution.py:451
  187.2 6.3 %all-to-all-start.8 = ((bf16[8,224,256]{2,1,0:T(8,128)(2,1)}), bf16[8,224,256]{2,1,0:T(8,128)(2,1)S(1)}, u32[]{:S(2)}, u32[]{:S(2)}) async-start(bf16[8,224,256]{2,1,0:T(8,128)(2,1)} %broadcast_in_dim.145), calls=%async_computation.8 | async-start | bytes 1835008 | tf_op jit(solution)/shard_map/cond/branch_0_fun/all_to_all | solution.py:510
  194.9 12.2 %all-to-all-done.8.got_ref = bf16[8,224,256]{2,1,0:T(8,128)(2,1)S(1)} async-done(((bf16[8,224,256]{2,1,0:T(8,128)(2,1)}), bf16[8,224,256]{2,1,0:T(8,128)(2,1)S(1)}, u32[]{:S(2)}, u32[]{:S(2)}) %all-to-all-start.8) | async-done | bytes 917536 | tf_op jit(solution)/shard_map/cond/branch_0_fun/all_to_all | solution.py:510
  207.1 2.2 %settle.2 = (f32[4,256]{1,0:T(4,128)}, f32[4,256]{1,0:T(4,128)}, f32[4,256]{1,0:T(4,128)}, f32[256,256]{1,0:T(8,128)}) custom-call(s32[2,8]{1,0:T(2,128)S(1)} %pad_add_fusion.at_ref, s32[4,8]{1,0:T(4,128)S(1)} %get-tuple-element.607.to_ref, bf16[8,224,256]{2,1,0:T(8,128)(2,1)S(1)} %all-to-all-done.8.got_ref, bf16[8,64,256]{2,1,0:T(8,128)(2,1)S(1)} %slice.48.left_ref, ...), custom_call_target="tpu_custom_call" | custom-call | tf_op jit(solution)/shard_map/cond/branch_0_fun/settle/pallas_call | solution.py:493
  (83 shorter events, 11.0 us)
Async XLA Ops:
  0.6 4.2 %collective-permute-start = (f32[256,256]{1,0:T(8,128)}, f32[256,256]{1,0:T(8,128)S(1)}, u32[]{:S(2)}, u32[]{:S(2)}) collective-permute-start(f32[256,256]{1,0:T(8,128)} %param.15), channel_id=1, source_target_pairs={{0,16},{16,0},{32,48},{48,32},{64,80},{80,64},{96,112},{112,96},{1... | collective-permute-start | bytes 786440 | tf_op jit(solution)/shard_map/ppermute | solution.py:642
  4.9 9.3 %copy-start.15 = (s32[4,4]{1,0:T(4,128)S(1)}, s32[4,4]{1,0:T(4,128)}, u32[]{:S(2)}) copy-start(s32[4,4]{1,0:T(4,128)} %get-tuple-element.522) | copy-start | bytes 196 | tf_op jit(solution)/shard_map/cond
  4.9 9.7 %copy-start.13 = (s32[4,256]{1,0:T(4,128)S(1)}, s32[4,256]{1,0:T(4,128)}, u32[]{:S(2)}) copy-start(s32[4,256]{1,0:T(4,128)} %get-tuple-element.265) | copy-start | bytes 12292 | tf_op jit(solution)/shard_map/cond
  4.9 9.7 %copy-start.7 = (s32[4,32,256]{2,1,0:T(8,128)S(1)}, s32[4,32,256]{2,1,0:T(8,128)}, u32[]{:S(2)}) copy-start(s32[4,32,256]{2,1,0:T(8,128)} %get-tuple-element.263) | copy-start | bytes 393220 | tf_op jit(solution)/shard_map/cond
  7.3 32.2 %all-to-all-start = ((bf16[16,192,256]{2,1,0:T(8,128)(2,1)}), bf16[16,192,256]{2,1,0:T(8,128)(2,1)S(1)}, u32[]{:S(2)}, u32[]{:S(2)}) async-start(bf16[16,192,256]{2,1,0:T(8,128)(2,1)} %get-tuple-element.113), calls=%async_computation | async-start | bytes 3145728 | tf_op jit(solution)/shard_map/cond/branch_0_fun/all_to_all | solution.py:510
  29.5 1.0 copy-start.6
  30.5 2.1 %copy-start.9 = (bf16[18,1024]{1,0:T(8,128)(2,1)S(1)}, bf16[18,1024]{1,0:T(8,128)(2,1)}, u32[]{:S(2)}) copy-start(bf16[18,1024]{1,0:T(8,128)(2,1)} %get-tuple-element.269.act_ref) | copy-start | bytes 110596 | tf_op jit(solution)/shard_map/cond
  32.7 4.8 %copy-start.16 = (s32[64]{0:T(128)S(1)}, s32[64]{0:T(128)}, u32[]{:S(2)}) copy-start(s32[64]{0:T(128)} %get-tuple-element.128) | copy-start | bytes 772 | tf_op jit(solution)/shard_map/cond
  39.6 5.0 %copy-start = (bf16[16,192,256]{2,1,0:T(8,128)(2,1)}, bf16[16,192,256]{2,1,0:T(8,128)(2,1)S(1)}, u32[]{:S(2)}) copy-start(bf16[16,192,256]{2,1,0:T(8,128)(2,1)S(1)} %all-to-all-done.x_hbm) | copy-start | bytes 4718596 | tf_op jit(solution)/shard_map/cond
  44.6 11.5 %all-to-all-start.1 = ((f32[16,2,256]{2,1,0:T(2,128)}), f32[16,2,256]{2,1,0:T(2,128)S(1)}, u32[]{:S(2)}, u32[]{:S(2)}) async-start(f32[16,2,256]{2,1,0:T(2,128)} %get-tuple-element.126), calls=%async_computation.1 | async-start | bytes 65536 | tf_op jit(solution)/shard_map/cond/branch_0_fun/all_to_all | solution.py:510
  57.8 24.6 %all-to-all-start.2 = ((bf16[16,192,256]{2,1,0:T(8,128)(2,1)}), bf16[16,192,256]{2,1,0:T(8,128)(2,1)S(1)}, u32[]{:S(2)}, u32[]{:S(2)}) async-start(bf16[16,192,256]{2,1,0:T(8,128)(2,1)} %get-tuple-element.129), calls=%async_computation.2 | async-start | bytes 3145728 | tf_op jit(solution)/shard_map/cond/branch_0_fun/all_to_all | solution.py:510
  61.6 8.7 %copy-start.11 = (bf16[2,1024]{1,0:T(2,128)(2,1)S(1)}, bf16[2,1024]{1,0:T(2,128)(2,1)}, u32[]{:S(2)}) copy-start(bf16[2,1024]{1,0:T(2,128)(2,1)} %get-tuple-element.132.head_ref) | copy-start | bytes 12292 | tf_op jit(solution)/shard_map/cond
  82.5 4.4 %copy-start.1 = (bf16[16,192,256]{2,1,0:T(8,128)(2,1)}, bf16[16,192,256]{2,1,0:T(8,128)(2,1)S(1)}, u32[]{:S(2)}) copy-start(bf16[16,192,256]{2,1,0:T(8,128)(2,1)S(1)} %all-to-all-done.2.x_hbm) | copy-start | bytes 4718596 | tf_op jit(solution)/shard_map/cond
  101.1 24.3 %all-to-all-start.4 = ((bf16[16,192,256]{2,1,0:T(8,128)(2,1)}), bf16[16,192,256]{2,1,0:T(8,128)(2,1)S(1)}, u32[]{:S(2)}, u32[]{:S(2)}) async-start(bf16[16,192,256]{2,1,0:T(8,128)(2,1)} %get-tuple-element.141), calls=%async_computation.4 | async-start | bytes 3145728 | tf_op jit(solution)/shard_map/cond/branch_0_fun/all_to_all | solution.py:510
  125.4 4.4 %copy-start.2 = (bf16[16,192,256]{2,1,0:T(8,128)(2,1)}, bf16[16,192,256]{2,1,0:T(8,128)(2,1)S(1)}, u32[]{:S(2)}) copy-start(bf16[16,192,256]{2,1,0:T(8,128)(2,1)S(1)} %all-to-all-done.4.x_hbm) | copy-start | bytes 4718596 | tf_op jit(solution)/shard_map/cond
  143.5 24.1 %all-to-all-start.6 = ((bf16[16,192,256]{2,1,0:T(8,128)(2,1)}), bf16[16,192,256]{2,1,0:T(8,128)(2,1)S(1)}, u32[]{:S(2)}, u32[]{:S(2)}) async-start(bf16[16,192,256]{2,1,0:T(8,128)(2,1)} %get-tuple-element.148), calls=%async_computation.6 | async-start | bytes 3145728 | tf_op jit(solution)/shard_map/cond/branch_0_fun/all_to_all | solution.py:510
  167.6 5.0 %copy-start.3 = (bf16[16,192,256]{2,1,0:T(8,128)(2,1)}, bf16[16,192,256]{2,1,0:T(8,128)(2,1)S(1)}, u32[]{:S(2)}) copy-start(bf16[16,192,256]{2,1,0:T(8,128)(2,1)S(1)} %all-to-all-done.6.x_hbm) | copy-start | bytes 4718596 | tf_op jit(solution)/shard_map/cond
  172.6 12.5 %all-to-all-start.7 = ((f32[16,2,256]{2,1,0:T(2,128)}), f32[16,2,256]{2,1,0:T(2,128)S(1)}, u32[]{:S(2)}, u32[]{:S(2)}) async-start(f32[16,2,256]{2,1,0:T(2,128)} %get-tuple-element.153), calls=%async_computation.7 | async-start | bytes 65536 | tf_op jit(solution)/shard_map/cond/branch_0_fun/all_to_all | solution.py:510
  187.2 20.0 %all-to-all-start.8 = ((bf16[8,224,256]{2,1,0:T(8,128)(2,1)}), bf16[8,224,256]{2,1,0:T(8,128)(2,1)S(1)}, u32[]{:S(2)}, u32[]{:S(2)}) async-start(bf16[8,224,256]{2,1,0:T(8,128)(2,1)} %broadcast_in_dim.145), calls=%async_computation.8 | async-start | bytes 1835008 | tf_op jit(solution)/shard_map/cond/branch_0_fun/all_to_all | solution.py:510

commit v4 on v3

--- a/solution.py
+++ b/solution.py
@@ -612,7 +612,10 @@
     high, low_part = two_parts(outs)
     pad = jnp.zeros((16 - high.shape[0], share), BF16)
     sent = jnp.concatenate([low[0], high, pad, low_part, pad], axis=0)
-    got = exchange(jnp.broadcast_to(sent[None], (holders, *sent.shape)), "task")
+    if count in ROLLED:
+        got = exchange(jnp.broadcast_to(sent[None], (holders, *sent.shape)), "task")
+    else:
+        got = lax.all_gather(sent, "task")
     outs = got[:, rows:]
     if not rest:
         left = got

time: 211 us -> 206 us (0.976)
  blocking collectives: 39.2 us -> 54.7 us
  waiting for transfers between devices: 52.3 us -> 39.7 us
  starting transfers between devices: 36.3 us -> 30 us
    all_gather x0 -> x1, blocking collectives: none -> 15.5 us  [window(): got = lax.all_gather(sent, 'task')]
    all_to_all x7 -> x6, waiting for transfers between devices: 52.3 us -> 39.7 us  [exchange(): return lax.all_to_all(copies, axis, 0, 0, tiled=True)]
    all_to_all x7 -> x6, starting transfers between devices: 34.8 us -> 28.5 us  [exchange(): return lax.all_to_all(copies, axis, 0, 0, tiled=True)]
  transfers between devices with their start and end apart: 8 -> 7, of which waited for: 6 -> 5; matrix products, arithmetic and copies ran while one was open for 3% -> 3% of each run, Pallas kernels for 20% -> 20%
where the time goes in v4:
time: 206 us; the launch traced here: 205 us
  Pallas kernels  71.2 us (35%)
  blocking collectives  54.7 us (27%)
  waiting for transfers between devices  39.7 us (19%)
  starting transfers between devices  30 us (15%)
  local copies, waits for them, and re-layouts  5.48 us (3%)
  other arithmetic  2.21 us (1%)
    all_to_all x6, waiting for transfers between devices, exchange(): return lax.all_to_all(copies, axis, 0, 0, tiled=True)  39.7 us
    all_to_all x6, starting transfers between devices, exchange(): return lax.all_to_all(copies, axis, 0, 0, tiled=True)  28.5 us
    pallas_call x4, Pallas kernels, prior(): pl.pallas_call(kernel, in_specs=specs, out_shape=jax.ShapeDtypeStruct((8,...  28.1 us
    all_to_all x2, blocking collectives, exchange(): return lax.all_to_all(copies, axis, 0, 0, tiled=True)  24.4 us
    pallas_call x4, Pallas kernels, gates(): pl.pallas_call(kernel, in_specs=specs, out_shape=[jax.ShapeDtypeStruct((r...  18.8 us
    all_gather x1, blocking collectives, window(): got = lax.all_gather(sent, 'task')  15.5 us
    all_gather x1, blocking collectives, window(): everyone = lax.all_gather(sent, 'task')  14.8 us
    pallas_call x2, Pallas kernels, embed(): pl.pallas_call(functools.partial(embed_kernel, first), in_specs=specs, ou...  13.5 us
  transfers between devices with their start and end apart: 7, of which 5 were waited for; matrix products, arithmetic and copies ran while one was open for 3% of the time, Pallas kernels for 20%

profile of v4, /device:TPU:1, one launch (start us, length us, event | category | flops | bytes accessed | tf_op | source)
XLA Modules:
  0.0 205.5 jit_solution(3071988272863899309)
XLA Ops:
  4.9 200.4 %conditional.1 = ((f32[4,256]{1,0:T(4,128)}, f32[4,256]{1,0:T(4,128)}, f32[4,256]{1,0:T(4,128)}, f32[256,256]{1,0:T(8,128)})) conditional(s32[]{:T(128)} %clamp.3, (s32[4,4]{1,0:T(4,128)}, s32[4,16]{1,0:T(4,128)S(1)}, f32[256,256]{1,0:T(8,128)}, f32[256,256]{1,0:T(8,128)S(1)}, s32[8]{0:T(128)S(1)}, /*index=5*/s32[8]{0:T(128)S(1)}, ...), branch_computations={%region_5.10_spmd, %region_10.17_spmd} | conditional | flops 426391 | bytes 55239516 | solution.py:672
  5.0 2.3 %pick.2 = (f32[192,256]{1,0:T(8,128)S(1)}, bf16[16,192,256]{2,1,0:T(8,128)(2,1)}, bf16[64,256]{1,0:T(8,128)(2,1)S(1)}) custom-call(s32[8]{0:T(128)S(1)} %get-tuple-element.624.at_ref, f32[8,32,256]{2,1,0:T(8,128)} %bitcast.40, f32[8,32,256]{2,1,0:T(8,128)S(1)} %bitcast.42), custom_call_target="tpu_custom_call" | custom-call | tf_op jit(solution)/shard_map/cond/branch_0_fun/pick/pallas_call | solution.py:479
  7.3 6.8 %all-to-all-start = ((bf16[16,192,256]{2,1,0:T(8,128)(2,1)}), bf16[16,192,256]{2,1,0:T(8,128)(2,1)S(1)}, u32[]{:S(2)}, u32[]{:S(2)}) async-start(bf16[16,192,256]{2,1,0:T(8,128)(2,1)} %get-tuple-element.113), calls=%async_computation | async-start | bytes 3145728 | tf_op jit(solution)/shard_map/cond/branch_0_fun/all_to_all | solution.py:510
  14.7 14.8 %all-gather.2 = bf16[8,196,256]{2,1,0:T(8,128)(2,1)S(1)} all-gather(bf16[1,196,256]{2,1,0:T(8,128)(2,1)S(1)} %maximum_bitcast_fusion), channel_id=2, replica_groups=mesh['task'=8,'mp'=16] {'task'}, dimensions={0}, use_global_device_ids=true | all-gather | bytes 903168 | tf_op jit(solution)/shard_map/cond/branch_0_fun/all_gather | solution.py:538
  30.6 1.9 copy.74
  32.7 4.8 %embed.3 = (f32[1,192,768]{2,1,0:T(8,128)}, bf16[1,192,1024]{2,1,0:T(8,128)(2,1)}) custom-call(s32[4,8]{1,0:T(4,128)S(1)} %fusion.11.at_ref, bf16[4,2048,33]{2,1,0:T(8,128)(2,1)} %bitcast.35, bf16[1024,1024]{1,0:T(8,128)(2,1)} %get-tuple-element.267.stoch_hbm, bf16[18,1024]{1,0:T(8,128)(2,1)S(1)} %copy-done.9, ...), custom_call_target="tpu_custom_call" | custom-call | tf_op jit(solution)/shard_map/cond/branch_0_fun/embed/pallas_call | solution.py:371
  37.7 1.9 all-to-all-done.x_hbm
  39.6 5.0 %gates.6 = (f32[192,768]{1,0:T(8,128)S(1)}, f32[16,2,256]{2,1,0:T(2,128)}) custom-call(f32[1,192,768]{2,1,0:T(8,128)} %get-tuple-element.123.emb_hbm, bf16[16,192,256]{2,1,0:T(8,128)(2,1)S(1)} %all-to-all-done.x_hbm, bf16[3,5120,256]{2,1,0:T(8,128)(2,1)} %get-tuple-element.120.w_hbm.w_ref), custom_call_target="tpu_custom_call" | custom-call | tf_op jit(solution)/shard_map/cond/branch_0_fun/gates/pallas_call | solution.py:408
  44.6 5.1 %all-to-all-start.1 = ((f32[16,2,256]{2,1,0:T(2,128)}), f32[16,2,256]{2,1,0:T(2,128)S(1)}, u32[]{:S(2)}, u32[]{:S(2)}) async-start(f32[16,2,256]{2,1,0:T(2,128)} %get-tuple-element.126), calls=%async_computation.1 | async-start | bytes 65536 | tf_op jit(solution)/shard_map/cond/branch_0_fun/all_to_all | solution.py:510
  49.9 6.2 %all-to-all-done.1.stat_ref = f32[16,2,256]{2,1,0:T(2,128)S(1)} async-done(((f32[16,2,256]{2,1,0:T(2,128)}), f32[16,2,256]{2,1,0:T(2,128)S(1)}, u32[]{:S(2)}, u32[]{:S(2)}) %all-to-all-start.1) | async-done | bytes 32800 | tf_op jit(solution)/shard_map/cond/branch_0_fun/all_to_all | solution.py:510
  56.1 1.7 renew.6
  57.9 3.7 %all-to-all-start.2 = ((bf16[16,192,256]{2,1,0:T(8,128)(2,1)}), bf16[16,192,256]{2,1,0:T(8,128)(2,1)S(1)}, u32[]{:S(2)}, u32[]{:S(2)}) async-start(bf16[16,192,256]{2,1,0:T(8,128)(2,1)} %get-tuple-element.129), calls=%async_computation.2 | async-start | bytes 3145728 | tf_op jit(solution)/shard_map/cond/branch_0_fun/all_to_all | solution.py:510
  61.6 8.7 %embed.4 = (f32[3,192,768]{2,1,0:T(8,128)}, bf16[3,192,1024]{2,1,0:T(8,128)(2,1)}) custom-call(s32[4,8]{1,0:T(4,128)S(1)} %fusion.11.at_ref, bf16[4,2048,33]{2,1,0:T(8,128)(2,1)} %bitcast.36, bf16[1024,1024]{1,0:T(8,128)(2,1)} %get-tuple-element.267.stoch_hbm, bf16[18,1024]{1,0:T(8,128)(2,1)S(1)} %copy-done.9, ...), custom_call_target="tpu_custom_call" | custom-call | tf_op jit(solution)/shard_map/cond/branch_0_fun/embed/pallas_call | solution.py:371
  70.3 7.0 %prior.6 = f32[8,256]{1,0:T(8,128)S(1)} custom-call(bf16[16,192,256]{2,1,0:T(8,128)(2,1)} %copy-done, bf16[4096,1024]{1,0:T(8,128)(2,1)} %get-tuple-element.271.w_ref, bf16[1024,1024]{1,0:T(8,128)(2,1)} %get-tuple-element.273.logit_ref, bf16[2,1024]{1,0:T(2,128)(2,1)S(1)} %copy-done.11, bf16[1,192,1024]{2,1,0:T(8,128)(2,1)} %get-tuple-element.133.hot_hbm, ...), custom_call_target="tpu_custom_call" | custom-call | tf_op jit(solution)/shard_map/cond/branch_0_fun/prior/pallas_call | solution.py:451
  77.4 5.1 %all-to-all-done.2.x_hbm = bf16[16,192,256]{2,1,0:T(8,128)(2,1)S(1)} async-done(((bf16[16,192,256]{2,1,0:T(8,128)(2,1)}), bf16[16,192,256]{2,1,0:T(8,128)(2,1)S(1)}, u32[]{:S(2)}, u32[]{:S(2)}) %all-to-all-start.2) | async-done | bytes 1572896 | tf_op jit(solution)/shard_map/cond/branch_0_fun/all_to_all | solution.py:510
  82.5 4.4 %gates.7 = (f32[192,768]{1,0:T(8,128)S(1)}, f32[16,2,256]{2,1,0:T(2,128)S(1)}) custom-call(f32[3,192,768]{2,1,0:T(8,128)} %get-tuple-element.150.emb_hbm, bf16[16,192,256]{2,1,0:T(8,128)(2,1)S(1)} %all-to-all-done.2.x_hbm, bf16[3,5120,256]{2,1,0:T(8,128)(2,1)} %get-tuple-element.120.w_hbm.w_ref), custom_call_target="tpu_custom_call" | custom-call | tf_op jit(solution)/shard_map/cond/branch_0_fun/gates/pallas_call | solution.py:408
  86.9 12.5 %all_to_all.58.stat_ref = f32[16,2,256]{2,1,0:T(2,128)S(1)} all-to-all(f32[16,2,256]{2,1,0:T(2,128)S(1)} %get-tuple-element.139), channel_id=1, replica_groups=mesh['task'=8,'mp'=16] {'mp'}, dimensions={0} | all-to-all | bytes 65536 | tf_op jit(solution)/shard_map/cond/branch_0_fun/all_to_all | solution.py:510
  99.4 1.7 renew.7
  101.1 3.7 %all-to-all-start.4 = ((bf16[16,192,256]{2,1,0:T(8,128)(2,1)}), bf16[16,192,256]{2,1,0:T(8,128)(2,1)S(1)}, u32[]{:S(2)}, u32[]{:S(2)}) async-start(bf16[16,192,256]{2,1,0:T(8,128)(2,1)} %get-tuple-element.141), calls=%async_computation.4 | async-start | bytes 3145728 | tf_op jit(solution)/shard_map/cond/branch_0_fun/all_to_all | solution.py:510
  104.9 7.0 %prior.7 = f32[8,256]{1,0:T(8,128)S(1)} custom-call(bf16[16,192,256]{2,1,0:T(8,128)(2,1)} %copy-done.3, bf16[4096,1024]{1,0:T(8,128)(2,1)} %get-tuple-element.271.w_ref, bf16[1024,1024]{1,0:T(8,128)(2,1)} %get-tuple-element.273.logit_ref, bf16[2,1024]{1,0:T(2,128)(2,1)S(1)} %copy-done.11, bf16[3,192,1024]{2,1,0:T(8,128)(2,1)} %get-tuple-element.157.hot_hbm, ...), custom_call_target="tpu_custom_call" | custom-call | tf_op jit(solution)/shard_map/cond/branch_0_fun/prior/pallas_call | solution.py:451
  111.9 13.6 %all-to-all-done.4.x_hbm = bf16[16,192,256]{2,1,0:T(8,128)(2,1)S(1)} async-done(((bf16[16,192,256]{2,1,0:T(8,128)(2,1)}), bf16[16,192,256]{2,1,0:T(8,128)(2,1)S(1)}, u32[]{:S(2)}, u32[]{:S(2)}) %all-to-all-start.4) | async-done | bytes 1572896 | tf_op jit(solution)/shard_map/cond/branch_0_fun/all_to_all | solution.py:510
  125.4 4.4 %gates.8 = (f32[192,768]{1,0:T(8,128)S(1)}, f32[16,2,256]{2,1,0:T(2,128)S(1)}) custom-call(f32[3,192,768]{2,1,0:T(8,128)} %get-tuple-element.150.emb_hbm, bf16[16,192,256]{2,1,0:T(8,128)(2,1)S(1)} %all-to-all-done.4.x_hbm, bf16[3,5120,256]{2,1,0:T(8,128)(2,1)} %get-tuple-element.120.w_hbm.w_ref), custom_call_target="tpu_custom_call" | custom-call | tf_op jit(solution)/shard_map/cond/branch_0_fun/gates/pallas_call | solution.py:408
  129.8 11.9 %all_to_all.59.stat_ref = f32[16,2,256]{2,1,0:T(2,128)S(1)} all-to-all(f32[16,2,256]{2,1,0:T(2,128)S(1)} %get-tuple-element.146), channel_id=1, replica_groups=mesh['task'=8,'mp'=16] {'mp'}, dimensions={0} | all-to-all | bytes 65536 | tf_op jit(solution)/shard_map/cond/branch_0_fun/all_to_all | solution.py:510
  141.8 1.7 renew.8
  143.5 3.7 %all-to-all-start.6 = ((bf16[16,192,256]{2,1,0:T(8,128)(2,1)}), bf16[16,192,256]{2,1,0:T(8,128)(2,1)S(1)}, u32[]{:S(2)}, u32[]{:S(2)}) async-start(bf16[16,192,256]{2,1,0:T(8,128)(2,1)} %get-tuple-element.148), calls=%async_computation.6 | async-start | bytes 3145728 | tf_op jit(solution)/shard_map/cond/branch_0_fun/all_to_all | solution.py:510
  147.7 7.0 %prior.8 = f32[8,256]{1,0:T(8,128)S(1)} custom-call(bf16[16,192,256]{2,1,0:T(8,128)(2,1)} %copy-done.1, bf16[4096,1024]{1,0:T(8,128)(2,1)} %get-tuple-element.271.w_ref, bf16[1024,1024]{1,0:T(8,128)(2,1)} %get-tuple-element.273.logit_ref, bf16[2,1024]{1,0:T(2,128)(2,1)S(1)} %copy-done.11, bf16[3,192,1024]{2,1,0:T(8,128)(2,1)} %get-tuple-element.157.hot_hbm, ...), custom_call_target="tpu_custom_call" | custom-call | tf_op jit(solution)/shard_map/cond/branch_0_fun/prior/pallas_call | solution.py:451
  154.7 12.9 %all-to-all-done.6.x_hbm = bf16[16,192,256]{2,1,0:T(8,128)(2,1)S(1)} async-done(((bf16[16,192,256]{2,1,0:T(8,128)(2,1)}), bf16[16,192,256]{2,1,0:T(8,128)(2,1)S(1)}, u32[]{:S(2)}, u32[]{:S(2)}) %all-to-all-start.6) | async-done | bytes 1572896 | tf_op jit(solution)/shard_map/cond/branch_0_fun/all_to_all | solution.py:510
  167.6 5.0 %gates.9 = (f32[192,768]{1,0:T(8,128)S(1)}, f32[16,2,256]{2,1,0:T(2,128)}) custom-call(f32[3,192,768]{2,1,0:T(8,128)} %get-tuple-element.150.emb_hbm, bf16[16,192,256]{2,1,0:T(8,128)(2,1)S(1)} %all-to-all-done.6.x_hbm, bf16[3,5120,256]{2,1,0:T(8,128)(2,1)} %get-tuple-element.120.w_hbm.w_ref), custom_call_target="tpu_custom_call" | custom-call | tf_op jit(solution)/shard_map/cond/branch_0_fun/gates/pallas_call | solution.py:408
  172.7 5.5 %all-to-all-start.7 = ((f32[16,2,256]{2,1,0:T(2,128)}), f32[16,2,256]{2,1,0:T(2,128)S(1)}, u32[]{:S(2)}, u32[]{:S(2)}) async-start(f32[16,2,256]{2,1,0:T(2,128)} %get-tuple-element.153), calls=%async_computation.7 | async-start | bytes 65536 | tf_op jit(solution)/shard_map/cond/branch_0_fun/all_to_all | solution.py:510
  179.2 7.0 %prior.9 = f32[8,256]{1,0:T(8,128)S(1)} custom-call(bf16[16,192,256]{2,1,0:T(8,128)(2,1)} %copy-done.2, bf16[4096,1024]{1,0:T(8,128)(2,1)} %get-tuple-element.271.w_ref, bf16[1024,1024]{1,0:T(8,128)(2,1)} %get-tuple-element.273.logit_ref, bf16[2,1024]{1,0:T(2,128)(2,1)S(1)} %copy-done.11, bf16[3,192,1024]{2,1,0:T(8,128)(2,1)} %get-tuple-element.157.hot_hbm, ...), custom_call_target="tpu_custom_call" | custom-call | tf_op jit(solution)/shard_map/cond/branch_0_fun/prior/pallas_call | solution.py:451
  187.3 15.5 %all-gather.1 = bf16[1792,256]{1,0:T(8,128)(2,1)S(1)} all-gather(bf16[224,256]{1,0:T(8,128)(2,1)S(1)} %concatenate.19), channel_id=3, replica_groups=mesh['task'=8,'mp'=16] {'task'}, dimensions={0}, use_global_device_ids=true | all-gather | bytes 1032192 | tf_op jit(solution)/shard_map/cond/branch_0_fun/all_gather | solution.py:618
  202.8 2.2 %settle.2 = (f32[4,256]{1,0:T(4,128)}, f32[4,256]{1,0:T(4,128)}, f32[4,256]{1,0:T(4,128)}, f32[256,256]{1,0:T(8,128)}) custom-call(s32[2,8]{1,0:T(2,128)S(1)} %pad_add_fusion.at_ref, s32[4,8]{1,0:T(4,128)S(1)} %get-tuple-element.607.to_ref, bf16[8,224,256]{2,1,0:T(8,128)(2,1)S(1)} %bitcast.30, bf16[8,64,256]{2,1,0:T(8,128)(2,1)S(1)} %slice.48.left_ref, ...), custom_call_target="tpu_custom_call" | custom-call | tf_op jit(solution)/shard_map/cond/branch_0_fun/settle/pallas_call | solution.py:493
  (81 shorter events, 8.3 us)
Async XLA Ops:
  0.6 4.2 %collective-permute-start = (f32[256,256]{1,0:T(8,128)}, f32[256,256]{1,0:T(8,128)S(1)}, u32[]{:S(2)}, u32[]{:S(2)}) collective-permute-start(f32[256,256]{1,0:T(8,128)} %param.15), channel_id=1, source_target_pairs={{0,16},{16,0},{32,48},{48,32},{64,80},{80,64},{96,112},{112,96},{1... | collective-permute-start | bytes 786440 | tf_op jit(solution)/shard_map/ppermute | solution.py:645
  4.9 9.3 %copy-start.15 = (s32[4,4]{1,0:T(4,128)S(1)}, s32[4,4]{1,0:T(4,128)}, u32[]{:S(2)}) copy-start(s32[4,4]{1,0:T(4,128)} %get-tuple-element.522) | copy-start | bytes 196 | tf_op jit(solution)/shard_map/cond
  4.9 9.6 %copy-start.13 = (s32[4,256]{1,0:T(4,128)S(1)}, s32[4,256]{1,0:T(4,128)}, u32[]{:S(2)}) copy-start(s32[4,256]{1,0:T(4,128)} %get-tuple-element.265) | copy-start | bytes 12292 | tf_op jit(solution)/shard_map/cond
  4.9 9.6 %copy-start.7 = (s32[4,32,256]{2,1,0:T(8,128)S(1)}, s32[4,32,256]{2,1,0:T(8,128)}, u32[]{:S(2)}) copy-start(s32[4,32,256]{2,1,0:T(8,128)} %get-tuple-element.263) | copy-start | bytes 393220 | tf_op jit(solution)/shard_map/cond
  7.3 32.2 %all-to-all-start = ((bf16[16,192,256]{2,1,0:T(8,128)(2,1)}), bf16[16,192,256]{2,1,0:T(8,128)(2,1)S(1)}, u32[]{:S(2)}, u32[]{:S(2)}) async-start(bf16[16,192,256]{2,1,0:T(8,128)(2,1)} %get-tuple-element.113), calls=%async_computation | async-start | bytes 3145728 | tf_op jit(solution)/shard_map/cond/branch_0_fun/all_to_all | solution.py:510
  29.5 1.0 copy-start.6
  30.5 2.2 %copy-start.9 = (bf16[18,1024]{1,0:T(8,128)(2,1)S(1)}, bf16[18,1024]{1,0:T(8,128)(2,1)}, u32[]{:S(2)}) copy-start(bf16[18,1024]{1,0:T(8,128)(2,1)} %get-tuple-element.269.act_ref) | copy-start | bytes 110596 | tf_op jit(solution)/shard_map/cond
  32.7 4.8 %copy-start.16 = (s32[64]{0:T(128)S(1)}, s32[64]{0:T(128)}, u32[]{:S(2)}) copy-start(s32[64]{0:T(128)} %get-tuple-element.128) | copy-start | bytes 772 | tf_op jit(solution)/shard_map/cond
  39.6 5.0 %copy-start = (bf16[16,192,256]{2,1,0:T(8,128)(2,1)}, bf16[16,192,256]{2,1,0:T(8,128)(2,1)S(1)}, u32[]{:S(2)}) copy-start(bf16[16,192,256]{2,1,0:T(8,128)(2,1)S(1)} %all-to-all-done.x_hbm) | copy-start | bytes 4718596 | tf_op jit(solution)/shard_map/cond
  44.6 11.5 %all-to-all-start.1 = ((f32[16,2,256]{2,1,0:T(2,128)}), f32[16,2,256]{2,1,0:T(2,128)S(1)}, u32[]{:S(2)}, u32[]{:S(2)}) async-start(f32[16,2,256]{2,1,0:T(2,128)} %get-tuple-element.126), calls=%async_computation.1 | async-start | bytes 65536 | tf_op jit(solution)/shard_map/cond/branch_0_fun/all_to_all | solution.py:510
  57.9 24.6 %all-to-all-start.2 = ((bf16[16,192,256]{2,1,0:T(8,128)(2,1)}), bf16[16,192,256]{2,1,0:T(8,128)(2,1)S(1)}, u32[]{:S(2)}, u32[]{:S(2)}) async-start(bf16[16,192,256]{2,1,0:T(8,128)(2,1)} %get-tuple-element.129), calls=%async_computation.2 | async-start | bytes 3145728 | tf_op jit(solution)/shard_map/cond/branch_0_fun/all_to_all | solution.py:510
  61.6 8.7 %copy-start.11 = (bf16[2,1024]{1,0:T(2,128)(2,1)S(1)}, bf16[2,1024]{1,0:T(2,128)(2,1)}, u32[]{:S(2)}) copy-start(bf16[2,1024]{1,0:T(2,128)(2,1)} %get-tuple-element.132.head_ref) | copy-start | bytes 12292 | tf_op jit(solution)/shard_map/cond
  82.5 4.4 %copy-start.3 = (bf16[16,192,256]{2,1,0:T(8,128)(2,1)}, bf16[16,192,256]{2,1,0:T(8,128)(2,1)S(1)}, u32[]{:S(2)}) copy-start(bf16[16,192,256]{2,1,0:T(8,128)(2,1)S(1)} %all-to-all-done.2.x_hbm) | copy-start | bytes 4718596 | tf_op jit(solution)/shard_map/cond
  101.1 24.3 %all-to-all-start.4 = ((bf16[16,192,256]{2,1,0:T(8,128)(2,1)}), bf16[16,192,256]{2,1,0:T(8,128)(2,1)S(1)}, u32[]{:S(2)}, u32[]{:S(2)}) async-start(bf16[16,192,256]{2,1,0:T(8,128)(2,1)} %get-tuple-element.141), calls=%async_computation.4 | async-start | bytes 3145728 | tf_op jit(solution)/shard_map/cond/branch_0_fun/all_to_all | solution.py:510
  125.4 4.4 %copy-start.1 = (bf16[16,192,256]{2,1,0:T(8,128)(2,1)}, bf16[16,192,256]{2,1,0:T(8,128)(2,1)S(1)}, u32[]{:S(2)}) copy-start(bf16[16,192,256]{2,1,0:T(8,128)(2,1)S(1)} %all-to-all-done.4.x_hbm) | copy-start | bytes 4718596 | tf_op jit(solution)/shard_map/cond
  143.5 24.1 %all-to-all-start.6 = ((bf16[16,192,256]{2,1,0:T(8,128)(2,1)}), bf16[16,192,256]{2,1,0:T(8,128)(2,1)S(1)}, u32[]{:S(2)}, u32[]{:S(2)}) async-start(bf16[16,192,256]{2,1,0:T(8,128)(2,1)} %get-tuple-element.148), calls=%async_computation.6 | async-start | bytes 3145728 | tf_op jit(solution)/shard_map/cond/branch_0_fun/all_to_all | solution.py:510
  167.6 5.0 %copy-start.2 = (bf16[16,192,256]{2,1,0:T(8,128)(2,1)}, bf16[16,192,256]{2,1,0:T(8,128)(2,1)S(1)}, u32[]{:S(2)}) copy-start(bf16[16,192,256]{2,1,0:T(8,128)(2,1)S(1)} %all-to-all-done.6.x_hbm) | copy-start | bytes 4718596 | tf_op jit(solution)/shard_map/cond
  172.7 13.6 %all-to-all-start.7 = ((f32[16,2,256]{2,1,0:T(2,128)}), f32[16,2,256]{2,1,0:T(2,128)S(1)}, u32[]{:S(2)}, u32[]{:S(2)}) async-start(f32[16,2,256]{2,1,0:T(2,128)} %get-tuple-element.153), calls=%async_computation.7 | async-start | bytes 65536 | tf_op jit(solution)/shard_map/cond/branch_0_fun/all_to_all | solution.py:510
